TPU v7x, 32 devices: a whole 2x2x4 slice. The times are simulated.
32 devices in a mesh: dp: 4 (over x, core), fsdp: 8 (over z, y).
Axes of the slice: x: 2, y: 2, z: 4, core: 2. Of those that a mesh axis runs over, the one named last changes fastest.
Arguments:
- patches_in: bfloat16 [32, 256, 1152], P(('dp', 'fsdp')), may hold values from -6 to 6
- condition: bfloat16 [32, 1152], P(('dp', 'fsdp')), may hold values from -6 to 6
- keep_count: int32 [32], P(('dp', 'fsdp')), may hold values from 48 to 192, as said below
- keep_index: int32 [32, 192], P(('dp', 'fsdp')), may hold values from 0 to 255, as said below
- w_ada: bfloat16 [1152, 6912], P('dp', 'fsdp'), may hold values from -0.1875 to 0.1875
- b_ada: bfloat16 [6912], P(('dp', 'fsdp')), may hold values from -3 to 3
- w_qkv: bfloat16 [1152, 3456], P('dp', 'fsdp'), may hold values from -0.1875 to 0.1875
- qv_bias: bfloat16 [2304], P(('dp', 'fsdp')), may hold values from -3 to 3
- w_proj: bfloat16 [1152, 1152], P('dp', 'fsdp'), may hold values from -1.5 to 1.5
- w_fc1: bfloat16 [1152, 4608], P('dp', 'fsdp'), may hold values from -0.1875 to 0.1875
- fc1_bias: bfloat16 [4608], P(('dp', 'fsdp')), may hold values from -3 to 3
- w_fc2: bfloat16 [4608, 1152], P('dp', 'fsdp'), may hold values from -0.1875 to 0.1875
- out_bias: bfloat16 [2304], P(('dp', 'fsdp')), may hold values from -3 to 3
- cotangent: bfloat16 [32, 192, 1152], P(('dp', 'fsdp')), may hold values from -6 to 6
Outputs:
- block_out: bfloat16 [32, 192, 1152], P(('dp', 'fsdp'))
- grad_patches: float32 [32, 256, 1152], P(('dp', 'fsdp'))
- grad_condition: float32 [32, 1152], P(('dp', 'fsdp'))
- grad_w_ada: float32 [1152, 6912], P('dp', 'fsdp')
- grad_b_ada: float32 [6912], P(('dp', 'fsdp'))
- grad_w_qkv: float32 [1152, 3456], P('dp', 'fsdp')
- grad_qv_bias: float32 [2304], P(('dp', 'fsdp'))
- grad_w_proj: float32 [1152, 1152], P('dp', 'fsdp')
- grad_w_fc1: float32 [1152, 4608], P('dp', 'fsdp')
- grad_fc1_bias: float32 [4608], P(('dp', 'fsdp'))
- grad_w_fc2: float32 [4608, 1152], P('dp', 'fsdp')
- grad_out_bias: float32 [2304], P(('dp', 'fsdp'))
Inputs may be any that keep to these rules, and one draw needn't show every extreme that they name: `keep_count`: the first image keeps 192 tokens and the last 48. `keep_index`: the 192 entries of an image are distinct patch numbers.
All inputs are finite; a program needn't handle non-finite values.
Results may differ from a plain program's by a relative error of at most 0.017.
The roundings to bfloat16 on the way count: a program that leaves them out, or rounds other values in their place, can miss the bound.
Values may be sent and summed in bfloat16 or wider, within the bound.
A program may use at most 192 MiB of HBM per device.

v0:
```python
import math

import jax
import jax.numpy as jnp
from jax import lax
from jax.sharding import PartitionSpec as P

HEADS = 16


epsilon = 1e-06
negative = -1e30


def layer_norm(inputs):
    centred = inputs - jnp.mean(inputs, axis=-1, keepdims=True)
    rstd = lax.rsqrt(jnp.mean(centred * centred, axis=-1, keepdims=True) + epsilon)
    return (centred * rstd, rstd)


def norm_back(upstream, normed, rstd):
    return rstd * (
        upstream
        - jnp.mean(upstream, axis=-1, keepdims=True)
        - normed * jnp.mean(upstream * normed, axis=-1, keepdims=True)
    )


def swish(inputs):
    return inputs / (1.0 + jnp.exp(-inputs))


def gelu_tanh(inputs):
    return (
        0.5
        * inputs
        * (1.0 + jnp.tanh(0.7978845608028654 * (inputs + 0.044715 * inputs * inputs * inputs)))
    )


def inner_rows(left, right):
    return lax.dot_general(
        left, right, (((0,), (0,)), ((), ())), preferred_element_type=jnp.float32
    )


def times_transposed(left, right):
    return lax.dot_general(
        left, right, (((1,), (1,)), ((), ())), preferred_element_type=jnp.float32
    )


def flat_bias(collected):
    return collected.reshape(-1)


def gather_forward(w_ada, b_ada, w_qkv, qv_bias, w_proj, w_fc1, fc1_bias, w_fc2, out_bias):
    part_ada, part_qkv, part_proj, part_one, part_two, bias_ada, bias_qv, bias_one, bias_out = (
        lax.all_gather(w_ada, "fsdp", axis=1, tiled=True),
        lax.all_gather(w_qkv, "fsdp", axis=1, tiled=True),
        lax.all_gather(w_proj, "fsdp", axis=1, tiled=True),
        lax.all_gather(w_fc1, "fsdp", axis=1, tiled=True),
        lax.all_gather(w_fc2, "fsdp", axis=1, tiled=True),
        lax.all_gather(b_ada.reshape(1, 1, -1), "fsdp", axis=1, tiled=True),
        lax.all_gather(qv_bias.reshape(1, 1, -1), "fsdp", axis=1, tiled=True),
        lax.all_gather(fc1_bias.reshape(1, 1, -1), "fsdp", axis=1, tiled=True),
        lax.all_gather(out_bias.reshape(1, 1, -1), "fsdp", axis=1, tiled=True),
    )
    gathered = (
        lax.all_gather(part_ada, "dp", axis=0, tiled=True),
        lax.all_gather(part_qkv, "dp", axis=0, tiled=True),
        lax.all_gather(part_proj, "dp", axis=0, tiled=True),
        lax.all_gather(part_one, "dp", axis=0, tiled=True),
        lax.all_gather(part_two, "dp", axis=0, tiled=True),
        lax.all_gather(bias_ada, "dp", axis=0, tiled=True),
        lax.all_gather(bias_qv, "dp", axis=0, tiled=True),
        lax.all_gather(bias_one, "dp", axis=0, tiled=True),
        lax.all_gather(bias_out, "dp", axis=0, tiled=True),
    )
    return (
        gathered[0],
        flat_bias(gathered[5]),
        gathered[1],
        flat_bias(gathered[6]),
        gathered[2],
        gathered[3],
        flat_bias(gathered[7]),
        gathered[4],
        flat_bias(gathered[8]),
    )


def gather_backward(w_ada, w_qkv, w_proj, w_fc1, w_fc2):
    part_ada, part_qkv, part_proj, part_one, part_two = (
        lax.all_gather(w_ada, "fsdp", axis=1, tiled=True),
        lax.all_gather(w_qkv, "fsdp", axis=1, tiled=True),
        lax.all_gather(w_proj, "fsdp", axis=1, tiled=True),
        lax.all_gather(w_fc1, "fsdp", axis=1, tiled=True),
        lax.all_gather(w_fc2, "fsdp", axis=1, tiled=True),
    )
    return (
        lax.all_gather(part_ada, "dp", axis=0, tiled=True),
        lax.all_gather(part_qkv, "dp", axis=0, tiled=True),
        lax.all_gather(part_proj, "dp", axis=0, tiled=True),
        lax.all_gather(part_one, "dp", axis=0, tiled=True),
        lax.all_gather(part_two, "dp", axis=0, tiled=True),
    )


def split_bias(term):
    return term.reshape(lax.axis_size("dp"), lax.axis_size("fsdp"), -1)


def own_bias(summed):
    return lax.dynamic_index_in_dim(summed, lax.axis_index("dp"), 0, keepdims=False).reshape(-1)


def owned_columns(matrix, width):
    return lax.dynamic_slice_in_dim(matrix, lax.axis_index("dp") * width, width, 1)


def column_totals(matrix):
    return jnp.sum(matrix.astype(jnp.float32), axis=0)


def shards(
    patches_in,
    condition,
    keep_count,
    keep_index,
    w_ada,
    b_ada,
    w_qkv,
    qv_bias,
    w_proj,
    w_fc1,
    fc1_bias,
    w_fc2,
    out_bias,
    cotangent,
):
    images, kept_slots = keep_index.shape
    features = patches_in.shape[2]
    hidden_units = w_fc2.shape[0] * lax.axis_size("dp")
    all_rows = images * kept_slots
    head_size = features // HEADS
    factor = 1.0 / math.sqrt(head_size)
    head_shape = (images, kept_slots, HEADS, head_size)
    row_width = features // lax.axis_size("dp")
    unit_width = hidden_units // lax.axis_size("dp")
    ada_full, ada_bias, qkv_full, qv_full, proj_full, one_full, one_bias, two_full, out_full = (
        gather_forward(w_ada, b_ada, w_qkv, qv_bias, w_proj, w_fc1, fc1_bias, w_fc2, out_bias)
    )
    inputs = patches_in.astype(jnp.float32)
    kept_in = jnp.take_along_axis(inputs, keep_index[:, :, None], axis=1)
    allowed = (jnp.arange(kept_slots)[None, :] < keep_count[:, None])[:, None, None, :]
    cond_float = condition.astype(jnp.float32)
    signal = swish(cond_float).astype(jnp.bfloat16)
    modulation = jnp.dot(signal, ada_full, preferred_element_type=jnp.float32) + ada_bias.astype(
        jnp.float32
    )
    shift_one, scale_one, gate_one, shift_two, scale_two, gate_two = [
        modulation[:, None, column * features : (column + 1) * features] for column in range(6)
    ]
    normed_one, rstd_one = layer_norm(kept_in)
    hidden_one = (
        (normed_one * (1.0 + scale_one) + shift_one)
        .astype(jnp.bfloat16)
        .reshape(all_rows, features)
    )
    qv_float = qv_full.astype(jnp.float32)
    qkv_bias = jnp.concatenate(
        [qv_float[:features], jnp.zeros((features,), jnp.float32), qv_float[features:]]
    )
    projected = (
        jnp.dot(hidden_one, qkv_full, preferred_element_type=jnp.float32) + qkv_bias
    ).astype(jnp.bfloat16)
    queries = projected[:, :features].reshape(head_shape)
    key_rows = projected[:, features : 2 * features].reshape(head_shape)
    values = projected[:, 2 * features :].reshape(head_shape)
    scores = (
        jnp.einsum("iqhe,ikhe->ihqk", queries, key_rows, preferred_element_type=jnp.float32)
        * factor
    )
    scores = jnp.where(allowed, scores, negative)
    top_score = jnp.max(scores, axis=-1, keepdims=True)
    exponent = jnp.exp(scores - top_score)
    row_total = jnp.sum(exponent, axis=-1, keepdims=True)
    log_total = top_score + jnp.log(row_total)
    softmax_low = (exponent / row_total).astype(jnp.bfloat16)
    mixed = jnp.einsum("ihqk,ikhe->iqhe", softmax_low, values, preferred_element_type=jnp.float32)
    mixed_low = mixed.reshape(all_rows, features).astype(jnp.bfloat16)
    out_float = out_full.astype(jnp.float32)
    attended = (
        jnp.dot(mixed_low, proj_full, preferred_element_type=jnp.float32) + out_float[:features]
    ).reshape(images, kept_slots, features)
    middle = kept_in + gate_one * attended
    normed_two, rstd_two = layer_norm(middle)
    hidden_two = (
        (normed_two * (1.0 + scale_two) + shift_two)
        .astype(jnp.bfloat16)
        .reshape(all_rows, features)
    )
    raised = jnp.dot(hidden_two, one_full, preferred_element_type=jnp.float32) + one_bias.astype(
        jnp.float32
    )
    activated = gelu_tanh(raised).astype(jnp.bfloat16)
    branch = (
        jnp.dot(activated, two_full, preferred_element_type=jnp.float32) + out_float[features:]
    ).reshape(images, kept_slots, features)
    block_out = (middle + gate_two * branch).astype(jnp.bfloat16)
    ada_back, qkv_back, proj_back, one_back, two_back = gather_backward(
        w_ada, w_qkv, w_proj, w_fc1, w_fc2
    )
    upstream = cotangent.astype(jnp.float32)
    d_gate_two = jnp.sum(upstream * branch, axis=1)
    d_branch = (gate_two * upstream).reshape(all_rows, features).astype(jnp.bfloat16)
    d_activated = times_transposed(d_branch, two_back)
    unused, gelu_pull = jax.vjp(gelu_tanh, raised)
    d_raised = gelu_pull(d_activated)[0].astype(jnp.bfloat16)
    d_hidden_two = times_transposed(d_raised, one_back).reshape(images, kept_slots, features)
    d_shift_two = jnp.sum(d_hidden_two, axis=1)
    d_scale_two = jnp.sum(d_hidden_two * normed_two, axis=1)
    d_middle = upstream + norm_back(d_hidden_two * (1.0 + scale_two), normed_two, rstd_two)
    d_gate_one = jnp.sum(d_middle * attended, axis=1)
    d_attended = (gate_one * d_middle).reshape(all_rows, features).astype(jnp.bfloat16)
    d_mixed = times_transposed(d_attended, proj_back).astype(jnp.bfloat16).reshape(head_shape)
    scores_again = (
        jnp.einsum("iqhe,ikhe->ihqk", queries, key_rows, preferred_element_type=jnp.float32)
        * factor
    )
    scores_again = jnp.where(allowed, scores_again, negative)
    softmax_again = jnp.exp(scores_again - log_total)
    d_softmax = jnp.einsum("iqhe,ikhe->ihqk", d_mixed, values, preferred_element_type=jnp.float32)
    row_delta = jnp.sum(d_softmax * softmax_again, axis=-1, keepdims=True)
    d_scores = (softmax_again * (d_softmax - row_delta)).astype(jnp.bfloat16)
    d_queries = (
        jnp.einsum("ihqk,ikhe->iqhe", d_scores, key_rows, preferred_element_type=jnp.float32)
        * factor
    )
    d_keys = (
        jnp.einsum("ihqk,iqhe->ikhe", d_scores, queries, preferred_element_type=jnp.float32)
        * factor
    )
    d_values = jnp.einsum(
        "ihqk,iqhe->ikhe",
        softmax_again.astype(jnp.bfloat16),
        d_mixed,
        preferred_element_type=jnp.float32,
    )
    d_projected = jnp.concatenate(
        [
            d_queries.reshape(all_rows, features),
            d_keys.reshape(all_rows, features),
            d_values.reshape(all_rows, features),
        ],
        axis=1,
    ).astype(jnp.bfloat16)
    d_hidden_one = times_transposed(d_projected, qkv_back).reshape(images, kept_slots, features)
    d_shift_one = jnp.sum(d_hidden_one, axis=1)
    d_scale_one = jnp.sum(d_hidden_one * normed_one, axis=1)
    d_kept = d_middle + norm_back(d_hidden_one * (1.0 + scale_one), normed_one, rstd_one)
    grad_patches = jnp.zeros_like(inputs).at[jnp.arange(images)[:, None], keep_index].add(d_kept)
    d_modulation = jnp.concatenate(
        [d_shift_one, d_scale_one, d_gate_one, d_shift_two, d_scale_two, d_gate_two], axis=1
    ).astype(jnp.bfloat16)
    d_signal = times_transposed(d_modulation, ada_back)
    unused_too, swish_pull = jax.vjp(swish, cond_float)
    grad_condition = swish_pull(d_signal)[0]
    piece_one = lax.all_gather(hidden_one, "dp", axis=0, tiled=True)
    piece_proj_d = lax.all_gather(d_projected, "dp", axis=0, tiled=True)
    piece_mixed = lax.all_gather(mixed_low, "dp", axis=0, tiled=True)
    piece_att_d = lax.all_gather(d_attended, "dp", axis=0, tiled=True)
    piece_two = lax.all_gather(hidden_two, "dp", axis=0, tiled=True)
    piece_raised_d = lax.all_gather(d_raised, "dp", axis=0, tiled=True)
    piece_act = lax.all_gather(activated, "dp", axis=0, tiled=True)
    piece_branch_d = lax.all_gather(d_branch, "dp", axis=0, tiled=True)
    grad_qkv = inner_rows(owned_columns(piece_one, row_width), piece_proj_d)
    grad_proj = inner_rows(owned_columns(piece_mixed, row_width), piece_att_d)
    grad_one = inner_rows(owned_columns(piece_two, row_width), piece_raised_d)
    grad_two = inner_rows(owned_columns(piece_act, unit_width), piece_branch_d)
    qkv_sums = column_totals(piece_proj_d)
    proj_sums = column_totals(piece_att_d)
    one_sums = column_totals(piece_raised_d)
    two_sums = column_totals(piece_branch_d)
    piece_signal = lax.all_gather(signal, "dp", axis=0, tiled=True)
    piece_mod_d = lax.all_gather(d_modulation, "dp", axis=0, tiled=True)
    grad_ada = inner_rows(owned_columns(piece_signal, row_width), piece_mod_d)
    ada_sums = column_totals(piece_mod_d)
    grad_qv = jnp.concatenate([qkv_sums[:features], qkv_sums[2 * features :]])
    grad_out = jnp.concatenate([proj_sums, two_sums])
    terms = (
        grad_ada,
        grad_qkv,
        grad_proj,
        grad_one,
        grad_two,
        split_bias(ada_sums),
        split_bias(grad_qv),
        split_bias(one_sums),
        split_bias(grad_out),
    )
    (
        final_ada,
        final_qkv,
        final_proj,
        final_one,
        final_two,
        final_ada_bias,
        final_qv,
        final_bias,
        final_out,
    ) = (
        lax.psum_scatter(
            terms[0].astype(jnp.bfloat16), "fsdp", scatter_dimension=1, tiled=True
        ).astype(jnp.float32),
        lax.psum_scatter(
            terms[1].astype(jnp.bfloat16), "fsdp", scatter_dimension=1, tiled=True
        ).astype(jnp.float32),
        lax.psum_scatter(
            terms[2].astype(jnp.bfloat16), "fsdp", scatter_dimension=1, tiled=True
        ).astype(jnp.float32),
        lax.psum_scatter(
            terms[3].astype(jnp.bfloat16), "fsdp", scatter_dimension=1, tiled=True
        ).astype(jnp.float32),
        lax.psum_scatter(
            terms[4].astype(jnp.bfloat16), "fsdp", scatter_dimension=1, tiled=True
        ).astype(jnp.float32),
        lax.psum_scatter(
            terms[5].astype(jnp.bfloat16), "fsdp", scatter_dimension=1, tiled=True
        ).astype(jnp.float32),
        lax.psum_scatter(
            terms[6].astype(jnp.bfloat16), "fsdp", scatter_dimension=1, tiled=True
        ).astype(jnp.float32),
        lax.psum_scatter(
            terms[7].astype(jnp.bfloat16), "fsdp", scatter_dimension=1, tiled=True
        ).astype(jnp.float32),
        lax.psum_scatter(
            terms[8].astype(jnp.bfloat16), "fsdp", scatter_dimension=1, tiled=True
        ).astype(jnp.float32),
    )
    return (
        block_out,
        grad_patches,
        grad_condition,
        final_ada,
        own_bias(final_ada_bias),
        final_qkv,
        own_bias(final_qv),
        final_proj,
        final_one,
        own_bias(final_bias),
        final_two,
        own_bias(final_out),
    )


def solution(mesh):
    placed = (
        P(("dp", "fsdp"), None, None),
        P(("dp", "fsdp"), None),
        P(("dp", "fsdp")),
        P(("dp", "fsdp"), None),
        P("dp", "fsdp"),
        P(("dp", "fsdp")),
        P("dp", "fsdp"),
        P(("dp", "fsdp")),
        P("dp", "fsdp"),
        P("dp", "fsdp"),
        P(("dp", "fsdp")),
        P("dp", "fsdp"),
        P(("dp", "fsdp")),
        P(("dp", "fsdp"), None, None),
    )
    return jax.shard_map(
        shards,
        mesh=mesh,
        in_specs=placed,
        out_specs=(
            P(("dp", "fsdp"), None, None),
            P(("dp", "fsdp"), None, None),
            P(("dp", "fsdp"), None),
            P("dp", "fsdp"),
            P(("dp", "fsdp")),
            P("dp", "fsdp"),
            P(("dp", "fsdp")),
            P("dp", "fsdp"),
            P("dp", "fsdp"),
            P(("dp", "fsdp")),
            P("dp", "fsdp"),
            P(("dp", "fsdp")),
        ),
        check_vma=False,
    )
```

profile of v0, /device:TPU:0, one launch (start us, length us, event | category | flops | bytes accessed | tf_op | source)
XLA Modules:
  0.0 1289.3 jit_solution(15727656072078803900)
XLA Ops:
  10.0 75.5 %all-gather.57.cloned.1.call-done = bf16[8,864,288]{1,2,0:T(8,128)(2,1)} async-done(((bf16[1,864,288]{1,2,0:T(8,128)(2,1)}), bf16[8,864,288]{1,2,0:T(8,128)(2,1)}) %all-gather.57.cloned.1.call-update) | async-done | bytes 3981328 | tf_op jit(solution)/shard_map/all_gather | solution.py:59
  98.8 39.3 %all-gather.59.cloned.1.call-done = bf16[8,432,288]{1,2,0:T(8,128)(2,1)} async-done(((bf16[1,432,288]{1,2,0:T(8,128)(2,1)}), bf16[8,432,288]{1,2,0:T(8,128)(2,1)}) %all-gather.59.cloned.1.call-update) | async-done | bytes 1990672 | tf_op jit(solution)/shard_map/all_gather | solution.py:60
  145.2 34.0 %all_gather.102 = bf16[288,1152]{0,1:T(8,128)(2,1)S(1)} all-gather(bf16[288,144]{0,1:T(8,128)(2,1)S(1)} %copy-done.19), channel_id=1, replica_groups=mesh['dp'=4,'fsdp'=8] {'fsdp'}, dimensions={1}, use_global_device_ids=true | all-gather | bytes 746496 | tf_op jit(solution)/shard_map/all_gather | solution.py:61
  180.3 23.3 %all-gather.61.cloned.1.call-done = bf16[8,576,288]{1,2,0:T(8,128)(2,1)} async-done(((bf16[1,576,288]{1,2,0:T(8,128)(2,1)}), bf16[8,576,288]{1,2,0:T(8,128)(2,1)}) %all-gather.61.cloned.1.call-update) | async-done | bytes 2654224 | tf_op jit(solution)/shard_map/all_gather | solution.py:62
  209.8 50.1 %all-gather.37.cloned.1.call-done = bf16[1152,1152]{0,1:T(8,128)(2,1)} async-done(((bf16[1152,144]{0,1:T(8,128)(2,1)}), bf16[1152,1152]{0,1:T(8,128)(2,1)}) %all-gather.37.cloned.1.call-update) | async-done | bytes 2654224 | tf_op jit(solution)/shard_map/all_gather | solution.py:63
  263.6 34.7 %all-reduce.10 = (bf16[1728]{0:T(1024)(128)(2,1)S(1)}, bf16[576]{0:T(1024)(128)(2,1)S(1)}, bf16[576]{0:T(1024)(128)(2,1)S(1)}, bf16[1152]{0:T(1024)(128)(2,1)S(1)}) all-reduce(bf16[1728]{0:T(1024)(128)(2,1)S(1)} %dynamic-update-slice, bf16[576]{0:T(1024)(128)(2,1)S(1)} %dynamic-update-slice.1, ...), channel_id=2, replica_groups=mesh['dp'=4,'fsdp'=8] {'fsdp'}, use_global_device_ids=true, to_apply=%add.1 | all-reduce | flops 4032 | bytes 16128
  322.9 38.3 %all-gather.29.cloned.1.call-done = bf16[1152,6912]{1,0:T(8,128)(2,1)} async-done(((bf16[288,6912]{1,0:T(8,128)(2,1)}), bf16[1152,6912]{1,0:T(8,128)(2,1)}) %all-gather.29.cloned.1.call-update) | async-done | bytes 15925264 | tf_op jit(solution)/shard_map/all_gather | solution.py:70
  369.4 49.2 %all-gather.31.cloned.1.call-done = bf16[1152,3456]{1,0:T(8,128)(2,1)} async-done(((bf16[288,3456]{1,0:T(8,128)(2,1)}), bf16[1152,3456]{1,0:T(8,128)(2,1)}) %all-gather.31.cloned.1.call-update) | async-done | bytes 7962640 | tf_op jit(solution)/shard_map/all_gather | solution.py:71
  431.4 15.1 %all-gather.33.cloned.1.call-done = bf16[1152,1152]{1,0:T(8,128)(2,1)} async-done(((bf16[288,1152]{1,0:T(8,128)(2,1)}), bf16[1152,1152]{1,0:T(8,128)(2,1)}) %all-gather.33.cloned.1.call-update) | async-done | bytes 2654224 | tf_op jit(solution)/shard_map/all_gather | solution.py:72
  454.7 64.3 %all-gather.35.cloned.1.call-done = bf16[1152,4608]{1,0:T(8,128)(2,1)} async-done(((bf16[288,4608]{1,0:T(8,128)(2,1)}), bf16[1152,4608]{1,0:T(8,128)(2,1)}) %all-gather.35.cloned.1.call-update) | async-done | bytes 10616848 | tf_op jit(solution)/shard_map/all_gather | solution.py:73
  519.0 9.5 multiply_convert_fusion
  528.6 63.0 %all-gather.39.cloned.1.call-done = bf16[4608,1152]{0,1:T(8,128)(2,1)} async-done(((bf16[1152,1152]{0,1:T(8,128)(2,1)}), bf16[4608,1152]{0,1:T(8,128)(2,1)}) %all-gather.39.cloned.1.call-update) | async-done | bytes 10616848 | tf_op jit(solution)/shard_map/all_gather | solution.py:74
  654.0 10.4 convert_bitcast_fusion
  690.2 39.4 %all-gather.43.cloned.1.call-done = bf16[768,3456]{1,0:T(8,128)(2,1)} async-done(((bf16[192,3456]{1,0:T(8,128)(2,1)}), bf16[768,3456]{1,0:T(8,128)(2,1)}) %all-gather.43.cloned.1.call-update) | async-done | bytes 5308432 | tf_op jit(solution)/shard_map/all_gather | solution.py:271
  737.2 14.6 %all-gather.47.cloned.1.call-done = bf16[768,1152]{1,0:T(8,128)(2,1)} async-done(((bf16[192,1152]{1,0:T(8,128)(2,1)}), bf16[768,1152]{1,0:T(8,128)(2,1)}) %all-gather.47.cloned.1.call-update) | async-done | bytes 1769488 | tf_op jit(solution)/shard_map/all_gather | solution.py:274
  751.8 52.3 %all-gather.49.cloned.1.call-done = bf16[768,4608]{1,0:T(8,128)(2,1)} async-done(((bf16[192,4608]{1,0:T(8,128)(2,1)}), bf16[768,4608]{1,0:T(8,128)(2,1)}) %all-gather.49.cloned.1.call-update) | async-done | bytes 7077904 | tf_op jit(solution)/shard_map/all_gather | solution.py:275
  812.9 13.4 %all-gather.55.cloned.1.call-done = bf16[1,768,1152]{2,1,0:T(8,128)(2,1)} async-done(((bf16[1,192,1152]{2,1,0:T(8,128)(2,1)}), bf16[1,768,1152]{2,1,0:T(8,128)(2,1)}) %all-gather.55.cloned.1.call-update) | async-done | bytes 1769488 | tf_op jit(solution)/shard_map/all_gather | solution.py:277
  826.3 52.3 %all-gather.51.cloned.1.call-done = bf16[768,4608]{1,0:T(8,128)(2,1)} async-done(((bf16[192,4608]{1,0:T(8,128)(2,1)}), bf16[768,4608]{1,0:T(8,128)(2,1)}) %all-gather.51.cloned.1.call-update) | async-done | bytes 7077904 | tf_op jit(solution)/shard_map/all_gather | solution.py:276
  899.7 43.4 %reduce-scatter.12.cloned.1.call-done = bf16[288,144]{0,1:T(8,128)(2,1)} async-done(((bf16[288,1152]{0,1:T(8,128)(2,1)}), bf16[288,144]{0,1:T(8,128)(2,1)}) %reduce-scatter.12.cloned.1.call-update) | async-done | bytes 82960 | tf_op jit(solution)/shard_map/reduce_scatter | solution.py:320
  944.6 105.2 %reduce-scatter.16.cloned.1.call-done = bf16[864,288]{1,0:T(8,128)(2,1)} async-done(((bf16[6912,288]{1,0:T(8,128)(2,1)}), bf16[864,288]{1,0:T(8,128)(2,1)}) %reduce-scatter.16.cloned.1.call-update) | async-done | bytes 497680
  1060.1 37.4 %all-reduce.9 = (bf16[4,8,216]{2,0,1:T(4,128)(2,1)S(1)}, bf16[4,8,72]{2,0,1:T(4,128)(2,1)S(1)}, bf16[4,8,144]{2,0,1:T(4,128)(2,1)S(1)}, bf16[4,8,72]{2,0,1:T(4,128)(2,1)S(1)}) all-reduce(bf16[4,8,216]{2,0,1:T(4,128)(2,1)S(1)} %copy-done.20, bf16[4,8,72]{2,0,1:T(4,128)(2,1)S(1)} %copy.101, ...), channel_id=9, replica_groups=mesh['dp'=4,'fsdp'=8] {'fsdp'}, use_global_device_ids=true, to_apply=%region_20.21.clone | all-reduce | flops 16128 | bytes 64512
  1102.4 22.0 %reduce-scatter.18.cloned.1.call-done = bf16[432,288]{1,0:T(8,128)(2,1)} async-done(((bf16[3456,288]{1,0:T(8,128)(2,1)}), bf16[432,288]{1,0:T(8,128)(2,1)}) %reduce-scatter.18.cloned.1.call-update) | async-done | bytes 248848
  1126.4 80.0 %reduce-scatter.20.cloned.1.call-done = bf16[576,288]{1,0:T(8,128)(2,1)} async-done(((bf16[4608,288]{1,0:T(8,128)(2,1)}), bf16[576,288]{1,0:T(8,128)(2,1)}) %reduce-scatter.20.cloned.1.call-update) | async-done | bytes 331792
  1208.5 71.7 %reduce-scatter.14.cloned.1.call-done = bf16[1152,144]{0,1:T(8,128)(2,1)} async-done(((bf16[1152,1152]{0,1:T(8,128)(2,1)}), bf16[1152,144]{0,1:T(8,128)(2,1)}) %reduce-scatter.14.cloned.1.call-update) | async-done | bytes 331792 | tf_op jit(solution)/shard_map/reduce_scatter | solution.py:326
  (252 shorter events, 233.1 us)
Async XLA Ops:
  7.2 78.3 %all-gather.57.cloned.1.call-start = ((), (), s32[]{:S(2)}) async-start(), calls=%async_computation.21 | async-start | bytes 4644864 | tf_op jit(solution)/shard_map/all_gather | solution.py:59
  7.9 130.2 %all-gather.59.cloned.1.call-start = ((), (), s32[]{:S(2)}) async-start(), calls=%async_computation.22 | async-start | bytes 2654208 | tf_op jit(solution)/shard_map/all_gather | solution.py:60
  8.7 194.9 %all-gather.61.cloned.1.call-start = ((), (), s32[]{:S(2)}) async-start(), calls=%async_computation.23 | async-start | bytes 3317760 | tf_op jit(solution)/shard_map/all_gather | solution.py:62
  9.4 250.5 %all-gather.37.cloned.1.call-start = ((), (), s32[]{:S(2)}) async-start(), calls=%async_computation.9 | async-start | bytes 2985984 | tf_op jit(solution)/shard_map/all_gather | solution.py:63
  10.0 351.3 %all-gather.29.cloned.1.call-start = ((), (), s32[]{:S(2)}) async-start(), calls=%async_computation.5 | async-start | bytes 19906560 | tf_op jit(solution)/shard_map/all_gather | solution.py:70
  98.8 319.8 %all-gather.31.cloned.1.call-start = ((), (), s32[]{:S(2)}) async-start(), calls=%async_computation.6 | async-start | bytes 9953280 | tf_op jit(solution)/shard_map/all_gather | solution.py:71
  145.1 301.4 %all-gather.33.cloned.1.call-start = ((), (), s32[]{:S(2)}) async-start(), calls=%async_computation.7 | async-start | bytes 3317760 | tf_op jit(solution)/shard_map/all_gather | solution.py:72
  180.3 338.7 %all-gather.35.cloned.1.call-start = ((), (), s32[]{:S(2)}) async-start(), calls=%async_computation.8 | async-start | bytes 13271040 | tf_op jit(solution)/shard_map/all_gather | solution.py:73
  209.7 111.5 %copy-start.18 = (bf16[1,256,1152]{2,1,0:T(8,128)(2,1)S(1)}, bf16[1,256,1152]{2,1,0:T(8,128)(2,1)}, u32[]{:S(2)}) copy-start(bf16[1,256,1152]{2,1,0:T(8,128)(2,1)} %param.14) | copy-start | bytes 1769476
  209.7 381.8 %all-gather.39.cloned.1.call-start = ((), (), s32[]{:S(2)}) async-start(), calls=%async_computation.10 | async-start | bytes 13271040 | tf_op jit(solution)/shard_map/all_gather | solution.py:74
  259.9 409.7 %all-gather.53.cloned.1.call-start = ((), (), s32[]{:S(2)}) async-start(), calls=%async_computation.19 | async-start | bytes 2211840 | tf_op jit(solution)/shard_map/all_gather | solution.py:273
  322.9 322.1 %copy-start.22 = (f32[192]{0:T(256)}, f32[192]{0:T(256)S(1)}, u32[]{:S(2)}) copy-start(f32[192]{0:T(256)S(1)} %add_rsqrt_fusion.1) | copy-start | bytes 2308
  621.0 48.6 %all-gather.45.cloned.1.call-start = ((), (), s32[]{:S(2)}) async-start(), calls=%async_computation.13 | async-start | bytes 2211840 | tf_op jit(solution)/shard_map/all_gather | solution.py:272
  623.1 67.0 %all-gather.41.cloned.1.call-start = ((), (), s32[]{:S(2)}) async-start(), calls=%async_computation.11 | async-start | bytes 2211840 | tf_op jit(solution)/shard_map/all_gather | solution.py:270
  623.7 105.9 %all-gather.43.cloned.1.call-start = ((), (), s32[]{:S(2)}) async-start(), calls=%async_computation.12 | async-start | bytes 6635520 | tf_op jit(solution)/shard_map/all_gather | solution.py:271
  642.6 109.2 %all-gather.47.cloned.1.call-start = ((), (), s32[]{:S(2)}) async-start(), calls=%async_computation.15 | async-start | bytes 2211840 | tf_op jit(solution)/shard_map/all_gather | solution.py:274
  643.2 160.9 %all-gather.49.cloned.1.call-start = ((), (), s32[]{:S(2)}) async-start(), calls=%async_computation.16 | async-start | bytes 8847360 | tf_op jit(solution)/shard_map/all_gather | solution.py:275
  643.8 182.5 %all-gather.55.cloned.1.call-start = ((), (), s32[]{:S(2)}) async-start(), calls=%async_computation.20 | async-start | bytes 2211840 | tf_op jit(solution)/shard_map/all_gather | solution.py:277
  644.4 234.2 %all-gather.51.cloned.1.call-start = ((), (), s32[]{:S(2)}) async-start(), calls=%async_computation.17 | async-start | bytes 8847360 | tf_op jit(solution)/shard_map/all_gather | solution.py:276
  645.0 298.1 %reduce-scatter.12.cloned.1.call-start = ((), (), s32[]{:S(2)}) async-start(), calls=%async_computation.14 | async-start | bytes 995328 | tf_op jit(solution)/shard_map/reduce_scatter | solution.py:320
  673.6 376.2 %reduce-scatter.16.cloned.1.call-start = ((), (), s32[]{:S(2)}) async-start(), calls=%async_computation.24 | async-start | bytes 5971968
  690.1 434.2 %reduce-scatter.18.cloned.1.call-start = ((), (), s32[]{:S(2)}) async-start(), calls=%async_computation.25 | async-start | bytes 2985984
  736.9 469.5 %reduce-scatter.20.cloned.1.call-start = ((), (), s32[]{:S(2)}) async-start(), calls=%async_computation.26 | async-start | bytes 3981312
  812.8 467.4 %reduce-scatter.14.cloned.1.call-start = ((), (), s32[]{:S(2)}) async-start(), calls=%async_computation.18 | async-start | bytes 2985984 | tf_op jit(solution)/shard_map/reduce_scatter | solution.py:326
  (27 other events, 586.8 us)
Sparse Core Ops, SparseCore 0:
  10.2 75.2 all-gather.56
  87.7 50.3 all-gather.58
  140.3 63.2 all-gather.60
  205.6 54.2 all-gather.36
  261.3 99.9 all-gather.28
  362.7 55.8 all-gather.30
  420.7 25.7 all-gather.32
  448.0 70.9 all-gather.34
  520.6 70.8 all-gather.38
  621.1 20.8 all-gather.52
  643.6 20.7 all-gather.44
  665.8 21.3 all-gather.40
  688.7 40.7 all-gather.42
  731.0 20.7 all-gather.46
  753.2 50.8 all-gather.48
  805.5 20.7 all-gather.54
  827.7 50.8 all-gather.50
  881.8 61.1 reduce-scatter.11
  946.6 103.1 reduce-scatter.15
  1053.7 70.5 reduce-scatter.17
  1128.0 78.3 reduce-scatter.19
  1210.0 70.0 reduce-scatter.13
where the time goes:
time: 1300 us; the launch traced here: 1290 us
  waiting for transfers between devices  917 us (71%)
  blocking collectives  138 us (11%)
  matrix products  108 us (8%)
  local copies, waits for them, and re-layouts  66.9 us (5%)
  other arithmetic  38.9 us (3%)
  between operations  18.1 us (1%)
    unnamed x25, waiting for transfers between devices  212 us
    all_gather x1, waiting for transfers between devices, gather_forward(): lax.all_gather(w_ada, 'fsdp', axis=1, tiled=True)  75.5 us
    unnamed x2, blocking collectives  72.1 us
    reduce_scatter x1, waiting for transfers between devices, shards(): lax.psum_scatter(terms[4].astype(jnp.bfloat16), 'fsdp', scatter_dimension...  71.7 us
    all_gather x1, waiting for transfers between devices, gather_forward(): lax.all_gather(part_one, 'dp', axis=0, tiled=True)  64.3 us
    all_gather x1, waiting for transfers between devices, gather_forward(): lax.all_gather(part_two, 'dp', axis=0, tiled=True)  63 us
    all_gather x1, waiting for transfers between devices, shards(): piece_raised_d = lax.all_gather(d_raised, 'dp', axis=0, tiled=True)  52.3 us
    all_gather x1, waiting for transfers between devices, shards(): piece_act = lax.all_gather(activated, 'dp', axis=0, tiled=True)  52.3 us
  transfers between devices with their start and end apart: 22, of which 19 were waited for; matrix products, arithmetic and copies ran while one was open for 14% of the time, Pallas kernels for 0%

commit v1 on v0

--- a/solution.py
+++ b/solution.py
@@ -1,8 +1,11 @@
+import functools
 import math
 
 import jax
 import jax.numpy as jnp
 from jax import lax
+from jax.experimental import pallas as pl
+from jax.experimental.pallas import tpu as pltpu
 from jax.sharding import PartitionSpec as P
 
 HEADS = 16
@@ -38,15 +41,126 @@
     )
 
 
+def contract(left, right, left_dims, right_dims):
+    return lax.dot_general(
+        left, right, ((left_dims, right_dims), ((), ())), preferred_element_type=jnp.float32
+    )
+
+
+def rows_rows(left, right):
+    return contract(left, right, (0,), (0,))
+
+
+def times_transposed(left, right):
+    return contract(left, right, (1,), (1,))
+
+
+def swap(value, axis, mask):
+    size = lax.axis_size(axis)
+    return lax.ppermute(value, axis, [(index, index ^ mask) for index in range(size)])
+
+
+def pick(pieces, index):
+    return lax.dynamic_index_in_dim(pieces, index, 0, keepdims=False)
+
+
+def put(pieces, value, index):
+    return lax.dynamic_update_index_in_dim(pieces, value, index, 0)
+
+
+def after(value, other):
+    return lax.optimization_barrier((value, other))[0]
+
+
+def ordered(parts, axis):
+    here = lax.axis_index(axis)
+    result = jnp.zeros((len(parts),) + parts[0].shape, parts[0].dtype)
+    for mask, part in enumerate(parts):
+        result = put(result, part, here ^ mask)
+    return result
+
+
+def trade(pieces, axis):
+    size = lax.axis_size(axis)
+    here = lax.axis_index(axis)
+    parts = [pick(pieces, here)]
+    for mask in range(1, size):
+        parts.append(swap(pick(pieces, here ^ mask), axis, mask))
+    return ordered(parts, axis)
+
+
+def spread_small(value, axis):
+    size = lax.axis_size(axis)
+    return ordered([value] + [swap(value, axis, mask) for mask in range(1, size)], axis)
+
+
+def fsdp_masks():
+    size = lax.axis_size("fsdp")
+    inner = size // 4
+    return [inner * step for step in range(1, 4)], list(range(1, inner))
+
+
+def collect(shard):
+    outer, inner = fsdp_masks()
+    parts = {0: shard}
+    for mask in inner:
+        parts[mask] = swap(shard, "fsdp", mask)
+    for wide in outer:
+        parts[wide] = swap(shard, "fsdp", wide)
+    for wide in outer:
+        for mask in inner:
+            parts[wide ^ mask] = swap(parts[wide], "fsdp", mask)
+    return [parts[mask] for mask in range(lax.axis_size("fsdp"))]
+
+
+def reduce_blocks(blocks):
+    outer, inner = fsdp_masks()
+    here = lax.axis_index("fsdp")
+    wide_all = [0] + outer
+    kept = {wide: pick(blocks, here ^ wide).astype(jnp.float32) for wide in wide_all}
+    for mask in inner:
+        leaving = jnp.stack([pick(blocks, here ^ (wide ^ mask)) for wide in wide_all])
+        arrived = swap(leaving, "fsdp", mask)
+        for place, wide in enumerate(wide_all):
+            kept[wide] = kept[wide] + arrived[place].astype(jnp.float32)
+    total = kept[0]
+    for wide in outer:
+        total = total + swap(kept[wide].astype(jnp.bfloat16), "fsdp", wide).astype(jnp.float32)
+    return total
+
+
+def spread_dp(value):
+    size = lax.axis_size("dp")
+    slots = {0: value}
+    mask = size // 2
+    while mask:
+        keys = sorted(slots)
+        arrived = swap(jnp.stack([slots[key] for key in keys]), "dp", mask)
+        for place, key in enumerate(keys):
+            slots[key ^ mask] = arrived[place]
+        mask //= 2
+    return jnp.stack([slots[key] for key in range(size)])
+
+
+def reduce_dp(slots):
+    size = lax.axis_size("dp")
+    held = {key: slots[key] for key in range(size)}
+    mask = 1
+    while mask < size:
+        leaving = sorted(key for key in held if key & mask)
+        arrived = swap(
+            jnp.stack([held[key].astype(jnp.bfloat16) for key in leaving]), "dp", mask
+        )
+        for place, key in enumerate(leaving):
+            held[key ^ mask] = held[key ^ mask] + arrived[place].astype(jnp.float32)
+            del held[key]
+        mask *= 2
+    return held[0]
+
+
 def inner_rows(left, right):
     return lax.dot_general(
         left, right, (((0,), (0,)), ((), ())), preferred_element_type=jnp.float32
-    )
-
-
-def times_transposed(left, right):
-    return lax.dot_general(
-        left, right, (((1,), (1,)), ((), ())), preferred_element_type=jnp.float32
     )
 
 
@@ -123,7 +237,7 @@
     return jnp.sum(matrix.astype(jnp.float32), axis=0)
 
 
-def shards(
+def plain_shards(
     patches_in,
     condition,
     keep_count,
@@ -355,40 +469,627 @@
     )
 
 
+MESH = pl.DeviceIdType.MESH
+
+
+def remote(source, target, send, recv, device):
+    return pltpu.make_async_remote_copy(
+        src_ref=source,
+        dst_ref=target,
+        send_sem=send,
+        recv_sem=recv,
+        device_id=device,
+        device_id_type=MESH,
+    )
+
+
+def greet(devices):
+    barrier = pltpu.get_barrier_semaphore()
+    for device in devices:
+        pl.semaphore_signal(barrier, 1, device_id=device, device_id_type=MESH)
+    pl.semaphore_wait(barrier, len(devices))
+
+
+def everyone_body(n_dp, n_fs, source, target, send, recv, local):
+    d_at, f_at = lax.axis_index("dp"), lax.axis_index("fsdp")
+    own = d_at * n_fs + f_at
+    others = [(a, b) for a in range(n_dp) for b in range(n_fs) if a or b]
+    greet([(d_at ^ a, f_at ^ b) for a, b in others])
+    copies = []
+    for place, (a, b) in enumerate(others):
+        there = (d_at ^ a) * n_fs + (f_at ^ b)
+        copies.append(
+            remote(
+                source.at[there],
+                target.at[own],
+                send.at[place],
+                recv.at[place],
+                (d_at ^ a, f_at ^ b),
+            )
+        )
+    for copy in copies:
+        copy.start()
+    stay = pltpu.make_async_copy(source.at[own], target.at[own], local)
+    stay.start()
+    stay.wait()
+    for copy in copies:
+        copy.wait()
+
+
+def exchange_everyone(pieces, ident):
+    n_dp, n_fs = lax.axis_size("dp"), lax.axis_size("fsdp")
+    count = n_dp * n_fs - 1
+    return pl.pallas_call(
+        functools.partial(everyone_body, n_dp, n_fs),
+        out_shape=jax.ShapeDtypeStruct(pieces.shape, pieces.dtype),
+        in_specs=[pl.BlockSpec(memory_space=pltpu.VMEM)],
+        out_specs=pl.BlockSpec(memory_space=pltpu.VMEM),
+        scratch_shapes=[
+            pltpu.SemaphoreType.DMA((count,)),
+            pltpu.SemaphoreType.DMA((count,)),
+            pltpu.SemaphoreType.DMA,
+        ],
+        compiler_params=pltpu.CompilerParams(collective_id=ident, has_side_effects=True),
+        name="exchange_everyone",
+    )(pieces)
+
+
+def tiles(rows, height):
+    width = height * 128
+    return jnp.pad(rows, ((0, 0), (0, width - rows.shape[1]))).reshape(-1, height, 128)
+
+
+def untiles(pieces, width):
+    return pieces.reshape(pieces.shape[0], -1)[:, :width]
+
+
+def normed(value):
+    centred = value - jnp.mean(value, axis=-1, keepdims=True)
+    rstd = lax.rsqrt(jnp.mean(centred * centred, axis=-1, keepdims=True) + epsilon)
+    return centred * rstd, rstd
+
+
+def head_place(block, per_shard):
+    return block // per_shard, block % per_shard
+
+
+def forward_body(
+    sizes,
+    att_ref,
+    one_ref,
+    two_ref,
+    kept_ref,
+    mod_ref,
+    bias_ref,
+    out_bias_ref,
+    cot_ref,
+    count_ref,
+    att_all,
+    one_all,
+    two_all,
+    hidden_one_ref,
+    projected_ref,
+    mixed_ref,
+    attended_ref,
+    hidden_all,
+    branch_all,
+    proj_dense,
+    send_z,
+    send_y,
+    send_x,
+    recv_w,
+    send_e,
+    recv_e,
+    local,
+):
+    n_dp, n_fs, heads, size, cols = sizes
+    d_at, f_at = lax.axis_index("dp"), lax.axis_index("fsdp")
+    slots, features = kept_ref.shape
+    row_width = att_ref.shape[0]
+    unit = one_ref.shape[0]
+    inner = n_fs // 4
+    wide_masks = [inner * step for step in range(1, 4)]
+    near_masks = list(range(1, inner))
+    dp_masks = []
+    mask = n_dp // 2
+    while mask:
+        dp_masks.append(mask)
+        mask //= 2
+    low = jnp.bfloat16
+    full = jnp.float32
+    greet(
+        [(d_at, f_at ^ b) for b in wide_masks + near_masks] + [(d_at ^ a, f_at) for a in dp_masks]
+    )
+
+    def slot(array, a, b):
+        if array == 0:
+            start = pl.multiple_of((d_at ^ a) * row_width, 16)
+            return att_all.at[f_at ^ b, pl.ds(start, row_width), :]
+        start = pl.multiple_of((f_at ^ b) * unit, 16)
+        return (one_all if array == 1 else two_all).at[pl.ds(start, unit), :]
+
+    def block(array, a, b):
+        if a == 0 and b == 0:
+            return (att_ref, one_ref, two_ref)[array]
+        return slot(array, a, b)
+
+    started = []
+
+    def send(array, a, b, axis, mask, sem):
+        device = (d_at ^ mask, f_at) if axis == 0 else (d_at, f_at ^ mask)
+        to_a, to_b = (a ^ mask, b) if axis == 0 else (a, b ^ mask)
+        copy = remote(
+            block(array, a, b), slot(array, a, b), sem, recv_w.at[array, to_a, to_b], device
+        )
+        copy.start()
+        started.append(copy)
+
+    def arrive(array, a, b):
+        place = slot(array, a, b)
+        pltpu.make_async_copy(place, place, recv_w.at[array, a, b]).wait()
+
+    def send_wide(array):
+        for place, mask in enumerate(wide_masks):
+            send(array, 0, 0, 1, mask, send_z.at[array, place])
+
+    def send_near(array, wide, place):
+        for step, mask in enumerate(near_masks):
+            send(array, 0, wide, 1, mask, send_y.at[array, place, step])
+
+    send_wide(0)
+    send_near(0, 0, 0)
+    send_wide(1)
+    send_wide(2)
+
+    def onward(a, b):
+        for step, mask in enumerate(dp_masks):
+            if a & (mask | (mask - 1)) == 0:
+                send(0, a, b, 0, mask, send_x.at[a, b, step])
+
+    onward(0, 0)
+    keep_own = pltpu.make_async_copy(att_ref, slot(0, 0, 0), local.at[1])
+    keep_own.start()
+    keep_one = pltpu.make_async_copy(one_ref, slot(1, 0, 0), local.at[2])
+    keep_one.start()
+    keep_two = pltpu.make_async_copy(two_ref, slot(2, 0, 0), local.at[3])
+    keep_two.start()
+
+    kept = kept_ref[...]
+    mods = [mod_ref[row : row + 1, :] for row in range(6)]
+    normed_one, _ = normed(kept)
+    hidden_one = (normed_one * (1.0 + mods[1]) + mods[0]).astype(low)
+    hidden_one_ref[...] = hidden_one
+    branch_all[0] = (mods[5] * cot_ref[...].astype(full)).astype(low)
+
+    for mask in near_masks:
+        arrive(0, 0, mask)
+        onward(0, mask)
+    for place, wide in enumerate(wide_masks):
+        arrive(0, 0, wide)
+        send_near(0, wide, place + 1)
+        onward(0, wide)
+    send_near(1, 0, 0)
+    send_near(2, 0, 0)
+    for wide in wide_masks:
+        for mask in near_masks:
+            arrive(0, 0, wide ^ mask)
+            onward(0, wide ^ mask)
+    order = sorted(range(1, n_dp), key=lambda a: (-(a & -a), a))
+    for a in order:
+        for b in range(n_fs):
+            arrive(0, a, b)
+            onward(a, b)
+    keep_own.wait()
+
+    def spread(buffer, kind):
+        held = [0]
+        for step, mask in enumerate(dp_masks):
+            copies = []
+            for key in held:
+                copies.append(
+                    remote(
+                        buffer.at[key],
+                        buffer.at[key ^ mask],
+                        send_e.at[kind, key ^ mask],
+                        recv_e.at[kind, key ^ mask],
+                        (d_at ^ mask, f_at),
+                    )
+                )
+                copies[-1].start()
+            yield copies
+            held = sorted(held + [key ^ mask for key in held])
+
+    for copies in spread(branch_all, 0):
+        for copy in copies:
+            copy.wait()
+
+    per_shard = cols // size
+    for f in range(n_fs):
+        out = jnp.dot(hidden_one, att_all[f, :, :cols], preferred_element_type=full)
+        projected_ref[f] = (out + bias_ref[f]).astype(low)
+
+    allowed = lax.broadcasted_iota(jnp.int32, (slots, slots), 1) < count_ref[0]
+    factor = 1.0 / math.sqrt(size)
+    for h in range(heads):
+        parts = []
+        for kind in range(3):
+            f, j = head_place(kind * heads + h, per_shard)
+            parts.append(projected_ref[f, :, j * size : (j + 1) * size])
+        scores = contract(parts[0], parts[1], (1,), (1,)) * factor
+        scores = jnp.where(allowed, scores, negative)
+        top = jnp.max(scores, axis=-1, keepdims=True)
+        exponent = jnp.exp(scores - top)
+        softmax = exponent / jnp.sum(exponent, axis=-1, keepdims=True)
+        mix = jnp.dot(softmax.astype(low), parts[2], preferred_element_type=full)
+        mixed_ref[:, h * size : (h + 1) * size] = mix.astype(low)
+
+    width = proj_dense.shape[1] // n_fs
+    for f in range(n_fs):
+        proj_dense[:, f * width : (f + 1) * width] = att_all[f, :, cols : cols + width]
+    attended = (
+        jnp.dot(mixed_ref[...], proj_dense[...], preferred_element_type=full) + out_bias_ref[...]
+    )
+    attended_ref[...] = attended
+    middle = kept + mods[2] * attended
+    normed_two, _ = normed(middle)
+    hidden_all[0] = (normed_two * (1.0 + mods[4]) + mods[3]).astype(low)
+    for copies in spread(hidden_all, 1):
+        for copy in copies:
+            copy.wait()
+
+    for array in (1, 2):
+        for place, wide in enumerate(wide_masks):
+            arrive(array, 0, wide)
+            send_near(array, wide, place + 1)
+    for array in (1, 2):
+        for wide in [0] + wide_masks:
+            for mask in near_masks:
+                arrive(array, 0, wide ^ mask)
+    keep_one.wait()
+    keep_two.wait()
+    for copy in started:
+        copy.wait_send()
+
+
+def forward_kernel(att, one_block, two_block, kept, mods, bias, out_bias, cot, count, cols):
+    n_dp, n_fs = lax.axis_size("dp"), lax.axis_size("fsdp")
+    slots, features = kept.shape
+    unit = one_block.shape[0]
+    size = features // HEADS
+    inner = n_fs // 4
+    low, full = jnp.bfloat16, jnp.float32
+    vmem = pl.BlockSpec(memory_space=pltpu.VMEM)
+    shapes = [
+        ((n_fs, features, att.shape[1]), low),
+        ((n_fs * unit, features), low),
+        ((n_fs * two_block.shape[0], two_block.shape[1]), low),
+        ((slots, features), low),
+        ((n_fs, slots, cols), low),
+        ((slots, features), low),
+        ((slots, features), full),
+        ((n_dp, slots, features), low),
+        ((n_dp, slots, features), low),
+        ((features, features), low),
+    ]
+    return pl.pallas_call(
+        functools.partial(forward_body, (n_dp, n_fs, HEADS, size, cols)),
+        out_shape=[jax.ShapeDtypeStruct(shape, kind) for shape, kind in shapes],
+        in_specs=[vmem] * 8 + [pl.BlockSpec(memory_space=pltpu.SMEM)],
+        out_specs=[vmem] * len(shapes),
+        scratch_shapes=[
+            pltpu.SemaphoreType.DMA((3, 3)),
+            pltpu.SemaphoreType.DMA((3, 4, max(inner - 1, 1))),
+            pltpu.SemaphoreType.DMA((n_dp, n_fs, n_dp.bit_length() - 1)),
+            pltpu.SemaphoreType.DMA((3, n_dp, n_fs)),
+            pltpu.SemaphoreType.DMA((2, n_dp)),
+            pltpu.SemaphoreType.DMA((2, n_dp)),
+            pltpu.SemaphoreType.DMA((4,)),
+        ],
+        compiler_params=pltpu.CompilerParams(
+            collective_id=5, has_side_effects=True, vmem_limit_bytes=64 * 1024 * 1024 - 65536
+        ),
+        name="forward",
+    )(att, one_block, two_block, kept, mods, bias, out_bias, cot, count)
+
+
+def shards(
+    patches_in,
+    condition,
+    keep_count,
+    keep_index,
+    w_ada,
+    b_ada,
+    w_qkv,
+    qv_bias,
+    w_proj,
+    w_fc1,
+    fc1_bias,
+    w_fc2,
+    out_bias,
+    cotangent,
+):
+    n_dp, n_fs = lax.axis_size("dp"), lax.axis_size("fsdp")
+    n_all = n_dp * n_fs
+    d_at, f_at = lax.axis_index("dp"), lax.axis_index("fsdp")
+    kept_slots = keep_index.shape[1]
+    features = patches_in.shape[2]
+    hidden_units = w_fc2.shape[0] * n_dp
+    head_size = features // HEADS
+    factor = 1.0 / math.sqrt(head_size)
+    head_shape = (kept_slots, HEADS, head_size)
+    row_width = features // n_dp
+    low = jnp.bfloat16
+    full = jnp.float32
+
+    unit_width = w_fc1.shape[1] // n_dp
+    one_pieces = w_fc1.reshape(row_width, n_dp, unit_width).transpose(1, 2, 0)
+    two_pieces = (
+        w_fc2.reshape(n_fs // n_dp, n_dp, unit_width, w_fc2.shape[1])
+        .transpose(1, 3, 0, 2)
+        .reshape(n_dp, w_fc2.shape[1], -1)
+    )
+    both_pieces = jnp.concatenate([one_pieces, two_pieces], axis=2)
+    cond_float = condition.astype(full)
+    signal = swish(cond_float).astype(low)
+    message = jnp.concatenate(
+        [signal, b_ada[None], qv_bias[None], fc1_bias[None], out_bias[None]], axis=1
+    )
+    sizes = [features, b_ada.shape[0], qv_bias.shape[0], fc1_bias.shape[0], out_bias.shape[0]]
+    ends = [sum(sizes[: place + 1]) for place in range(len(sizes))]
+    shared = exchange_everyone(
+        jnp.broadcast_to(tiles(message, 16), (n_all, 16, 128)), 1
+    )
+    shared = untiles(shared, ends[-1])
+    both = trade(both_pieces, "dp")
+    one_block = both[:, :, :row_width].transpose(1, 0, 2).reshape(unit_width, features)
+    two_block = (
+        both[:, :, row_width:].transpose(1, 0, 2).reshape(w_fc2.shape[1], hidden_units // n_dp)
+    )
+    signals = lax.dynamic_slice_in_dim(shared[:, :features], d_at * row_width, row_width, 1)
+    ada_bias, qv_full, one_bias, out_full = [
+        shared[:, ends[place] : ends[place + 1]].reshape(-1).astype(full) for place in range(4)
+    ]
+
+    partial_mod = jnp.dot(signals, w_ada, preferred_element_type=full)
+    rows_mod = untiles(exchange_everyone(tiles(partial_mod, 8), 2), partial_mod.shape[1])
+    modulation = jnp.sum(rows_mod.reshape(n_dp, n_fs, -1), axis=0).reshape(1, -1) + ada_bias
+    mods = modulation.reshape(6, features)
+    shift_one, scale_one, gate_one, shift_two, scale_two, gate_two = [
+        mods[row : row + 1] for row in range(6)
+    ]
+    own_one_bias = pick(
+        one_bias.reshape(n_fs, n_dp, unit_width).transpose(1, 0, 2), d_at
+    ).reshape(-1)
+
+    indices = keep_index[0]
+    inputs = patches_in[0]
+    kept_in = jnp.take(inputs, indices, axis=0).astype(full)
+    qkv_bias = jnp.concatenate(
+        [qv_full[:features], jnp.zeros((features,), full), qv_full[features:]]
+    )
+    qkv_cols = w_qkv.shape[1]
+    (
+        att_all,
+        one_full,
+        two_full,
+        hidden_one,
+        projected_all,
+        mixed_low,
+        attended,
+        hidden_two_all,
+        d_branch_all,
+        proj_full,
+    ) = forward_kernel(
+        jnp.concatenate([w_qkv, w_proj], axis=1),
+        one_block,
+        two_block,
+        kept_in,
+        mods,
+        qkv_bias.reshape(n_fs, 1, qkv_cols),
+        out_full[None, :features],
+        cotangent[0],
+        keep_count,
+        qkv_cols,
+    )
+    hidden_two_all = hidden_two_all.reshape(n_dp * kept_slots, features)
+    d_branch_all = d_branch_all.reshape(n_dp * kept_slots, features)
+    d_branch = d_branch_all[:kept_slots]
+    qkv_full = att_all[:, :, :qkv_cols].transpose(1, 0, 2).reshape(features, -1)
+    projected = projected_all.transpose(1, 0, 2).reshape(kept_slots, -1)
+    allowed = (jnp.arange(kept_slots) < keep_count[0])[None, None, :]
+    normed_one, rstd_one = layer_norm(kept_in)
+    middle = kept_in + gate_one * attended
+    normed_two, rstd_two = layer_norm(middle)
+    upstream = cotangent[0].astype(full)
+    queries = projected[:, :features].reshape(head_shape)
+    key_rows = projected[:, features : 2 * features].reshape(head_shape)
+    values = projected[:, 2 * features :].reshape(head_shape)
+    scores = jnp.einsum("qhe,khe->hqk", queries, key_rows, preferred_element_type=full) * factor
+    scores = jnp.where(allowed, scores, negative)
+    top_score = jnp.max(scores, axis=-1, keepdims=True)
+    exponent = jnp.exp(scores - top_score)
+    softmax = exponent / jnp.sum(exponent, axis=-1, keepdims=True)
+    softmax_low = softmax.astype(low)
+
+    raised = times_transposed(hidden_two_all, one_full) + own_one_bias
+    activated = gelu_tanh(raised).astype(low)
+    grad_two = rows_rows(d_branch_all, activated).astype(low)
+    branch_part = times_transposed(activated, two_full)
+    branch = (
+        reduce_dp(branch_part.reshape(n_dp, kept_slots, features)) + out_full[features:]
+    )
+    block_out = (middle + gate_two * branch).astype(low)
+    d_gate_two = jnp.sum(upstream * branch, axis=0)
+    d_activated = jnp.dot(d_branch_all, two_full, preferred_element_type=full)
+    unused, gelu_pull = jax.vjp(gelu_tanh, raised)
+    d_raised = gelu_pull(d_activated)[0].astype(low)
+    d_hidden_part = jnp.dot(d_raised, one_full, preferred_element_type=full)
+    d_hidden_two = reduce_dp(d_hidden_part.reshape(n_dp, kept_slots, features))
+    grad_one = rows_rows(d_raised, hidden_two_all).astype(low)
+    one_sums = jnp.sum(d_raised.astype(full), axis=0)
+    final_two = reduce_blocks(grad_two.reshape(n_fs, -1, hidden_units // n_dp)).astype(low)
+    final_one = reduce_blocks(grad_one.reshape(n_fs, unit_width, features)).astype(low)
+    one_out = trade(final_one.reshape(unit_width, n_dp, row_width).transpose(1, 0, 2), "dp")
+    one_out = one_out.reshape(-1, row_width).T.astype(full)
+    two_out = trade(
+        final_two.reshape(final_two.shape[0], n_dp, -1).transpose(1, 0, 2), "dp"
+    )
+    two_out = (
+        two_out.reshape(n_dp, final_two.shape[0], n_fs // n_dp, unit_width)
+        .transpose(2, 0, 3, 1)
+        .reshape(w_fc2.shape)
+        .astype(full)
+    )
+
+    d_shift_two = jnp.sum(d_hidden_two, axis=0)
+    d_scale_two = jnp.sum(d_hidden_two * normed_two, axis=0)
+    d_middle = upstream + norm_back(d_hidden_two * (1.0 + scale_two), normed_two, rstd_two)
+    d_gate_one = jnp.sum(d_middle * attended, axis=0)
+    d_attended = (gate_one * d_middle).astype(low)
+    d_mixed = times_transposed(d_attended, proj_full).astype(low).reshape(head_shape)
+    d_softmax = jnp.einsum("qhe,khe->hqk", d_mixed, values, preferred_element_type=full)
+    row_delta = jnp.sum(d_softmax * softmax, axis=-1, keepdims=True)
+    d_scores = (softmax * (d_softmax - row_delta)).astype(low)
+    d_queries = jnp.einsum("hqk,khe->qhe", d_scores, key_rows, preferred_element_type=full)
+    d_keys = jnp.einsum("hqk,qhe->khe", d_scores, queries, preferred_element_type=full)
+    d_values = jnp.einsum("hqk,qhe->khe", softmax_low, d_mixed, preferred_element_type=full)
+    d_projected = jnp.concatenate(
+        [
+            (d_queries * factor).reshape(kept_slots, features),
+            (d_keys * factor).reshape(kept_slots, features),
+            d_values.reshape(kept_slots, features),
+        ],
+        axis=1,
+    ).astype(low)
+    d_hidden_one = times_transposed(d_projected, qkv_full)
+    d_shift_one = jnp.sum(d_hidden_one, axis=0)
+    d_scale_one = jnp.sum(d_hidden_one * normed_one, axis=0)
+    d_kept = d_middle + norm_back(d_hidden_one * (1.0 + scale_one), normed_one, rstd_one)
+    grad_patches = jnp.zeros(inputs.shape, full).at[indices].set(d_kept, unique_indices=True)[None]
+
+    def own_rows(rows):
+        return trade(rows.reshape(kept_slots, n_dp, row_width).transpose(1, 0, 2), "dp").reshape(
+            n_dp * kept_slots, row_width
+        )
+
+    def by_index(rows):
+        here = lax.axis_index("dp")
+        slots = spread_dp(rows)
+        return ordered([slots[mask] for mask in range(n_dp)], "dp").reshape(
+            n_dp * kept_slots, -1
+        )
+
+    grad_proj = rows_rows(own_rows(mixed_low), by_index(d_attended)).astype(low)
+    grad_qkv = rows_rows(own_rows(hidden_one), by_index(d_projected)).astype(low)
+    proj_out = reduce_blocks(grad_proj.reshape(row_width, n_fs, -1).transpose(1, 0, 2))
+    qkv_out = reduce_blocks(grad_qkv.reshape(row_width, n_fs, -1).transpose(1, 0, 2))
+
+    d_modulation = jnp.concatenate(
+        [d_shift_one, d_scale_one, d_gate_one, d_shift_two, d_scale_two, d_gate_two]
+    ).astype(low)
+    group_d = trade(d_modulation.reshape(n_fs, -1), "fsdp")
+    all_d = spread_small(group_d, "dp").reshape(n_all, -1)
+    grad_ada = rows_rows(signals, all_d)
+    part_signal = times_transposed(all_d, w_ada).reshape(n_dp, n_fs, row_width)
+    group_signal = jnp.sum(trade(part_signal.transpose(1, 0, 2), "fsdp"), axis=0)
+    d_signal = trade(group_signal, "dp").reshape(1, features)
+    unused_too, swish_pull = jax.vjp(swish, cond_float)
+    grad_condition = swish_pull(d_signal)[0]
+
+    sums = jnp.sum(d_projected.astype(full), axis=0)
+    one_spread = jnp.zeros((n_fs, n_dp, unit_width), full)
+    one_spread = lax.dynamic_update_index_in_dim(
+        one_spread, one_sums.reshape(n_fs, unit_width), d_at, 1
+    )
+    bias_parts = [
+        d_modulation.astype(full),
+        jnp.concatenate([sums[:features], sums[2 * features :]]),
+        one_spread.reshape(-1),
+        jnp.concatenate(
+            [
+                jnp.sum(d_attended.astype(full), axis=0),
+                jnp.sum(d_branch.astype(full), axis=0),
+            ]
+        ),
+    ]
+    bias_all = jnp.concatenate([part.reshape(n_all, -1) for part in bias_parts], axis=1)
+    bias_all = bias_all.reshape(n_dp, n_fs, -1)
+    bias_group = jnp.sum(trade(bias_all.transpose(1, 0, 2), "fsdp"), axis=0)
+    bias_own = jnp.sum(trade(bias_group, "dp"), axis=0)
+    starts = [end - features for end in ends]
+    ada_out, qv_out, bias_out, out_out = [
+        bias_own[starts[place] : starts[place + 1]] for place in range(4)
+    ]
+    return (
+        block_out[None],
+        grad_patches,
+        grad_condition,
+        grad_ada,
+        ada_out,
+        qkv_out,
+        qv_out,
+        proj_out,
+        one_out,
+        bias_out,
+        two_out,
+        out_out,
+    )
+
+
+def kernels_fit(*arrays):
+    w_qkv, w_fc1 = arrays[6], arrays[9]
+    features = arrays[0].shape[2]
+    unit_width = w_fc1.shape[1] // lax.axis_size("dp")
+    return (
+        w_qkv.shape[1] % (features // HEADS) == 0
+        and w_qkv.shape[0] % 16 == 0
+        and unit_width % 16 == 0
+        and unit_width == arrays[11].shape[1]
+        and lax.axis_size("fsdp") % 4 == 0
+    )
+
+
 def solution(mesh):
+    both = ("dp", "fsdp")
+    weight = P("dp", "fsdp")
+    flat = P(both)
     placed = (
-        P(("dp", "fsdp"), None, None),
-        P(("dp", "fsdp"), None),
-        P(("dp", "fsdp")),
-        P(("dp", "fsdp"), None),
-        P("dp", "fsdp"),
-        P(("dp", "fsdp")),
-        P("dp", "fsdp"),
-        P(("dp", "fsdp")),
-        P("dp", "fsdp"),
-        P("dp", "fsdp"),
-        P(("dp", "fsdp")),
-        P("dp", "fsdp"),
-        P(("dp", "fsdp")),
-        P(("dp", "fsdp"), None, None),
-    )
+        P(both, None, None),
+        P(both, None),
+        flat,
+        P(both, None),
+        weight,
+        flat,
+        weight,
+        flat,
+        weight,
+        weight,
+        flat,
+        weight,
+        flat,
+        P(both, None, None),
+    )
+
+    def chosen(*arrays):
+        return (shards if kernels_fit(*arrays) else plain_shards)(*arrays)
+
     return jax.shard_map(
-        shards,
+        chosen,
         mesh=mesh,
         in_specs=placed,
         out_specs=(
-            P(("dp", "fsdp"), None, None),
-            P(("dp", "fsdp"), None, None),
-            P(("dp", "fsdp"), None),
-            P("dp", "fsdp"),
-            P(("dp", "fsdp")),
-            P("dp", "fsdp"),
-            P(("dp", "fsdp")),
-            P("dp", "fsdp"),
-            P("dp", "fsdp"),
-            P(("dp", "fsdp")),
-            P("dp", "fsdp"),
-            P(("dp", "fsdp")),
+            P(both, None, None),
+            P(both, None, None),
+            P(both, None),
+            weight,
+            flat,
+            weight,
+            flat,
+            weight,
+            weight,
+            flat,
+            weight,
+            flat,
         ),
         check_vma=False,
     )

time: 1300 us -> 682 us (0.52)
  waiting for transfers between devices: 917 us -> 140 us
  Pallas kernels: 0 us -> 186 us
  blocking collectives: 138 us -> 0 us
  local copies, waits for them, and re-layouts: 66.9 us -> 170 us
  starting transfers between devices: 1.34 us -> 75.9 us
  matrix products: 108 us -> 50 us
  between operations: 18.1 us -> 3.41 us
    all_gather x17 -> x0, waiting for transfers between devices: 590 us -> none  [the longest x1 75.5 us: gather_forward(): lax.all_gather(w_ada, 'fsdp', axis=1, tiled=True)]
    unnamed x25 -> x0, waiting for transfers between devices: 212 us -> none
    pallas_call x0 -> x3, Pallas kernels: none -> 186 us  [the longest x1 163 us: forward_kernel(): pl.pallas_call(functools.partial(forward_body, (n_dp, n_fs, HEADS, size,...]
    ppermute x0 -> x69, waiting for transfers between devices: none -> 140 us  [swap(): lax.ppermute(value, axis, [(index, index ^ mask) for index in range(size)])]
    reduce_scatter x2 -> x0, waiting for transfers between devices: 115 us -> none  [the longest x1 71.7 us: shards(): lax.psum_scatter(terms[4].astype(jnp.bfloat16), 'fsdp', scatter_dimension...]
    ppermute x0 -> x69, starting transfers between devices: none -> 75.9 us  [swap(): lax.ppermute(value, axis, [(index, index ^ mask) for index in range(size)])]
    unnamed x2 -> x0, blocking collectives: 72.1 us -> none
    all_gather x7 -> x0, blocking collectives: 66.4 us -> none  [the longest x1 34 us: gather_forward(): lax.all_gather(w_proj, 'fsdp', axis=1, tiled=True)]
  transfers between devices with their start and end apart: 22 -> 69, of which waited for: 19 -> 20; matrix products, arithmetic and copies ran while one was open for 14% -> 28% of each run, Pallas kernels for 0% -> 4%
where the time goes in v1:
time: 682 us; the launch traced here: 673 us
  Pallas kernels  186 us (27%)
  local copies, waits for them, and re-layouts  170 us (25%)
  waiting for transfers between devices  140 us (21%)
  starting transfers between devices  75.9 us (11%)
  matrix products  50 us (7%)
  other arithmetic  47.4 us (7%)
    pallas_call x1, Pallas kernels, forward_kernel(): pl.pallas_call(functools.partial(forward_body, (n_dp, n_fs, HEADS, size,...  163 us
    ppermute x69, waiting for transfers between devices, swap(): lax.ppermute(value, axis, [(index, index ^ mask) for index in range(size)])  140 us
    ppermute x69, starting transfers between devices, swap(): lax.ppermute(value, axis, [(index, index ^ mask) for index in range(size)])  75.9 us
    dynamic_update_slice x62, local copies, waits for them, and re-layouts, put(): return lax.dynamic_update_index_in_dim(pieces, value, index, 0)  49.2 us
    dot_general x10, matrix products, contract(): lax.dot_general(left, right, ((left_dims, right_dims), ((), ())), preferr...  31.7 us
    pallas_call x2, Pallas kernels, exchange_everyone(): pl.pallas_call(functools.partial(everyone_body, n_dp, n_fs), out_shape=ja...  23.6 us
    another operation x19, local copies, waits for them, and re-layouts  21.9 us
    unnamed x202, local copies, waits for them, and re-layouts  20.6 us
  transfers between devices with their start and end apart: 69, of which 20 were waited for; matrix products, arithmetic and copies ran while one was open for 28% of the time, Pallas kernels for 4%

profile of v1, /device:TPU:0, one launch (start us, length us, event | category | flops | bytes accessed | tf_op | source)
XLA Modules:
  0.0 673.2 jit_solution(1495474033068645170)
XLA Ops:
  8.9 11.9 %exchange_everyone.2 = bf16[32,16,128]{2,1,0:T(8,128)(2,1)} custom-call(bf16[32,16,128]{2,1,0:T(8,128)(2,1)} %broadcast_in_dim.281.source), custom_call_target="tpu_custom_call" | custom-call | tf_op jit(solution)/shard_map/exchange_everyone/pallas_call | solution.py:522
  25.4 11.7 %exchange_everyone.3 = f32[32,8,128]{2,1,0:T(8,128)} custom-call(f32[32,8,128]{2,1,0:T(8,128)} %bitcast.491), custom_call_target="tpu_custom_call" | custom-call | tf_op jit(solution)/shard_map/exchange_everyone/pallas_call | solution.py:522
  44.5 5.7 dynamic_update_slice.207
  52.6 5.7 dynamic_update_slice.208
  58.3 5.7 dynamic_update_slice.209
  64.1 5.7 dynamic_update_slice.210
  72.3 162.5 %forward.1 = (bf16[8,1152,576]{2,1,0:T(8,128)(2,1)}, bf16[1152,1152]{1,0:T(8,128)(2,1)}, bf16[1152,1152]{1,0:T(8,128)(2,1)}, bf16[192,1152]{1,0:T(8,128)(2,1)}, ...) custom-call(bf16[288,576]{1,0:T(8,128)(2,1)} %pad_maximum_fusion.11., ...), custom_call_target="tpu_custom_call" | custom-call | tf_op jit(solution)/shard_map/forward/pallas_call | solution.py:774
  235.9 5.1 convolution_add_fusion
  241.1 5.5 fusion.110
  246.6 5.4 convert_reduce_fusion
  256.1 4.4 fusion.111
  268.8 7.9 %slice_bitcast_fusion = bf16[1152,8,432]{2,0,1:T(8,128)(2,1)} fusion(bf16[8,1152,576]{2,1,0:T(8,128)(2,1)} %get-tuple-element.29), kind=kLoop, calls=%fused_computation.3 | loop fusion | bytes 15925248 | tf_op jit(solution)/shard_map/transpose | solution.py:897
  276.7 11.7 %copy.193 = bf16[1152,8,432]{0,2,1:T(8,128)(2,1)} copy(bf16[1152,8,432]{2,0,1:T(8,128)(2,1)} %slice_bitcast_fusion) | data formatting | bytes 15925248 | tf_op jit(solution)/shard_map/transpose | solution.py:897
  344.9 22.9 %collective-permute-done.62 = bf16[4,144,1152]{2,1,0:T(8,128)(2,1)S(1)} collective-permute-done((bf16[4,144,1152]{2,1,0:T(8,128)(2,1)}, bf16[4,144,1152]{2,1,0:T(8,128)(2,1)S(1)}, u32[]{:S(2)}, u32[]{:S(2)}) %collective-permute-start.62) | collective-permute-done | bytes 1327136 | tf_op jit(solution)/shard_map/ppermute | solution.py:60
  370.6 25.5 %collective-permute-done.55 = bf16[4,144,1152]{2,1,0:T(8,128)(2,1)S(1)} collective-permute-done((bf16[4,144,1152]{2,1,0:T(8,128)(2,1)S(1)}, bf16[4,144,1152]{2,1,0:T(8,128)(2,1)S(1)}, u32[]{:S(2)}, u32[]{:S(2)}) %collective-permute-start.55) | collective-permute-done | bytes 1327136 | tf_op jit(solution)/shard_map/ppermute | solution.py:60
  462.5 5.1 collective-permute-start.31
  469.2 7.9 %collective-permute-done.30 = f32[4,504]{1,0:T(4,128)S(1)} collective-permute-done((f32[4,504]{1,0:T(4,128)}, f32[4,504]{1,0:T(4,128)S(1)}, u32[]{:S(2)}, u32[]{:S(2)}) %collective-permute-start.30) | collective-permute-done | bytes 8096 | tf_op jit(solution)/shard_map/ppermute | solution.py:60
  525.5 5.5 collective-permute-done.58
  531.0 14.4 %collective-permute-done.57 = bf16[144,1152]{1,0:T(8,128)(2,1)} collective-permute-done((bf16[144,1152]{1,0:T(8,128)(2,1)S(1)}, bf16[144,1152]{1,0:T(8,128)(2,1)}, u32[]{:S(2)}, u32[]{:S(2)}) %collective-permute-start.57) | collective-permute-done | bytes 331808 | tf_op jit(solution)/shard_map/ppermute | solution.py:60
  575.1 5.7 fusion.1
  580.8 6.2 reshape.574
  587.0 5.9 constant_dynamic-slice_fusion.27
  600.5 32.0 %collective-permute-done.51 = bf16[4,288,144]{1,2,0:T(8,128)(2,1)S(1)} collective-permute-done((bf16[4,288,144]{1,2,0:T(8,128)(2,1)S(1)}, bf16[4,288,144]{1,2,0:T(8,128)(2,1)S(1)}, u32[]{:S(2)}, u32[]{:S(2)}) %collective-permute-start.51) | collective-permute-done | bytes 331808 | tf_op jit(solution)/shard_map/ppermute | solution.py:60
  658.9 11.8 %collective-permute-done.44 = bf16[288,432]{1,0:T(8,128)(2,1)} collective-permute-done((bf16[288,432]{1,0:T(8,128)(2,1)}, bf16[288,432]{1,0:T(8,128)(2,1)}, u32[]{:S(2)}, u32[]{:S(2)}) %collective-permute-start.44) | collective-permute-done | bytes 248864 | tf_op jit(solution)/shard_map/ppermute | solution.py:60
  (576 shorter events, 278.1 us)
Async XLA Ops:
  4.8 46.9 %collective-permute-start = (bf16[144,576]{1,0:T(8,128)(2,1)S(1)}, bf16[144,576]{1,0:T(8,128)(2,1)S(1)}, u32[]{:S(2)}, u32[]{:S(2)}) collective-permute-start(bf16[144,576]{1,0:T(8,128)(2,1)S(1)} %get-tuple-element.160), channel_id=1, source_target_pairs={{0,8},{8,0},{16,24},{24,16},{1,9},{9,1},{17,25},{25,17},{2,10},{10... | collective-permute-start | bytes 497672 | tf_op jit(solution)/shard_map/ppermute | solution.py:60
  5.3 46.7 %collective-permute-start.1 = (bf16[144,576]{1,0:T(8,128)(2,1)S(1)}, bf16[144,576]{1,0:T(8,128)(2,1)S(1)}, u32[]{:S(2)}, u32[]{:S(2)}) collective-permute-start(bf16[144,576]{1,0:T(8,128)(2,1)S(1)} %get-tuple-element.161), channel_id=1, source_target_pairs={{0,16},{8,24},{16,0},{24,8},{1,17},{9,25},{17,1},{25,9},{2,18},{10... | collective-permute-start | bytes 497672 | tf_op jit(solution)/shard_map/ppermute | solution.py:60
  7.9 44.4 %collective-permute-start.2 = (bf16[144,576]{1,0:T(8,128)(2,1)S(1)}, bf16[144,576]{1,0:T(8,128)(2,1)S(1)}, u32[]{:S(2)}, u32[]{:S(2)}) collective-permute-start(bf16[144,576]{1,0:T(8,128)(2,1)S(1)} %get-tuple-element.158), channel_id=1, source_target_pairs={{0,24},{8,16},{16,8},{24,0},{1,25},{9,17},{17,9},{25,1},{2,26},{10... | collective-permute-start | bytes 497672 | tf_op jit(solution)/shard_map/ppermute | solution.py:60
  265.6 74.6 %collective-permute-start.3 = (bf16[2,192,1152]{2,1,0:T(8,128)(2,1)}, bf16[2,192,1152]{2,1,0:T(8,128)(2,1)}, u32[]{:S(2)}, u32[]{:S(2)}) collective-permute-start(bf16[2,192,1152]{2,1,0:T(8,128)(2,1)} %pad_maximum_fusion.6), channel_id=1, source_target_pairs={{0,8},{8,0},{16,24},{24,16},{1,9},{9,1},{17,25},{25,17},{2,10},{10... | collective-permute-start | bytes 2654216 | tf_op jit(solution)/shard_map/ppermute | solution.py:60
  268.2 74.6 %collective-permute-start.5 = (bf16[2,192,1152]{2,1,0:T(8,128)(2,1)}, bf16[2,192,1152]{2,1,0:T(8,128)(2,1)}, u32[]{:S(2)}, u32[]{:S(2)}) collective-permute-start(bf16[2,192,1152]{2,1,0:T(8,128)(2,1)} %pad_maximum_fusion.7), channel_id=1, source_target_pairs={{0,8},{8,0},{16,24},{24,16},{1,9},{9,1},{17,25},{25,17},{2,10},{10... | collective-permute-start | bytes 2654216 | tf_op jit(solution)/shard_map/ppermute | solution.py:60
  335.6 32.2 %collective-permute-start.62 = (bf16[4,144,1152]{2,1,0:T(8,128)(2,1)}, bf16[4,144,1152]{2,1,0:T(8,128)(2,1)S(1)}, u32[]{:S(2)}, u32[]{:S(2)}) collective-permute-start(bf16[4,144,1152]{2,1,0:T(8,128)(2,1)} %pad_maximum_fusion.4), channel_id=1, source_target_pairs={{0,1},{1,0},{2,3},{3,2},{4,5},{5,4},{6,7},{7,6},{8,9},{9,8},{10,11... | collective-permute-start | bytes 3981320 | tf_op jit(solution)/shard_map/ppermute | solution.py:60
  337.3 58.8 %collective-permute-start.55 = (bf16[4,144,1152]{2,1,0:T(8,128)(2,1)S(1)}, bf16[4,144,1152]{2,1,0:T(8,128)(2,1)S(1)}, u32[]{:S(2)}, u32[]{:S(2)}) collective-permute-start(bf16[4,144,1152]{2,1,0:T(8,128)(2,1)S(1)} %pad_maximum_fusion.3), channel_id=1, source_target_pairs={{0,1},{1,0},{2,3},{3,2},{4,5},{5,4},{6,7},{7,6},{8,9},{9,8},{10,11... | collective-permute-start | bytes 3981320 | tf_op jit(solution)/shard_map/ppermute | solution.py:60
  341.6 57.3 %collective-permute-start.4 = (bf16[1,192,1152]{2,1,0:T(8,128)(2,1)S(1)}, bf16[1,192,1152]{2,1,0:T(8,128)(2,1)S(1)}, u32[]{:S(2)}, u32[]{:S(2)}) collective-permute-start(bf16[1,192,1152]{2,1,0:T(8,128)(2,1)S(1)} %fusion.25), channel_id=1, source_target_pairs={{0,16},{8,24},{16,0},{24,8},{1,17},{9,25},{17,1},{25,9},{2,18},{10... | collective-permute-start | bytes 1327112 | tf_op jit(solution)/shard_map/ppermute | solution.py:60
  344.0 54.9 %collective-permute-start.6 = (bf16[1,192,1152]{2,1,0:T(8,128)(2,1)S(1)}, bf16[1,192,1152]{2,1,0:T(8,128)(2,1)S(1)}, u32[]{:S(2)}, u32[]{:S(2)}) collective-permute-start(bf16[1,192,1152]{2,1,0:T(8,128)(2,1)S(1)} %fusion.22), channel_id=1, source_target_pairs={{0,16},{8,24},{16,0},{24,8},{1,17},{9,25},{17,1},{25,9},{2,18},{10... | collective-permute-start | bytes 1327112 | tf_op jit(solution)/shard_map/ppermute | solution.py:60
  421.5 27.7 %collective-permute-start.10 = (bf16[864]{0:T(1024)(128)(2,1)}, bf16[864]{0:T(1024)(128)(2,1)}, u32[]{:S(2)}, u32[]{:S(2)}) collective-permute-start(bf16[864]{0:T(1024)(128)(2,1)} %get-tuple-element.95), channel_id=1, source_target_pairs={{0,4},{1,5},{2,6},{3,7},{4,0},{5,1},{6,2},{7,3},{8,12},{9,13},{10,... | collective-permute-start | bytes 5192 | tf_op jit(solution)/shard_map/ppermute | solution.py:60
  421.6 29.0 %collective-permute-start.11 = (bf16[864]{0:T(1024)(128)(2,1)}, bf16[864]{0:T(1024)(128)(2,1)}, u32[]{:S(2)}, u32[]{:S(2)}) collective-permute-start(bf16[864]{0:T(1024)(128)(2,1)} %get-tuple-element.94), channel_id=1, source_target_pairs={{0,5},{1,4},{2,7},{3,6},{4,1},{5,0},{6,3},{7,2},{8,13},{9,12},{10,... | collective-permute-start | bytes 5192 | tf_op jit(solution)/shard_map/ppermute | solution.py:60
  435.3 22.2 %collective-permute-start.27 = (f32[4,504]{1,0:T(4,128)}, f32[4,504]{1,0:T(4,128)}, u32[]{:S(2)}, u32[]{:S(2)}) collective-permute-start(f32[4,504]{1,0:T(4,128)} %bitcast.440), channel_id=1, source_target_pairs={{0,1},{1,0},{2,3},{3,2},{4,5},{5,4},{6,7},{7,6},{8,9},{9,8},{10,11... | collective-permute-start | bytes 24200 | tf_op jit(solution)/shard_map/ppermute | solution.py:60
  449.2 67.5 %collective-permute-start.65 = (bf16[144,1152]{1,0:T(8,128)(2,1)}, bf16[144,1152]{1,0:T(8,128)(2,1)S(1)}, u32[]{:S(2)}, u32[]{:S(2)}) collective-permute-start(bf16[144,1152]{1,0:T(8,128)(2,1)} %get-tuple-element.113), channel_id=1, source_target_pairs={{0,6},{1,7},{2,4},{3,5},{4,2},{5,3},{6,0},{7,1},{8,14},{9,15},{10,... | collective-permute-start | bytes 995336 | tf_op jit(solution)/shard_map/ppermute | solution.py:60
  450.7 67.1 %collective-permute-start.64 = (bf16[144,1152]{1,0:T(8,128)(2,1)}, bf16[144,1152]{1,0:T(8,128)(2,1)S(1)}, u32[]{:S(2)}, u32[]{:S(2)}) collective-permute-start(bf16[144,1152]{1,0:T(8,128)(2,1)} %get-tuple-element.114), channel_id=1, source_target_pairs={{0,4},{1,5},{2,6},{3,7},{4,0},{5,1},{6,2},{7,3},{8,12},{9,13},{10,... | collective-permute-start | bytes 995336 | tf_op jit(solution)/shard_map/ppermute | solution.py:60
  515.0 30.4 %collective-permute-start.57 = (bf16[144,1152]{1,0:T(8,128)(2,1)S(1)}, bf16[144,1152]{1,0:T(8,128)(2,1)}, u32[]{:S(2)}, u32[]{:S(2)}) collective-permute-start(bf16[144,1152]{1,0:T(8,128)(2,1)S(1)} %copy-done.41), channel_id=1, source_target_pairs={{0,4},{1,5},{2,6},{3,7},{4,0},{5,1},{6,2},{7,3},{8,12},{9,13},{10,... | collective-permute-start | bytes 995336 | tf_op jit(solution)/shard_map/ppermute | solution.py:60
  516.7 28.7 %collective-permute-start.56 = (bf16[144,1152]{1,0:T(8,128)(2,1)S(1)}, bf16[144,1152]{1,0:T(8,128)(2,1)S(1)}, u32[]{:S(2)}, u32[]{:S(2)}) collective-permute-start(bf16[144,1152]{1,0:T(8,128)(2,1)S(1)} %copy-done.40), channel_id=1, source_target_pairs={{0,2},{1,3},{2,0},{3,1},{4,6},{5,7},{6,4},{7,5},{8,10},{9,11},{10,... | collective-permute-start | bytes 995336 | tf_op jit(solution)/shard_map/ppermute | solution.py:60
  518.4 39.4 %collective-permute-start.40 = (bf16[1,192,3456]{2,1,0:T(8,128)(2,1)}, bf16[1,192,3456]{2,1,0:T(8,128)(2,1)S(1)}, u32[]{:S(2)}, u32[]{:S(2)}) collective-permute-start(bf16[1,192,3456]{2,1,0:T(8,128)(2,1)} %get-tuple-element.141), channel_id=1, source_target_pairs={{0,16},{8,24},{16,0},{24,8},{1,17},{9,25},{17,1},{25,9},{2,18},{10... | collective-permute-start | bytes 3981320 | tf_op jit(solution)/shard_map/ppermute | solution.py:60
  523.9 38.3 %collective-permute-start.49 = (bf16[1,192,1152]{2,1,0:T(8,128)(2,1)S(1)}, bf16[1,192,1152]{2,1,0:T(8,128)(2,1)}, u32[]{:S(2)}, u32[]{:S(2)}) collective-permute-start(bf16[1,192,1152]{2,1,0:T(8,128)(2,1)S(1)} %bitcast.453), channel_id=1, source_target_pairs={{0,16},{8,24},{16,0},{24,8},{1,17},{9,25},{17,1},{25,9},{2,18},{10... | collective-permute-start | bytes 1327112 | tf_op jit(solution)/shard_map/ppermute | solution.py:60
  564.8 33.0 %collective-permute-start.67 = (bf16[144,288]{1,0:T(8,128)(2,1)}, bf16[144,288]{1,0:T(8,128)(2,1)}, u32[]{:S(2)}, u32[]{:S(2)}) collective-permute-start(bf16[144,288]{1,0:T(8,128)(2,1)} %bitcast.429), channel_id=1, source_target_pairs={{0,16},{8,24},{16,0},{24,8},{1,17},{9,25},{17,1},{25,9},{2,18},{10... | collective-permute-start | bytes 248840 | tf_op jit(solution)/shard_map/ppermute | solution.py:60
  567.1 75.9 %collective-permute-start.68 = (bf16[144,288]{1,0:T(8,128)(2,1)}, bf16[144,288]{1,0:T(8,128)(2,1)}, u32[]{:S(2)}, u32[]{:S(2)}) collective-permute-start(bf16[144,288]{1,0:T(8,128)(2,1)} %bitcast.428), channel_id=1, source_target_pairs={{0,24},{8,16},{16,8},{24,0},{1,25},{9,17},{17,9},{25,1},{2,26},{10... | collective-permute-start | bytes 248840 | tf_op jit(solution)/shard_map/ppermute | solution.py:60
  594.4 44.1 %collective-permute-start.42 = (bf16[4,288,432]{2,1,0:T(8,128)(2,1)}, bf16[4,288,432]{2,1,0:T(8,128)(2,1)}, u32[]{:S(2)}, u32[]{:S(2)}) collective-permute-start(bf16[4,288,432]{2,1,0:T(8,128)(2,1)} %pad_maximum_fusion.5), channel_id=1, source_target_pairs={{0,1},{1,0},{2,3},{3,2},{4,5},{5,4},{6,7},{7,6},{8,9},{9,8},{10,11... | collective-permute-start | bytes 2985992 | tf_op jit(solution)/shard_map/ppermute | solution.py:60
  597.1 35.4 %collective-permute-start.51 = (bf16[4,288,144]{1,2,0:T(8,128)(2,1)S(1)}, bf16[4,288,144]{1,2,0:T(8,128)(2,1)S(1)}, u32[]{:S(2)}, u32[]{:S(2)}) collective-permute-start(bf16[4,288,144]{1,2,0:T(8,128)(2,1)S(1)} %pad_maximum_fusion.10), channel_id=1, source_target_pairs={{0,1},{1,0},{2,3},{3,2},{4,5},{5,4},{6,7},{7,6},{8,9},{9,8},{10,11... | collective-permute-start | bytes 995336 | tf_op jit(solution)/shard_map/ppermute | solution.py:60
  643.0 27.7 %collective-permute-start.44 = (bf16[288,432]{1,0:T(8,128)(2,1)}, bf16[288,432]{1,0:T(8,128)(2,1)}, u32[]{:S(2)}, u32[]{:S(2)}) collective-permute-start(bf16[288,432]{1,0:T(8,128)(2,1)} %get-tuple-element.148), channel_id=1, source_target_pairs={{0,4},{1,5},{2,6},{3,7},{4,0},{5,1},{6,2},{7,3},{8,12},{9,13},{10,... | collective-permute-start | bytes 746504 | tf_op jit(solution)/shard_map/ppermute | solution.py:60
  643.6 27.1 %collective-permute-start.43 = (bf16[288,432]{1,0:T(8,128)(2,1)}, bf16[288,432]{1,0:T(8,128)(2,1)}, u32[]{:S(2)}, u32[]{:S(2)}) collective-permute-start(bf16[288,432]{1,0:T(8,128)(2,1)} %get-tuple-element.146), channel_id=1, source_target_pairs={{0,2},{1,3},{2,0},{3,1},{4,6},{5,7},{6,4},{7,5},{8,10},{9,11},{10,... | collective-permute-start | bytes 746504 | tf_op jit(solution)/shard_map/ppermute | solution.py:60
  (128 other events, 1405.0 us)

commit v2 on v1

--- a/solution.py
+++ b/solution.py
@@ -792,6 +792,444 @@
     )(att, one_block, two_block, kept, mods, bias, out_bias, cot, count)
 
 
+def gelu_parts(raised):
+    square = raised * raised
+    inner = 0.7978845608028654 * raised * (1.0 + 0.044715 * square)
+    bend = jnp.tanh(inner)
+    slope = 0.7978845608028654 * (1.0 + 3.0 * 0.044715 * square)
+    half = 0.5 * (1.0 + bend)
+    return raised * half, half + 0.5 * raised * (1.0 - bend * bend) * slope
+
+
+def column_sums(value):
+    return jnp.sum(value, axis=0, keepdims=True)
+
+
+def backward_body(
+    sizes,
+    att_hbm,
+    proj_ref,
+    one_ref,
+    two_ref,
+    hidden_one_ref,
+    projected_ref,
+    mixed_ref,
+    attended_ref,
+    hidden_all,
+    branch_all,
+    kept_ref,
+    mod_ref,
+    one_bias_ref,
+    out_bias_ref,
+    cot_ref,
+    count_ref,
+    block_ref,
+    d_kept_ref,
+    d_mod_ref,
+    one_out,
+    two_out,
+    att_out,
+    qkv_sums,
+    wide_sums,
+    act_ref,
+    d_raised_ref,
+    part_ref,
+    core_got,
+    cross_put,
+    cross_got,
+    grad_one,
+    grad_two,
+    grad_att,
+    mlp_y,
+    mlp_z,
+    att_y,
+    att_z,
+    rows_put,
+    rows_got,
+    d_att_all,
+    d_mixed_ref,
+    d_proj_all,
+    weight_ring,
+    send_m,
+    recv_m,
+    send_d,
+    recv_d,
+    send_e,
+    recv_e,
+    send_p,
+    recv_p,
+    local,
+):
+    heads, size, cols = sizes
+    n_dp, n_fs = 4, 8
+    d_at, f_at = lax.axis_index("dp"), lax.axis_index("fsdp")
+    slots, features = kept_ref.shape
+    row_width = features // n_dp
+    unit = one_out.shape[0]
+    width = features // n_fs
+    wide_masks = [2, 4, 6]
+    low = jnp.bfloat16
+    full = jnp.float32
+    core, cross, near = (d_at ^ 1, f_at), (d_at ^ 2, f_at), (d_at, f_at ^ 1)
+    greet([core, cross, (d_at ^ 3, f_at), near] + [(d_at, f_at ^ b) for b in wide_masks])
+    sent = []
+
+    def push(source, target, send, recv, device):
+        copy = remote(source, target, send, recv, device)
+        copy.start()
+        sent.append(copy)
+        return copy
+
+    def arrive(place, recv):
+        pltpu.make_async_copy(place, place, recv).wait()
+
+    for kind, source in enumerate((hidden_one_ref, mixed_ref)):
+        for piece in range(n_dp):
+            rows_put[kind, piece] = source[:, piece * row_width : (piece + 1) * row_width]
+
+    def image_step(image, carry):
+        raised = contract(hidden_all[image], one_ref[...], (1,), (1,)) + one_bias_ref[...]
+        active, slope = gelu_parts(raised)
+        act_ref[image] = active.astype(low)
+        d_active = jnp.dot(branch_all[image], two_ref[...], preferred_element_type=full)
+        d_raised_ref[image] = (d_active * slope).astype(low)
+        return carry
+
+    lax.fori_loop(0, n_dp, image_step, 0)
+
+    def flat(ref, start, count):
+        return ref[:, :, pl.ds(start, count)].reshape(n_dp * slots, count)
+
+    def weight_grad(target, left, right):
+        step = features // 3
+        for part in range(3):
+            target[part * step : (part + 1) * step, :] = rows_rows(
+                flat(left, part * step, step), flat(right, 0, features)
+            ).astype(low)
+
+    def block_rows(index):
+        return pl.ds(pl.multiple_of(index * unit, 16), unit)
+
+    def send_blocks(kind, grad):
+        for place, wide in enumerate([0] + wide_masks):
+            push(
+                grad.at[block_rows(f_at ^ wide ^ 1), :],
+                mlp_y.at[kind, place],
+                send_m.at[kind, place],
+                recv_m.at[kind, place],
+                near,
+            )
+
+    def fold_blocks(kind, grad):
+        for place, wide in enumerate([0] + wide_masks):
+            arrive(mlp_y.at[kind, place], recv_m.at[kind, place])
+            rows = block_rows(f_at ^ wide)
+            grad[rows, :] = (
+                grad[rows, :].astype(full) + mlp_y[kind, place].astype(full)
+            ).astype(low)
+            if wide:
+                push(
+                    grad.at[rows, :],
+                    mlp_z.at[kind, place - 1],
+                    send_m.at[kind, 3 + place],
+                    recv_m.at[kind, 3 + place],
+                    (d_at, f_at ^ wide),
+                )
+
+    def finish_blocks(kind, grad, target):
+        total = grad[block_rows(f_at), :].astype(full)
+        for place in range(3):
+            arrive(mlp_z.at[kind, place], recv_m.at[kind, 4 + place])
+            total = total + mlp_z[kind, place].astype(full)
+        target[...] = total
+
+    weight_grad(grad_two, branch_all, act_ref)
+    send_blocks(1, grad_two)
+
+    for kind in range(2):
+        for mask in (2, 3, 1):
+            push(
+                rows_put.at[kind, d_at ^ mask],
+                rows_got.at[kind, mask],
+                send_p.at[kind, mask],
+                recv_p.at[kind, mask],
+                (d_at ^ mask, f_at),
+            )
+        keep = pltpu.make_async_copy(rows_put.at[kind, d_at], rows_got.at[kind, 0], local.at[0])
+        keep.start()
+        keep.wait()
+
+    def part_step(left, right, dims):
+        def step(image, carry):
+            part_ref[image] = contract(left[image], right[...], (1,), dims).astype(low)
+            return carry
+
+        lax.fori_loop(0, n_dp, step, 0)
+
+    def core_send(kind):
+        return [
+            push(
+                part_ref.at[image],
+                core_got.at[kind, place],
+                send_d.at[kind, place],
+                recv_d.at[kind, place],
+                core,
+            )
+            for place, image in enumerate((3, 1))
+        ]
+
+    def cross_send(kind):
+        arrive(core_got.at[kind, 0], recv_d.at[kind, 0])
+        cross_put[kind] = (
+            part_ref[2].astype(full) + core_got[kind, 0].astype(full)
+        ).astype(low)
+        push(
+            cross_put.at[kind], cross_got.at[kind], send_d.at[kind, 2], recv_d.at[kind, 2], cross
+        )
+        arrive(core_got.at[kind, 1], recv_d.at[kind, 1])
+
+    part_step(d_raised_ref, one_ref, (0,))
+    leaving = core_send(0)
+    cross_send(0)
+    own_part = part_ref[0].astype(full) + core_got[0, 1].astype(full)
+    weight_grad(grad_one, d_raised_ref, hidden_all)
+    send_blocks(0, grad_one)
+    fold_blocks(1, grad_two)
+    one_sum = jnp.zeros((1, features), full)
+    for image in range(n_dp):
+        one_sum = one_sum + column_sums(d_raised_ref[image].astype(full))
+    wide_sums[0:1, :] = one_sum
+    wide_sums[1:2, :] = column_sums(branch_all[0].astype(full))
+
+    mods = [mod_ref[row : row + 1, :] for row in range(6)]
+    kept = kept_ref[...]
+    attended = attended_ref[...]
+    middle = kept + mods[2] * attended
+    normed_two, rstd_two = normed(middle)
+    upstream = cot_ref[...].astype(full)
+    arrive(cross_got.at[0], recv_d.at[0, 2])
+    d_hidden_two = own_part + cross_got[0].astype(full)
+    d_mod_ref[3:4, :] = column_sums(d_hidden_two)
+    d_mod_ref[4:5, :] = column_sums(d_hidden_two * normed_two)
+    d_middle = upstream + norm_back(d_hidden_two * (1.0 + mods[4]), normed_two, rstd_two)
+    d_mod_ref[2:3, :] = column_sums(d_middle * attended)
+    d_attended = (mods[2] * d_middle).astype(low)
+    d_att_all[0] = d_attended
+    d_kept_ref[...] = d_middle
+    wide_sums[2:3, :] = column_sums(d_attended.astype(full))
+    d_mixed_ref[...] = contract(d_attended, proj_ref[...], (1,), (1,)).astype(low)
+    push(d_att_all.at[0], d_att_all.at[2], send_e.at[2], recv_e.at[2], cross)
+    push(d_att_all.at[0], d_att_all.at[1], send_e.at[1], recv_e.at[1], core)
+
+    for copy in leaving:
+        copy.wait_send()
+    part_step(act_ref, two_ref, (1,))
+    core_send(1)
+    cross_send(1)
+    fold_blocks(0, grad_one)
+
+    per_shard = cols // size
+    allowed = lax.broadcasted_iota(jnp.int32, (slots, slots), 1) < count_ref[0]
+    factor = 1.0 / math.sqrt(size)
+    for h in range(heads):
+        places = [head_place(kind * heads + h, per_shard) for kind in range(3)]
+        q, k, v = [projected_ref[f, :, j * size : (j + 1) * size] for f, j in places]
+        d_mix = d_mixed_ref[:, h * size : (h + 1) * size]
+        scores = contract(q, k, (1,), (1,)) * factor
+        scores = jnp.where(allowed, scores, negative)
+        exponent = jnp.exp(scores - jnp.max(scores, axis=-1, keepdims=True))
+        softmax = exponent / jnp.sum(exponent, axis=-1, keepdims=True)
+        d_softmax = contract(d_mix, v, (1,), (1,))
+        delta = jnp.sum(d_softmax * softmax, axis=-1, keepdims=True)
+        d_scores = (softmax * (d_softmax - delta)).astype(low)
+        results = [
+            jnp.dot(d_scores, k, preferred_element_type=full) * factor,
+            rows_rows(d_scores, q) * factor,
+            rows_rows(softmax.astype(low), d_mix),
+        ]
+        for (f, j), result in zip(places, results):
+            d_proj_all[0, f, :, j * size : (j + 1) * size] = result.astype(low)
+
+    for f in range(n_fs):
+        push(
+            d_proj_all.at[0, f], d_proj_all.at[2, f], send_p.at[2 + f, 2], recv_p.at[2 + f, 2], cross
+        )
+        push(
+            d_proj_all.at[0, f], d_proj_all.at[1, f], send_p.at[2 + f, 1], recv_p.at[2 + f, 1], core
+        )
+    arrive(d_att_all.at[2], recv_e.at[2])
+    push(d_att_all.at[2], d_att_all.at[3], send_e.at[3], recv_e.at[3], core)
+
+    loads = [
+        pltpu.make_async_copy(att_hbm.at[f], weight_ring.at[f % 2], local.at[1 + f % 2])
+        for f in range(n_fs)
+    ]
+    loads[0].start()
+    d_hidden_one = jnp.zeros((slots, features), full)
+    for f in range(n_fs):
+        if f + 1 < n_fs:
+            loads[f + 1].start()
+        loads[f].wait()
+        own = d_proj_all[0, f]
+        d_hidden_one = d_hidden_one + contract(
+            own, weight_ring[f % 2, :, :cols], (1,), (1,)
+        )
+        qkv_sums[f] = column_sums(own.astype(full))
+        arrive(d_proj_all.at[2, f], recv_p.at[2 + f, 2])
+        push(
+            d_proj_all.at[2, f], d_proj_all.at[3, f], send_p.at[2 + f, 3], recv_p.at[2 + f, 3], core
+        )
+    normed_one, rstd_one = normed(kept)
+    d_mod_ref[0:1, :] = column_sums(d_hidden_one)
+    d_mod_ref[1:2, :] = column_sums(d_hidden_one * normed_one)
+    d_kept_ref[...] = d_kept_ref[...] + norm_back(
+        d_hidden_one * (1.0 + mods[1]), normed_one, rstd_one
+    )
+
+    for kind in range(2):
+        for mask in (2, 3, 1):
+            arrive(rows_got.at[kind, mask], recv_p.at[kind, mask])
+    for mask in (1, 3):
+        arrive(d_att_all.at[mask], recv_e.at[mask])
+    grad_proj = rows_rows(
+        rows_got[1].reshape(n_dp * slots, row_width),
+        d_att_all[...].reshape(n_dp * slots, features),
+    ).astype(low)
+    for f in range(n_fs):
+        grad_att[f, :, cols : cols + width] = grad_proj[:, f * width : (f + 1) * width]
+    for f in range(n_fs):
+        for mask in (1, 3):
+            arrive(d_proj_all.at[mask, f], recv_p.at[2 + f, mask])
+
+    def qkv_grad(f):
+        grad_att[f, :, :cols] = rows_rows(
+            rows_got[0].reshape(n_dp * slots, row_width),
+            d_proj_all[:, f].reshape(n_dp * slots, cols),
+        ).astype(low)
+
+    for place, wide in enumerate([0] + wide_masks):
+        qkv_grad(f_at ^ wide ^ 1)
+        push(
+            grad_att.at[f_at ^ wide ^ 1],
+            att_y.at[place],
+            send_m.at[2, place],
+            recv_m.at[2, place],
+            near,
+        )
+    for wide in [0] + wide_masks:
+        qkv_grad(f_at ^ wide)
+    for place, wide in enumerate([0] + wide_masks):
+        arrive(att_y.at[place], recv_m.at[2, place])
+        index = f_at ^ wide
+        grad_att[index] = (grad_att[index].astype(full) + att_y[place].astype(full)).astype(low)
+        if wide:
+            push(
+                grad_att.at[index],
+                att_z.at[place - 1],
+                send_m.at[2, 3 + place],
+                recv_m.at[2, 3 + place],
+                (d_at, index),
+            )
+
+    arrive(cross_got.at[1], recv_d.at[1, 2])
+    branch = (
+        part_ref[0].astype(full)
+        + core_got[1, 1].astype(full)
+        + cross_got[1].astype(full)
+        + out_bias_ref[...]
+    )
+    d_mod_ref[5:6, :] = column_sums(upstream * branch)
+    block_ref[...] = (middle + mods[5] * branch).astype(low)
+    finish_blocks(1, grad_two, two_out)
+    finish_blocks(0, grad_one, one_out)
+    total = grad_att[f_at].astype(full)
+    for place in range(3):
+        arrive(att_z.at[place], recv_m.at[2, 4 + place])
+        total = total + att_z[place].astype(full)
+    att_out[...] = total
+    for copy in sent:
+        if not any(copy is gone for gone in leaving):
+            copy.wait_send()
+
+
+def backward_kernel(
+    att_all, proj, one_full, two_full, forward, kept, mods, one_bias, out_bias, cot, count, cols
+):
+    hidden_one, projected, mixed, attended, hidden_all, branch_all = forward
+    n_dp, n_fs = lax.axis_size("dp"), lax.axis_size("fsdp")
+    slots, features = kept.shape
+    row_width = features // n_dp
+    unit = features // n_fs
+    att_cols = att_all.shape[2]
+    low, full = jnp.bfloat16, jnp.float32
+    vmem = pl.BlockSpec(memory_space=pltpu.VMEM)
+    shapes = [
+        ((slots, features), low),
+        ((slots, features), full),
+        ((8, features), full),
+        ((unit, features), full),
+        ((unit, features), full),
+        ((row_width, att_cols), full),
+        ((n_fs, 1, cols), full),
+        ((8, features), full),
+    ]
+    image = (slots, features)
+    scratch = [
+        (n_dp,) + image,
+        (n_dp,) + image,
+        (n_dp,) + image,
+        (2, 2) + image,
+        (2,) + image,
+        (2,) + image,
+        (features, features),
+        (features, features),
+        (n_fs, row_width, att_cols),
+        (2, 4, unit, features),
+        (2, 3, unit, features),
+        (4, row_width, att_cols),
+        (3, row_width, att_cols),
+        (2, n_dp, slots, row_width),
+        (2, n_dp, slots, row_width),
+        (n_dp,) + image,
+        image,
+        (n_dp, n_fs, slots, cols),
+        (2, features, att_cols),
+    ]
+    dma = pltpu.SemaphoreType.DMA
+    return pl.pallas_call(
+        functools.partial(backward_body, (HEADS, features // HEADS, cols)),
+        out_shape=[jax.ShapeDtypeStruct(shape, kind) for shape, kind in shapes],
+        in_specs=[pl.BlockSpec(memory_space=pl.ANY)]
+        + [vmem] * 14
+        + [pl.BlockSpec(memory_space=pltpu.SMEM)],
+        out_specs=[vmem] * len(shapes),
+        scratch_shapes=[pltpu.VMEM(shape, low) for shape in scratch]
+        + [dma((3, 7)), dma((3, 7)), dma((2, 3)), dma((2, 3)), dma((4,)), dma((4,))]
+        + [dma((2 + n_fs, 4)), dma((2 + n_fs, 4)), dma((3,))],
+        compiler_params=pltpu.CompilerParams(
+            collective_id=6, has_side_effects=True, vmem_limit_bytes=64 * 1024 * 1024 - 65536
+        ),
+        name="backward",
+    )(
+        att_all,
+        proj,
+        one_full,
+        two_full,
+        hidden_one,
+        projected,
+        mixed,
+        attended,
+        hidden_all,
+        branch_all,
+        kept,
+        mods,
+        one_bias,
+        out_bias,
+        cot,
+        count,
+    )
+
+
 def shards(
     patches_in,
     condition,
@@ -891,48 +1329,38 @@
         keep_count,
         qkv_cols,
     )
-    hidden_two_all = hidden_two_all.reshape(n_dp * kept_slots, features)
-    d_branch_all = d_branch_all.reshape(n_dp * kept_slots, features)
-    d_branch = d_branch_all[:kept_slots]
-    qkv_full = att_all[:, :, :qkv_cols].transpose(1, 0, 2).reshape(features, -1)
-    projected = projected_all.transpose(1, 0, 2).reshape(kept_slots, -1)
-    allowed = (jnp.arange(kept_slots) < keep_count[0])[None, None, :]
-    normed_one, rstd_one = layer_norm(kept_in)
-    middle = kept_in + gate_one * attended
-    normed_two, rstd_two = layer_norm(middle)
-    upstream = cotangent[0].astype(full)
-    queries = projected[:, :features].reshape(head_shape)
-    key_rows = projected[:, features : 2 * features].reshape(head_shape)
-    values = projected[:, 2 * features :].reshape(head_shape)
-    scores = jnp.einsum("qhe,khe->hqk", queries, key_rows, preferred_element_type=full) * factor
-    scores = jnp.where(allowed, scores, negative)
-    top_score = jnp.max(scores, axis=-1, keepdims=True)
-    exponent = jnp.exp(scores - top_score)
-    softmax = exponent / jnp.sum(exponent, axis=-1, keepdims=True)
-    softmax_low = softmax.astype(low)
-
-    raised = times_transposed(hidden_two_all, one_full) + own_one_bias
-    activated = gelu_tanh(raised).astype(low)
-    grad_two = rows_rows(d_branch_all, activated).astype(low)
-    branch_part = times_transposed(activated, two_full)
-    branch = (
-        reduce_dp(branch_part.reshape(n_dp, kept_slots, features)) + out_full[features:]
-    )
-    block_out = (middle + gate_two * branch).astype(low)
-    d_gate_two = jnp.sum(upstream * branch, axis=0)
-    d_activated = jnp.dot(d_branch_all, two_full, preferred_element_type=full)
-    unused, gelu_pull = jax.vjp(gelu_tanh, raised)
-    d_raised = gelu_pull(d_activated)[0].astype(low)
-    d_hidden_part = jnp.dot(d_raised, one_full, preferred_element_type=full)
-    d_hidden_two = reduce_dp(d_hidden_part.reshape(n_dp, kept_slots, features))
-    grad_one = rows_rows(d_raised, hidden_two_all).astype(low)
-    one_sums = jnp.sum(d_raised.astype(full), axis=0)
-    final_two = reduce_blocks(grad_two.reshape(n_fs, -1, hidden_units // n_dp)).astype(low)
-    final_one = reduce_blocks(grad_one.reshape(n_fs, unit_width, features)).astype(low)
-    one_out = trade(final_one.reshape(unit_width, n_dp, row_width).transpose(1, 0, 2), "dp")
+    (
+        block_out,
+        d_kept,
+        d_mods,
+        final_one,
+        final_two,
+        att_out,
+        qkv_sums,
+        wide_sums,
+    ) = backward_kernel(
+        att_all,
+        proj_full,
+        one_full,
+        two_full,
+        (hidden_one, projected_all, mixed_low, attended, hidden_two_all, d_branch_all),
+        kept_in,
+        mods,
+        own_one_bias[None],
+        out_full[None, features:],
+        cotangent[0],
+        keep_count,
+        qkv_cols,
+    )
+    qkv_out = att_out[:, :qkv_cols]
+    proj_out = att_out[:, qkv_cols:]
+    grad_patches = jnp.zeros(inputs.shape, full).at[indices].set(d_kept, unique_indices=True)[None]
+    one_out = trade(
+        final_one.astype(low).reshape(unit_width, n_dp, row_width).transpose(1, 0, 2), "dp"
+    )
     one_out = one_out.reshape(-1, row_width).T.astype(full)
     two_out = trade(
-        final_two.reshape(final_two.shape[0], n_dp, -1).transpose(1, 0, 2), "dp"
+        final_two.astype(low).reshape(final_two.shape[0], n_dp, -1).transpose(1, 0, 2), "dp"
     )
     two_out = (
         two_out.reshape(n_dp, final_two.shape[0], n_fs // n_dp, unit_width)
@@ -941,52 +1369,7 @@
         .astype(full)
     )
 
-    d_shift_two = jnp.sum(d_hidden_two, axis=0)
-    d_scale_two = jnp.sum(d_hidden_two * normed_two, axis=0)
-    d_middle = upstream + norm_back(d_hidden_two * (1.0 + scale_two), normed_two, rstd_two)
-    d_gate_one = jnp.sum(d_middle * attended, axis=0)
-    d_attended = (gate_one * d_middle).astype(low)
-    d_mixed = times_transposed(d_attended, proj_full).astype(low).reshape(head_shape)
-    d_softmax = jnp.einsum("qhe,khe->hqk", d_mixed, values, preferred_element_type=full)
-    row_delta = jnp.sum(d_softmax * softmax, axis=-1, keepdims=True)
-    d_scores = (softmax * (d_softmax - row_delta)).astype(low)
-    d_queries = jnp.einsum("hqk,khe->qhe", d_scores, key_rows, preferred_element_type=full)
-    d_keys = jnp.einsum("hqk,qhe->khe", d_scores, queries, preferred_element_type=full)
-    d_values = jnp.einsum("hqk,qhe->khe", softmax_low, d_mixed, preferred_element_type=full)
-    d_projected = jnp.concatenate(
-        [
-            (d_queries * factor).reshape(kept_slots, features),
-            (d_keys * factor).reshape(kept_slots, features),
-            d_values.reshape(kept_slots, features),
-        ],
-        axis=1,
-    ).astype(low)
-    d_hidden_one = times_transposed(d_projected, qkv_full)
-    d_shift_one = jnp.sum(d_hidden_one, axis=0)
-    d_scale_one = jnp.sum(d_hidden_one * normed_one, axis=0)
-    d_kept = d_middle + norm_back(d_hidden_one * (1.0 + scale_one), normed_one, rstd_one)
-    grad_patches = jnp.zeros(inputs.shape, full).at[indices].set(d_kept, unique_indices=True)[None]
-
-    def own_rows(rows):
-        return trade(rows.reshape(kept_slots, n_dp, row_width).transpose(1, 0, 2), "dp").reshape(
-            n_dp * kept_slots, row_width
-        )
-
-    def by_index(rows):
-        here = lax.axis_index("dp")
-        slots = spread_dp(rows)
-        return ordered([slots[mask] for mask in range(n_dp)], "dp").reshape(
-            n_dp * kept_slots, -1
-        )
-
-    grad_proj = rows_rows(own_rows(mixed_low), by_index(d_attended)).astype(low)
-    grad_qkv = rows_rows(own_rows(hidden_one), by_index(d_projected)).astype(low)
-    proj_out = reduce_blocks(grad_proj.reshape(row_width, n_fs, -1).transpose(1, 0, 2))
-    qkv_out = reduce_blocks(grad_qkv.reshape(row_width, n_fs, -1).transpose(1, 0, 2))
-
-    d_modulation = jnp.concatenate(
-        [d_shift_one, d_scale_one, d_gate_one, d_shift_two, d_scale_two, d_gate_two]
-    ).astype(low)
+    d_modulation = d_mods[:6].reshape(-1).astype(low)
     group_d = trade(d_modulation.reshape(n_fs, -1), "fsdp")
     all_d = spread_small(group_d, "dp").reshape(n_all, -1)
     grad_ada = rows_rows(signals, all_d)
@@ -996,21 +1379,16 @@
     unused_too, swish_pull = jax.vjp(swish, cond_float)
     grad_condition = swish_pull(d_signal)[0]
 
-    sums = jnp.sum(d_projected.astype(full), axis=0)
+    sums = qkv_sums.reshape(-1)
     one_spread = jnp.zeros((n_fs, n_dp, unit_width), full)
     one_spread = lax.dynamic_update_index_in_dim(
-        one_spread, one_sums.reshape(n_fs, unit_width), d_at, 1
+        one_spread, wide_sums[0].reshape(n_fs, unit_width), d_at, 1
     )
     bias_parts = [
         d_modulation.astype(full),
         jnp.concatenate([sums[:features], sums[2 * features :]]),
         one_spread.reshape(-1),
-        jnp.concatenate(
-            [
-                jnp.sum(d_attended.astype(full), axis=0),
-                jnp.sum(d_branch.astype(full), axis=0),
-            ]
-        ),
+        jnp.concatenate([wide_sums[2], wide_sums[1]]),
     ]
     bias_all = jnp.concatenate([part.reshape(n_all, -1) for part in bias_parts], axis=1)
     bias_all = bias_all.reshape(n_dp, n_fs, -1)
@@ -1045,7 +1423,8 @@
         and w_qkv.shape[0] % 16 == 0
         and unit_width % 16 == 0
         and unit_width == arrays[11].shape[1]
-        and lax.axis_size("fsdp") % 4 == 0
+        and lax.axis_size("dp") == 4
+        and lax.axis_size("fsdp") == 8
     )
 
 

time: 682 us -> 505 us (0.74)
  Pallas kernels: 186 us -> 363 us
  waiting for transfers between devices: 140 us -> 14.2 us
  local copies, waits for them, and re-layouts: 170 us -> 57.3 us
  matrix products: 50 us -> 2.65 us
  other arithmetic: 47.4 us -> 5.1 us
  starting transfers between devices: 75.9 us -> 52.4 us
    pallas_call x0 -> x1, Pallas kernels: none -> 177 us  [backward_kernel(): pl.pallas_call(functools.partial(backward_body, (HEADS, features // HEADS...]
    ppermute x69 -> x39, waiting for transfers between devices: 140 us -> 14.2 us  [swap(): lax.ppermute(value, axis, [(index, index ^ mask) for index in range(size)])]
    dot_general x10 -> x2, matrix products: 31.7 us -> 2.37 us  [contract(): lax.dot_general(left, right, ((left_dims, right_dims), ((), ())), preferr...]
    dynamic_update_slice x62 -> x48, local copies, waits for them, and re-layouts: 49.2 us -> 24.1 us  [put(): return lax.dynamic_update_index_in_dim(pieces, value, index, 0)]
    ppermute x69 -> x39, starting transfers between devices: 75.9 us -> 52.4 us  [swap(): lax.ppermute(value, axis, [(index, index ^ mask) for index in range(size)])]
    transpose x3 -> x0, local copies, waits for them, and re-layouts: 21.8 us -> none  [the longest x2 19.6 us: shards(): qkv_full = att_all[:, :, :qkv_cols].transpose(1, 0, 2).reshape(features, -1)]
    another operation x19 -> x7, local copies, waits for them, and re-layouts: 21.9 us -> 2.73 us
    dot_general x6 -> x0, matrix products: 14.5 us -> none  [the longest x1 5.4 us: shards(): d_activated = jnp.dot(d_branch_all, two_full, preferred_element_type=full)]
  transfers between devices with their start and end apart: 69 -> 39, of which waited for: 20 -> 12; matrix products, arithmetic and copies ran while one was open for 28% -> 7% of each run, Pallas kernels for 4% -> 5%
where the time goes in v2:
time: 505 us; the launch traced here: 497 us
  Pallas kernels  363 us (72%)
  local copies, waits for them, and re-layouts  57.3 us (11%)
  starting transfers between devices  52.4 us (10%)
  waiting for transfers between devices  14.2 us (3%)
  other arithmetic  5.1 us (1%)
    pallas_call x1, Pallas kernels, backward_kernel(): pl.pallas_call(functools.partial(backward_body, (HEADS, features // HEADS...  177 us
    pallas_call x1, Pallas kernels, forward_kernel(): pl.pallas_call(functools.partial(forward_body, (n_dp, n_fs, HEADS, size,...  163 us
    ppermute x39, starting transfers between devices, swap(): lax.ppermute(value, axis, [(index, index ^ mask) for index in range(size)])  52.4 us
    dynamic_update_slice x48, local copies, waits for them, and re-layouts, put(): return lax.dynamic_update_index_in_dim(pieces, value, index, 0)  24.1 us
    pallas_call x2, Pallas kernels, exchange_everyone(): pl.pallas_call(functools.partial(everyone_body, n_dp, n_fs), out_shape=ja...  23.6 us
    ppermute x39, waiting for transfers between devices, swap(): lax.ppermute(value, axis, [(index, index ^ mask) for index in range(size)])  14.2 us
  transfers between devices with their start and end apart: 39, of which 12 were waited for; matrix products, arithmetic and copies ran while one was open for 7% of the time, Pallas kernels for 5%

profile of v2, /device:TPU:0, one launch (start us, length us, event | category | flops | bytes accessed | tf_op | source)
XLA Modules:
  0.0 497.4 jit_solution(3552758747095297010)
XLA Ops:
  4.5 2.6 collective-permute-start.1
  8.0 11.9 %exchange_everyone.2 = bf16[32,16,128]{2,1,0:T(8,128)(2,1)} custom-call(bf16[32,16,128]{2,1,0:T(8,128)(2,1)} %broadcast_in_dim.224.source), custom_call_target="tpu_custom_call" | custom-call | tf_op jit(solution)/shard_map/exchange_everyone/pallas_call | solution.py:522
  22.1 11.7 %exchange_everyone.3 = f32[32,8,128]{2,1,0:T(8,128)} custom-call(f32[32,8,128]{2,1,0:T(8,128)} %bitcast.201), custom_call_target="tpu_custom_call" | custom-call | tf_op jit(solution)/shard_map/exchange_everyone/pallas_call | solution.py:522
  41.5 5.7 %dynamic_update_slice.156 = bf16[4,144,576]{2,0,1:T(4,128)(2,1)S(1)} dynamic-update-slice(bf16[4,144,576]{2,0,1:T(4,128)(2,1)S(1)} %broadcast_in_dim.213, bf16[1,144,576]{2,0,1:T(2,128)(2,1)S(1)} %copy.74, s32[]{:T(128)S(6)} %select_n.159, s32[]{:T(128)} %constant.269.clone.1, s32[]{:T(128)} %constant.269.clone.1) | dynamic-update-slice | bytes 331780 | tf_op jit(solution)/shard_map/jit(dynamic_update_index_in_dim)/dynamic_update_slice | solution.py:68
  49.6 5.7 %dynamic_update_slice.157 = bf16[4,144,576]{2,0,1:T(4,128)(2,1)S(1)} dynamic-update-slice(bf16[4,144,576]{2,0,1:T(4,128)(2,1)S(1)} %dynamic_update_slice.156, bf16[1,144,576]{2,0,1:T(2,128)(2,1)S(1)} %copy.75, s32[]{:T(128)S(6)} %select_n.160, s32[]{:T(128)} %constant.269.clone.1, s32[]{:T(128)} %constant.269.clone.1) | dynamic-update-slice | bytes 331780 | tf_op jit(solution)/shard_map/jit(dynamic_update_index_in_dim)/dynamic_update_slice | solution.py:68
  55.3 5.7 %dynamic_update_slice.158 = bf16[4,144,576]{2,0,1:T(4,128)(2,1)S(1)} dynamic-update-slice(bf16[4,144,576]{2,0,1:T(4,128)(2,1)S(1)} %dynamic_update_slice.157, bf16[1,144,576]{2,0,1:T(2,128)(2,1)S(1)} %copy.76, s32[]{:T(128)S(6)} %select_n.161, s32[]{:T(128)} %constant.269.clone.1, s32[]{:T(128)} %constant.269.clone.1) | dynamic-update-slice | bytes 331780 | tf_op jit(solution)/shard_map/jit(dynamic_update_index_in_dim)/dynamic_update_slice | solution.py:68
  61.0 5.7 %dynamic_update_slice.159 = bf16[4,144,576]{2,0,1:T(4,128)(2,1)S(1)} dynamic-update-slice(bf16[4,144,576]{2,0,1:T(4,128)(2,1)S(1)} %dynamic_update_slice.158, bf16[1,144,576]{2,0,1:T(2,128)(2,1)S(1)} %copy.77, s32[]{:T(128)S(6)} %select_n.162, s32[]{:T(128)} %constant.269.clone.1, s32[]{:T(128)} %constant.269.clone.1) | dynamic-update-slice | bytes 331780 | tf_op jit(solution)/shard_map/jit(dynamic_update_index_in_dim)/dynamic_update_slice | solution.py:68
  69.3 162.5 %forward.1 = (bf16[8,1152,576]{2,1,0:T(8,128)(2,1)}, bf16[1152,1152]{1,0:T(8,128)(2,1)}, bf16[1152,1152]{1,0:T(8,128)(2,1)}, bf16[192,1152]{1,0:T(8,128)(2,1)}, ...) custom-call(bf16[288,576]{1,0:T(8,128)(2,1)} %pad_maximum_fusion.att, ...), custom_call_target="tpu_custom_call" | custom-call | tf_op jit(solution)/shard_map/forward/pallas_call | solution.py:774
  231.8 176.8 %backward.1 = (bf16[192,1152]{1,0:T(8,128)(2,1)}, f32[192,1152]{1,0:T(8,128)}, f32[8,1152]{1,0:T(8,128)}, f32[144,1152]{1,0:T(8,128)}, f32[144,1152]{1,0:T(8,128...) custom-call(bf16[8,1152,576]{2,1,0:T(8,128)(2,1)} %get-tuple-element.30.att_hbm, ...), custom_call_target="tpu_custom_call" | custom-call | tf_op jit(solution)/shard_map/backward/pallas_call | solution.py:1199
  415.6 7.3 %collective-permute-start.4 = (bf16[864]{0:T(1024)(128)(2,1)S(1)}, bf16[864]{0:T(1024)(128)(2,1)S(1)}, u32[]{:S(2)}, u32[]{:S(2)}) collective-permute-start(bf16[864]{0:T(1024)(128)(2,1)S(1)} %get-tuple-element.104), channel_id=1, source_target_pairs={{0,2},{1,3},{2,0},{3,1},{4,6},{5,7},{6,4},{7,5},{8,10},{9,11},{10,... | collective-permute-start | bytes 5192 | tf_op jit(solution)/shard_map/ppermute | solution.py:60
  427.7 2.1 collective-permute-start.6
  432.5 3.0 collective-permute-start.9
  435.5 2.9 scatter_custom_fusion
  441.0 2.7 collective-permute-start.25
  444.4 2.5 collective-permute-start.27
  448.4 3.1 collective-permute-start.29
  452.3 2.5 collective-permute-done.29
  464.3 2.5 collective-permute-start.15
  467.9 2.4 collective-permute-start.17
  470.3 2.3 collective-permute-start.18
  472.6 2.1 collective-permute-start.19
  475.8 3.2 collective-permute-done.19
  481.0 2.1 fusion.14
  488.1 3.2 collective-permute-done.34
  (278 shorter events, 62.5 us)
Async XLA Ops:
  4.0 44.7 %collective-permute-start = (bf16[144,576]{1,0:T(8,128)(2,1)S(1)}, bf16[144,576]{1,0:T(8,128)(2,1)S(1)}, u32[]{:S(2)}, u32[]{:S(2)}) collective-permute-start(bf16[144,576]{1,0:T(8,128)(2,1)S(1)} %get-tuple-element.111), channel_id=1, source_target_pairs={{0,8},{8,0},{16,24},{24,16},{1,9},{9,1},{17,25},{25,17},{2,10},{10... | collective-permute-start | bytes 497672 | tf_op jit(solution)/shard_map/ppermute | solution.py:60
  4.5 44.5 %collective-permute-start.1 = (bf16[144,576]{1,0:T(8,128)(2,1)S(1)}, bf16[144,576]{1,0:T(8,128)(2,1)S(1)}, u32[]{:S(2)}, u32[]{:S(2)}) collective-permute-start(bf16[144,576]{1,0:T(8,128)(2,1)S(1)} %get-tuple-element.112), channel_id=1, source_target_pairs={{0,16},{8,24},{16,0},{24,8},{1,17},{9,25},{17,1},{25,9},{2,18},{10... | collective-permute-start | bytes 497672 | tf_op jit(solution)/shard_map/ppermute | solution.py:60
  7.1 42.2 %collective-permute-start.2 = (bf16[144,576]{1,0:T(8,128)(2,1)S(1)}, bf16[144,576]{1,0:T(8,128)(2,1)S(1)}, u32[]{:S(2)}, u32[]{:S(2)}) collective-permute-start(bf16[144,576]{1,0:T(8,128)(2,1)S(1)} %get-tuple-element.109), channel_id=1, source_target_pairs={{0,24},{8,16},{16,8},{24,0},{1,25},{9,17},{17,9},{25,1},{2,26},{10... | collective-permute-start | bytes 497672 | tf_op jit(solution)/shard_map/ppermute | solution.py:60
  413.3 30.4 %collective-permute-start.23 = (f32[4,504]{1,0:T(4,128)S(1)}, f32[4,504]{1,0:T(4,128)S(1)}, u32[]{:S(2)}, u32[]{:S(2)}) collective-permute-start(f32[4,504]{1,0:T(4,128)S(1)} %bitcast.219), channel_id=1, source_target_pairs={{0,1},{1,0},{2,3},{3,2},{4,5},{5,4},{6,7},{7,6},{8,9},{9,8},{10,11... | collective-permute-start | bytes 24200 | tf_op jit(solution)/shard_map/ppermute | solution.py:60
  414.7 15.1 %collective-permute-start.3 = (bf16[864]{0:T(1024)(128)(2,1)S(1)}, bf16[864]{0:T(1024)(128)(2,1)S(1)}, u32[]{:S(2)}, u32[]{:S(2)}) collective-permute-start(bf16[864]{0:T(1024)(128)(2,1)S(1)} %get-tuple-element.105), channel_id=1, source_target_pairs={{0,1},{1,0},{2,3},{3,2},{4,5},{5,4},{6,7},{7,6},{8,9},{9,8},{10,11... | collective-permute-start | bytes 5192 | tf_op jit(solution)/shard_map/ppermute | solution.py:60
  415.6 15.3 %collective-permute-start.4 = (bf16[864]{0:T(1024)(128)(2,1)S(1)}, bf16[864]{0:T(1024)(128)(2,1)S(1)}, u32[]{:S(2)}, u32[]{:S(2)}) collective-permute-start(bf16[864]{0:T(1024)(128)(2,1)S(1)} %get-tuple-element.104), channel_id=1, source_target_pairs={{0,2},{1,3},{2,0},{3,1},{4,6},{5,7},{6,4},{7,5},{8,10},{9,11},{10,... | collective-permute-start | bytes 5192 | tf_op jit(solution)/shard_map/ppermute | solution.py:60
  422.9 9.6 %collective-permute-start.5 = (bf16[864]{0:T(1024)(128)(2,1)S(1)}, bf16[864]{0:T(1024)(128)(2,1)S(1)}, u32[]{:S(2)}, u32[]{:S(2)}) collective-permute-start(bf16[864]{0:T(1024)(128)(2,1)S(1)} %get-tuple-element.103), channel_id=1, source_target_pairs={{0,3},{1,2},{2,1},{3,0},{4,7},{5,6},{6,5},{7,4},{8,11},{9,10},{10,... | collective-permute-start | bytes 5192 | tf_op jit(solution)/shard_map/ppermute | solution.py:60
  427.7 11.8 %collective-permute-start.6 = (bf16[864]{0:T(1024)(128)(2,1)S(1)}, bf16[864]{0:T(1024)(128)(2,1)S(1)}, u32[]{:S(2)}, u32[]{:S(2)}) collective-permute-start(bf16[864]{0:T(1024)(128)(2,1)S(1)} %get-tuple-element.102), channel_id=1, source_target_pairs={{0,4},{1,5},{2,6},{3,7},{4,0},{5,1},{6,2},{7,3},{8,12},{9,13},{10,... | collective-permute-start | bytes 5192 | tf_op jit(solution)/shard_map/ppermute | solution.py:60
  429.8 9.9 %collective-permute-start.7 = (bf16[864]{0:T(1024)(128)(2,1)S(1)}, bf16[864]{0:T(1024)(128)(2,1)S(1)}, u32[]{:S(2)}, u32[]{:S(2)}) collective-permute-start(bf16[864]{0:T(1024)(128)(2,1)S(1)} %get-tuple-element.101), channel_id=1, source_target_pairs={{0,5},{1,4},{2,7},{3,6},{4,1},{5,0},{6,3},{7,2},{8,13},{9,12},{10,... | collective-permute-start | bytes 5192 | tf_op jit(solution)/shard_map/ppermute | solution.py:60
  430.9 9.8 %collective-permute-start.8 = (bf16[864]{0:T(1024)(128)(2,1)S(1)}, bf16[864]{0:T(1024)(128)(2,1)S(1)}, u32[]{:S(2)}, u32[]{:S(2)}) collective-permute-start(bf16[864]{0:T(1024)(128)(2,1)S(1)} %get-tuple-element.100), channel_id=1, source_target_pairs={{0,6},{1,7},{2,4},{3,5},{4,2},{5,3},{6,0},{7,1},{8,14},{9,15},{10,... | collective-permute-start | bytes 5192 | tf_op jit(solution)/shard_map/ppermute | solution.py:60
  432.5 8.6 %collective-permute-start.9 = (bf16[864]{0:T(1024)(128)(2,1)S(1)}, bf16[864]{0:T(1024)(128)(2,1)S(1)}, u32[]{:S(2)}, u32[]{:S(2)}) collective-permute-start(bf16[864]{0:T(1024)(128)(2,1)S(1)} %get-tuple-element.99), channel_id=1, source_target_pairs={{0,7},{1,6},{2,5},{3,4},{4,3},{5,2},{6,1},{7,0},{8,15},{9,14},{10,... | collective-permute-start | bytes 5192 | tf_op jit(solution)/shard_map/ppermute | solution.py:60
  439.5 46.8 %collective-permute-start.36 = (bf16[144,288]{1,0:T(8,128)(2,1)S(1)}, bf16[144,288]{1,0:T(8,128)(2,1)S(1)}, u32[]{:S(2)}, u32[]{:S(2)}) collective-permute-start(bf16[144,288]{1,0:T(8,128)(2,1)S(1)} %bitcast.217), channel_id=1, source_target_pairs={{0,8},{8,0},{16,24},{24,16},{1,9},{9,1},{17,25},{25,17},{2,10},{10... | collective-permute-start | bytes 248840 | tf_op jit(solution)/shard_map/ppermute | solution.py:60
  439.7 47.6 %collective-permute-start.37 = (bf16[144,288]{1,0:T(8,128)(2,1)S(1)}, bf16[144,288]{1,0:T(8,128)(2,1)S(1)}, u32[]{:S(2)}, u32[]{:S(2)}) collective-permute-start(bf16[144,288]{1,0:T(8,128)(2,1)S(1)} %bitcast.216), channel_id=1, source_target_pairs={{0,16},{8,24},{16,0},{24,8},{1,17},{9,25},{17,1},{25,9},{2,18},{10... | collective-permute-start | bytes 248840 | tf_op jit(solution)/shard_map/ppermute | solution.py:60
  441.0 5.8 %collective-permute-start.25 = (f32[4,504]{1,0:T(4,128)S(1)}, f32[4,504]{1,0:T(4,128)S(1)}, u32[]{:S(2)}, u32[]{:S(2)}) collective-permute-start(f32[4,504]{1,0:T(4,128)S(1)} %bitcast.224), channel_id=1, source_target_pairs={{0,3},{1,2},{2,1},{3,0},{4,7},{5,6},{6,5},{7,4},{8,11},{9,10},{10,... | collective-permute-start | bytes 24200 | tf_op jit(solution)/shard_map/ppermute | solution.py:60
  444.4 7.1 %collective-permute-start.27 = (f32[4,504]{1,0:T(4,128)S(1)}, f32[4,504]{1,0:T(4,128)S(1)}, u32[]{:S(2)}, u32[]{:S(2)}) collective-permute-start(f32[4,504]{1,0:T(4,128)S(1)} %bitcast.222), channel_id=1, source_target_pairs={{0,5},{1,4},{2,7},{3,6},{4,1},{5,0},{6,3},{7,2},{8,13},{9,12},{10,... | collective-permute-start | bytes 24200 | tf_op jit(solution)/shard_map/ppermute | solution.py:60
  446.9 5.4 %collective-permute-start.28 = (f32[4,504]{1,0:T(4,128)S(1)}, f32[4,504]{1,0:T(4,128)S(1)}, u32[]{:S(2)}, u32[]{:S(2)}) collective-permute-start(f32[4,504]{1,0:T(4,128)S(1)} %bitcast.221), channel_id=1, source_target_pairs={{0,6},{1,7},{2,4},{3,5},{4,2},{5,3},{6,0},{7,1},{8,14},{9,15},{10,... | collective-permute-start | bytes 24200 | tf_op jit(solution)/shard_map/ppermute | solution.py:60
  448.4 6.3 %collective-permute-start.29 = (f32[4,504]{1,0:T(4,128)S(1)}, f32[4,504]{1,0:T(4,128)S(1)}, u32[]{:S(2)}, u32[]{:S(2)}) collective-permute-start(f32[4,504]{1,0:T(4,128)S(1)} %bitcast.220), channel_id=1, source_target_pairs={{0,7},{1,6},{2,5},{3,4},{4,3},{5,2},{6,1},{7,0},{8,15},{9,14},{10,... | collective-permute-start | bytes 24200 | tf_op jit(solution)/shard_map/ppermute | solution.py:60
  464.3 6.0 %collective-permute-start.15 = (f32[4,288]{1,0:T(4,128)S(1)}, f32[4,288]{1,0:T(4,128)S(1)}, u32[]{:S(2)}, u32[]{:S(2)}) collective-permute-start(f32[4,288]{1,0:T(4,128)S(1)} %bitcast.230), channel_id=1, source_target_pairs={{0,3},{1,2},{2,1},{3,0},{4,7},{5,6},{6,5},{7,4},{8,11},{9,10},{10,... | collective-permute-start | bytes 13832 | tf_op jit(solution)/shard_map/ppermute | solution.py:60
  467.0 5.6 %collective-permute-start.16 = (f32[4,288]{1,0:T(4,128)S(1)}, f32[4,288]{1,0:T(4,128)S(1)}, u32[]{:S(2)}, u32[]{:S(2)}) collective-permute-start(f32[4,288]{1,0:T(4,128)S(1)} %bitcast.229), channel_id=1, source_target_pairs={{0,4},{1,5},{2,6},{3,7},{4,0},{5,1},{6,2},{7,3},{8,12},{9,13},{10,... | collective-permute-start | bytes 13832 | tf_op jit(solution)/shard_map/ppermute | solution.py:60
  467.9 6.8 %collective-permute-start.17 = (f32[4,288]{1,0:T(4,128)S(1)}, f32[4,288]{1,0:T(4,128)S(1)}, u32[]{:S(2)}, u32[]{:S(2)}) collective-permute-start(f32[4,288]{1,0:T(4,128)S(1)} %bitcast.228), channel_id=1, source_target_pairs={{0,5},{1,4},{2,7},{3,6},{4,1},{5,0},{6,3},{7,2},{8,13},{9,12},{10,... | collective-permute-start | bytes 13832 | tf_op jit(solution)/shard_map/ppermute | solution.py:60
  470.3 5.4 %collective-permute-start.18 = (f32[4,288]{1,0:T(4,128)S(1)}, f32[4,288]{1,0:T(4,128)S(1)}, u32[]{:S(2)}, u32[]{:S(2)}) collective-permute-start(f32[4,288]{1,0:T(4,128)S(1)} %bitcast.227), channel_id=1, source_target_pairs={{0,6},{1,7},{2,4},{3,5},{4,2},{5,3},{6,0},{7,1},{8,14},{9,15},{10,... | collective-permute-start | bytes 13832 | tf_op jit(solution)/shard_map/ppermute | solution.py:60
  472.6 6.3 %collective-permute-start.19 = (f32[4,288]{1,0:T(4,128)S(1)}, f32[4,288]{1,0:T(4,128)S(1)}, u32[]{:S(2)}, u32[]{:S(2)}) collective-permute-start(f32[4,288]{1,0:T(4,128)S(1)} %bitcast.226), channel_id=1, source_target_pairs={{0,7},{1,6},{2,5},{3,4},{4,3},{5,2},{6,1},{7,0},{8,15},{9,14},{10,... | collective-permute-start | bytes 13832 | tf_op jit(solution)/shard_map/ppermute | solution.py:60
  484.8 6.6 %collective-permute-start.34 = (bf16[144,288]{1,0:T(8,128)(2,1)S(1)}, bf16[144,288]{1,0:T(8,128)(2,1)S(1)}, u32[]{:S(2)}, u32[]{:S(2)}) collective-permute-start(bf16[144,288]{1,0:T(8,128)(2,1)S(1)} %bitcast.213), channel_id=1, source_target_pairs={{0,16},{8,24},{16,0},{24,8},{1,17},{9,25},{17,1},{25,9},{2,18},{10... | collective-permute-start | bytes 248840 | tf_op jit(solution)/shard_map/ppermute | solution.py:60
  486.3 8.6 %collective-permute-start.35 = (bf16[144,288]{1,0:T(8,128)(2,1)S(1)}, bf16[144,288]{1,0:T(8,128)(2,1)S(1)}, u32[]{:S(2)}, u32[]{:S(2)}) collective-permute-start(bf16[144,288]{1,0:T(8,128)(2,1)S(1)} %bitcast.212), channel_id=1, source_target_pairs={{0,24},{8,16},{16,8},{24,0},{1,25},{9,17},{17,9},{25,1},{2,26},{10... | collective-permute-start | bytes 248840 | tf_op jit(solution)/shard_map/ppermute | solution.py:60
  (34 other events, 219.8 us)

commit v3 on v0

--- a/solution.py
+++ b/solution.py
@@ -1,8 +1,11 @@
+import functools
 import math
 
 import jax
 import jax.numpy as jnp
 from jax import lax
+from jax.experimental import pallas as pl
+from jax.experimental.pallas import tpu as pltpu
 from jax.sharding import PartitionSpec as P
 
 HEADS = 16
@@ -38,15 +41,23 @@
     )
 
 
+def contract(left, right, left_dims, right_dims):
+    return lax.dot_general(
+        left, right, ((left_dims, right_dims), ((), ())), preferred_element_type=jnp.float32
+    )
+
+
+def rows_rows(left, right):
+    return contract(left, right, (0,), (0,))
+
+
+def times_transposed(left, right):
+    return contract(left, right, (1,), (1,))
+
+
 def inner_rows(left, right):
     return lax.dot_general(
         left, right, (((0,), (0,)), ((), ())), preferred_element_type=jnp.float32
-    )
-
-
-def times_transposed(left, right):
-    return lax.dot_general(
-        left, right, (((1,), (1,)), ((), ())), preferred_element_type=jnp.float32
     )
 
 
@@ -123,7 +134,7 @@
     return jnp.sum(matrix.astype(jnp.float32), axis=0)
 
 
-def shards(
+def plain_shards(
     patches_in,
     condition,
     keep_count,
@@ -355,40 +366,1283 @@
     )
 
 
+MESH = pl.DeviceIdType.MESH
+
+
+def remote(source, target, send, recv, device):
+    return pltpu.make_async_remote_copy(
+        src_ref=source,
+        dst_ref=target,
+        send_sem=send,
+        recv_sem=recv,
+        device_id=device,
+        device_id_type=MESH,
+    )
+
+
+def greet(devices):
+    barrier = pltpu.get_barrier_semaphore()
+    for device in devices:
+        pl.semaphore_signal(barrier, 1, device_id=device, device_id_type=MESH)
+    pl.semaphore_wait(barrier, len(devices))
+
+
+def normed(value):
+    centred = value - jnp.mean(value, axis=-1, keepdims=True)
+    rstd = lax.rsqrt(jnp.mean(centred * centred, axis=-1, keepdims=True) + epsilon)
+    return centred * rstd, rstd
+
+
+def forward_body(
+    sizes,
+    note_ref,
+    ada_ref,
+    piece_ref,
+    qkv_ref,
+    proj_ref,
+    kept_ref,
+    cot_ref,
+    count_ref,
+    qkv_all,
+    one_all,
+    two_all,
+    projected_ref,
+    attended_ref,
+    hidden_all,
+    branch_all,
+    proj_dense,
+    hidden_rows,
+    mixed_rows,
+    mod_ref,
+    bias_ref,
+    signal_ref,
+    proj_all,
+    mixed_ref,
+    piece_got,
+    one_block,
+    two_block,
+    note_got,
+    row_put,
+    row_got,
+    send_n,
+    recv_n,
+    send_z,
+    send_y,
+    send_x,
+    recv_w,
+    send_e,
+    recv_e,
+    local,
+):
+    heads, size, widths = sizes
+    n_dp, n_fs = 4, 8
+    d_at, f_at = lax.axis_index("dp"), lax.axis_index("fsdp")
+    own_at = d_at * n_fs + f_at
+    slots, features = kept_ref.shape
+    half_rows, cols = qkv_ref.shape[0], qkv_ref.shape[1] // 2
+    unit = one_block.shape[0]
+    row_width = 2 * half_rows
+    width = proj_ref.shape[1] // 2
+    low = jnp.bfloat16
+    full = jnp.float32
+    others = [(a, b) for a in range(n_dp) for b in range(n_fs) if a or b]
+    greet([(d_at ^ a, f_at ^ b) for a, b in others])
+
+    own_blocks = (qkv_ref, proj_ref, one_block, two_block)
+    gathered = (qkv_all, proj_all, one_all, two_all)
+    started = []
+
+    def slot(array, a, b):
+        if array < 2:
+            start = pl.multiple_of((d_at ^ a) * half_rows, 16)
+            return gathered[array].at[f_at ^ b, pl.ds(start, half_rows), :]
+        start = pl.multiple_of((f_at ^ b) * unit, 16)
+        return gathered[array].at[pl.ds(start, unit), :]
+
+    def push(source, target, send, recv, device):
+        copy = remote(source, target, send, recv, device)
+        copy.start()
+        started.append(copy)
+
+    def pass_on(array, a, b, axis, mask, sem):
+        device = (d_at ^ mask, f_at) if axis == 0 else (d_at, f_at ^ mask)
+        to_a, to_b = (a ^ mask, b) if axis == 0 else (a, b ^ mask)
+        source = own_blocks[array] if a == 0 and b == 0 else slot(array, a, b)
+        push(source, slot(array, a, b), sem, recv_w.at[array, to_a, to_b], device)
+
+    def arrive(array, a, b):
+        place = slot(array, a, b)
+        pltpu.make_async_copy(place, place, recv_w.at[array, a, b]).wait()
+
+    def wide(array):
+        for mask in (2, 4, 6):
+            pass_on(array, 0, 0, 1, mask, send_z.at[array, mask // 2 - 1])
+
+    def near(array, b):
+        pass_on(array, 0, b, 1, 1, send_y.at[array, b // 2])
+
+    def onward(array, a, b):
+        if a == 0:
+            pass_on(array, a, b, 0, 2, send_x.at[array, 0, b])
+        if a in (0, 2):
+            pass_on(array, a, b, 0, 1, send_x.at[array, 1 + a // 2, b])
+
+    near(0, 0)
+    wide(0)
+    onward(0, 0, 0)
+    for place, (a, b) in enumerate(others):
+        push(
+            note_ref.at[d_at ^ a],
+            note_got.at[own_at],
+            send_n.at[0, place],
+            recv_n.at[0, place],
+            (d_at ^ a, f_at ^ b),
+        )
+    stays = [
+        pltpu.make_async_copy(note_ref.at[d_at], note_got.at[own_at], local.at[0]),
+        pltpu.make_async_copy(qkv_ref, slot(0, 0, 0), local.at[1]),
+        pltpu.make_async_copy(proj_ref, slot(1, 0, 0), local.at[2]),
+        pltpu.make_async_copy(piece_ref.at[d_at], piece_got.at[d_at], local.at[3]),
+    ]
+    for stay in stays:
+        stay.start()
+    wide(1)
+    for mask in (1, 2, 3):
+        push(
+            piece_ref.at[d_at ^ mask],
+            piece_got.at[d_at],
+            send_e.at[2, mask],
+            recv_e.at[2, mask],
+            (d_at ^ mask, f_at),
+        )
+
+    kept = kept_ref[...]
+    normed_one, _ = normed(kept)
+
+    stays[0].wait()
+    for place, (a, b) in enumerate(others):
+        at = (d_at ^ a) * n_fs + (f_at ^ b)
+        pltpu.make_async_copy(note_got.at[at], note_got.at[at], recv_n.at[0, place]).wait()
+    notes = note_got[...]
+    signals = jnp.concatenate([notes[:, row, :] for row in range(3)], axis=1).astype(low)
+    signal_ref[...] = signals
+    terms = jnp.dot(signals, ada_ref[...], preferred_element_type=full)
+    ada_width = widths[0]
+    ada_piece = ada_width * n_fs // (n_dp * n_fs)
+
+    def bias_piece(index, start, count):
+        row = note_got[index]
+        line = jnp.concatenate([row[3 + step : 4 + step, :] for step in range(5)], axis=1)
+        return line[:, start : start + count]
+
+    block_bias = jnp.concatenate(
+        [bias_piece(f_at * n_dp + step, 0, ada_piece) for step in range(n_dp)], axis=1
+    )
+    first = (d_at == 0).astype(full)
+    for row in range(7):
+        piece = terms[:, row * 128 : (row + 1) * 128]
+        count = min(128, ada_width - row * 128)
+        add = block_bias[:, row * 128 : row * 128 + count] * first
+        if count < 128:
+            add = jnp.concatenate([add, jnp.zeros((1, 128 - count), full)], axis=1)
+        row_put[:, row, :] = piece + add
+    for place, (a, b) in enumerate(others):
+        push(
+            row_put.at[(d_at ^ a) * n_fs + (f_at ^ b)],
+            row_got.at[own_at],
+            send_n.at[1, place],
+            recv_n.at[1, place],
+            (d_at ^ a, f_at ^ b),
+        )
+    keep_row = pltpu.make_async_copy(row_put.at[own_at], row_got.at[own_at], local.at[0])
+    keep_row.start()
+
+    arrive(0, 0, 1)
+    onward(0, 0, 1)
+    arrive(0, 0, 2)
+    near(0, 2)
+    onward(0, 0, 2)
+
+    qv_width, one_width, out_width = widths[1:]
+    starts = [ada_piece, ada_piece + qv_width, ada_piece + qv_width + one_width]
+    lines = []
+    for index in range(n_dp * n_fs):
+        lines.append(
+            (
+                bias_piece(index, starts[0], qv_width),
+                bias_piece(index, starts[2], out_width),
+            )
+        )
+    heads_per = cols // size
+    for f in range(n_fs):
+        parts = []
+        for j in range(heads_per):
+            head = f * heads_per + j
+            if head < heads:
+                parts.append(lines[head][0])
+            elif head < 2 * heads:
+                parts.append(jnp.zeros((1, size), full))
+            else:
+                parts.append(lines[head - heads][0])
+        bias_ref[f : f + 1, :cols] = jnp.concatenate(parts, axis=1)
+    bias_ref[8:9, :] = jnp.concatenate([line[1] for line in lines[:heads]], axis=1)
+    bias_ref[9:10, :] = jnp.concatenate([line[1] for line in lines[heads:]], axis=1)
+    bias_ref[10:11, :] = jnp.concatenate(
+        [bias_piece(f * n_dp + d_at, starts[1], one_width) for f in range(n_fs)], axis=1
+    )
+
+    arrive(0, 0, 4)
+    near(0, 4)
+    onward(0, 0, 4)
+    arrive(0, 0, 3)
+    onward(0, 0, 3)
+
+    keep_row.wait()
+    for place, (a, b) in enumerate(others):
+        at = (d_at ^ a) * n_fs + (f_at ^ b)
+        pltpu.make_async_copy(row_got.at[at], row_got.at[at], recv_n.at[1, place]).wait()
+    sums = row_got[0:n_fs]
+    for d in range(1, n_dp):
+        sums = sums + row_got[d * n_fs : (d + 1) * n_fs]
+    sums = jnp.concatenate([sums[:, row, :] for row in range(7)], axis=1)
+    pieces = []
+    for index in range(6 * n_dp):
+        f, third = index // 3, index % 3
+        pieces.append(sums[f : f + 1, third * row_width : (third + 1) * row_width])
+    mods = []
+    for row in range(6):
+        mods.append(jnp.concatenate(pieces[row * n_dp : (row + 1) * n_dp], axis=1))
+        mod_ref[row : row + 1, :] = mods[row]
+    hidden_one = (normed_one * (1.0 + mods[1]) + mods[0]).astype(low)
+    branch_all[0] = (mods[5] * cot_ref[...].astype(full)).astype(low)
+    chunks = [
+        hidden_one[:, place * half_rows : (place + 1) * half_rows] for place in range(2 * n_dp)
+    ]
+    for d in range(n_dp):
+        hidden_rows[d] = jnp.concatenate(chunks[2 * d : 2 * d + 2], axis=1)
+    halves = [jnp.concatenate(chunks[part::2], axis=1) for part in range(2)]
+
+    stays[3].wait()
+    for mask in (1, 2, 3):
+        place = piece_got.at[d_at ^ mask]
+        pltpu.make_async_copy(place, place, recv_e.at[2, mask]).wait()
+    one_block[...] = jnp.concatenate([piece_got[d, :, :row_width] for d in range(n_dp)], axis=1)
+    two_block[...] = jnp.concatenate([piece_got[d, :, row_width:] for d in range(n_dp)], axis=1)
+
+    arrive(0, 0, 6)
+    near(0, 6)
+    onward(0, 0, 6)
+    near(1, 0)
+    arrive(0, 0, 5)
+    onward(0, 0, 5)
+    arrive(0, 0, 7)
+    onward(0, 0, 7)
+    onward(1, 0, 0)
+    arrive(1, 0, 1)
+    onward(1, 0, 1)
+    arrive(1, 0, 2)
+    near(1, 2)
+    onward(1, 0, 2)
+    wide(2)
+    wide(3)
+    keep_one = pltpu.make_async_copy(one_block, slot(2, 0, 0), local.at[0])
+    keep_one.start()
+    keep_two = pltpu.make_async_copy(two_block, slot(3, 0, 0), local.at[3])
+    keep_two.start()
+    arrive(1, 0, 4)
+    near(1, 4)
+    onward(1, 0, 4)
+    arrive(1, 0, 3)
+    onward(1, 0, 3)
+    arrive(1, 0, 6)
+    near(1, 6)
+    onward(1, 0, 6)
+    near(2, 0)
+    arrive(1, 0, 5)
+    onward(1, 0, 5)
+    arrive(1, 0, 7)
+    onward(1, 0, 7)
+
+    def spread_step(buffer, kind, mask):
+        for key in [0] if mask == 2 else [0, 2]:
+            push(
+                buffer.at[key],
+                buffer.at[key ^ mask],
+                send_e.at[kind, key ^ mask],
+                recv_e.at[kind, key ^ mask],
+                (d_at ^ mask, f_at),
+            )
+
+    def spread_wait(buffer, kind, keys):
+        for key in keys:
+            place = buffer.at[key]
+            pltpu.make_async_copy(place, place, recv_e.at[kind, key]).wait()
+
+    stays[1].wait()
+    order = [0, 1, 2, 4, 3, 6, 5, 7]
+    for place, b in enumerate(order):
+        arrive(0, 2, b)
+        onward(0, 2, b)
+        arrive(0, 1, b)
+        arrive(0, 3, b)
+        f = f_at ^ b
+        out = jnp.dot(halves[0], qkv_all[f, :, :cols], preferred_element_type=full)
+        out = out + jnp.dot(halves[1], qkv_all[f, :, cols:], preferred_element_type=full)
+        projected_ref[f] = (out + bias_ref[pl.ds(f, 1), :cols]).astype(low)
+    spread_step(branch_all, 0, 2)
+
+    relays = []
+    for array in (2, 3):
+        for mask in (2, 4, 6):
+            relays.append((array, mask))
+
+    def relay():
+        array, mask = relays.pop(0)
+        arrive(array, 0, mask)
+        near(array, mask)
+        if (array, mask) == (2, 6):
+            near(3, 0)
+
+    allowed = lax.broadcasted_iota(jnp.int32, (slots, slots), 1) < count_ref[0]
+    factor = 1.0 / math.sqrt(size)
+    for h in range(heads):
+        q, k, v = [
+            projected_ref[f, :, j * size : (j + 1) * size]
+            for f, j in (
+                ((kind * heads + h) // heads_per, (kind * heads + h) % heads_per)
+                for kind in range(3)
+            )
+        ]
+        scores = contract(q, k, (1,), (1,)) * factor
+        scores = jnp.where(allowed, scores, negative)
+        exponent = jnp.exp(scores - jnp.max(scores, axis=-1, keepdims=True))
+        softmax = exponent / jnp.sum(exponent, axis=-1, keepdims=True)
+        mix = jnp.dot(softmax.astype(low), v, preferred_element_type=full).astype(low)
+        pair, side = h // 2, h % 2
+        start = ((pair % 2) * n_dp + pair // 2) * half_rows + side * size
+        mixed_ref[:, start : start + size] = mix
+        start = (pair % 2) * half_rows + side * size
+        mixed_rows[pair // 2, :, start : start + size] = mix
+        if h in (3, 7, 11):
+            relay()
+        if h == 8:
+            spread_wait(branch_all, 0, [2])
+            spread_step(branch_all, 0, 1)
+
+    for b in order:
+        arrive(1, 2, b)
+        onward(1, 2, b)
+    stays[2].wait()
+    for b in order:
+        arrive(1, 1, b)
+        arrive(1, 3, b)
+    for f in range(n_fs):
+        for part in range(2):
+            proj_dense[
+                part * n_dp * half_rows : (part + 1) * n_dp * half_rows,
+                f * width : (f + 1) * width,
+            ] = proj_all[f, :, part * width : (part + 1) * width]
+    attended = (
+        jnp.dot(mixed_ref[...], proj_dense[...], preferred_element_type=full) + bias_ref[8:9, :]
+    )
+    attended_ref[...] = attended
+    middle = kept + mods[2] * attended
+    normed_two, _ = normed(middle)
+    hidden_all[0] = (normed_two * (1.0 + mods[4]) + mods[3]).astype(low)
+    spread_step(hidden_all, 1, 2)
+    relay()
+    spread_wait(hidden_all, 1, [2])
+    spread_step(hidden_all, 1, 1)
+    relay()
+    relay()
+    spread_wait(hidden_all, 1, [1, 3])
+    spread_wait(branch_all, 0, [1, 3])
+    for array in (2, 3):
+        for b in (1, 3, 5, 7):
+            arrive(array, 0, b)
+    keep_one.wait()
+    keep_two.wait()
+    for copy in started:
+        copy.wait_send()
+
+
+def forward_kernel(notes, ada, pieces, qkv, proj, kept, cot, count, widths):
+    n_dp, n_fs = lax.axis_size("dp"), lax.axis_size("fsdp")
+    slots, features = kept.shape
+    unit = pieces.shape[1]
+    size = features // HEADS
+    half_rows = qkv.shape[0]
+    cols = qkv.shape[1] // 2
+    n_all = n_dp * n_fs
+    low, full = jnp.bfloat16, jnp.float32
+    vmem = pl.BlockSpec(memory_space=pltpu.VMEM)
+    shapes = [
+        ((n_fs, n_dp * half_rows, 2 * cols), low),
+        ((n_fs * unit, features), low),
+        ((features, n_fs * unit), low),
+        ((n_fs, slots, cols), low),
+        ((slots, features), full),
+        ((n_dp, slots, features), low),
+        ((n_dp, slots, features), low),
+        ((features, features), low),
+        ((n_dp, slots, 2 * half_rows), low),
+        ((n_dp, slots, 2 * half_rows), low),
+        ((8, features), full),
+        ((16, features), full),
+        ((n_all, 384), low),
+    ]
+    scratch = [
+        ((n_fs, n_dp * half_rows, proj.shape[1]), low),
+        ((slots, features), low),
+        (pieces.shape, low),
+        ((unit, features), low),
+        ((unit, features), low),
+        ((n_all, 8, 128), full),
+        ((n_all, 8, 128), full),
+        ((n_all, 8, 128), full),
+    ]
+    dma = pltpu.SemaphoreType.DMA
+    return pl.pallas_call(
+        functools.partial(forward_body, (HEADS, size, widths)),
+        out_shape=[jax.ShapeDtypeStruct(shape, kind) for shape, kind in shapes],
+        in_specs=[vmem] * 7 + [pl.BlockSpec(memory_space=pltpu.SMEM)],
+        out_specs=[vmem] * len(shapes),
+        scratch_shapes=[pltpu.VMEM(shape, kind) for shape, kind in scratch]
+        + [dma((2, n_all - 1)), dma((2, n_all - 1)), dma((4, 3)), dma((4, 4))]
+        + [dma((2, 3, n_fs)), dma((4, n_dp, n_fs)), dma((3, 4)), dma((3, 4)), dma((4,))],
+        compiler_params=pltpu.CompilerParams(
+            collective_id=5, has_side_effects=True, vmem_limit_bytes=64 * 1024 * 1024 - 65536
+        ),
+        name="forward",
+    )(notes, ada, pieces, qkv, proj, kept, cot, count)
+
+
+def gelu_parts(raised):
+    square = raised * raised
+    inner = 0.7978845608028654 * raised * (1.0 + 0.044715 * square)
+    bend = jnp.tanh(inner)
+    slope = 0.7978845608028654 * (1.0 + 3.0 * 0.044715 * square)
+    half = 0.5 * (1.0 + bend)
+    return raised * half, half + 0.5 * raised * (1.0 - bend * bend) * slope
+
+
+def column_sums(value):
+    return jnp.sum(value, axis=0, keepdims=True)
+
+
+def store_tile(ref, index, line):
+    for row in range(8):
+        piece = line[:, row * 128 : (row + 1) * 128]
+        if piece.shape[1] == 0:
+            break
+        if piece.shape[1] < 128:
+            rest = jnp.zeros((1, 128 - piece.shape[1]), line.dtype)
+            piece = jnp.concatenate([piece, rest], axis=1)
+        ref[index, row : row + 1, :] = piece
+
+
+def backward_body(
+    sizes,
+    qkv_hbm,
+    ada_ref,
+    signal_ref,
+    proj_ref,
+    one_ref,
+    two_ref,
+    projected_ref,
+    attended_ref,
+    hidden_all,
+    branch_all,
+    hidden_rows,
+    mixed_rows,
+    kept_ref,
+    mod_ref,
+    bias_ref,
+    cot_ref,
+    count_ref,
+    block_ref,
+    d_kept_ref,
+    mlp_out,
+    att_out,
+    ada_out,
+    last_got,
+    act_ref,
+    d_raised_ref,
+    part_ref,
+    core_got,
+    cross_put,
+    cross_got,
+    grads,
+    got_y,
+    got_z,
+    rows_got,
+    d_att_all,
+    d_mixed_ref,
+    d_proj_all,
+    weight_ring,
+    mlp_put,
+    d_mod_ref,
+    sum_put,
+    sum_got,
+    note_put,
+    note_got,
+    last_put,
+    send_m,
+    recv_m,
+    send_d,
+    recv_d,
+    send_e,
+    recv_e,
+    send_p,
+    recv_p,
+    send_n,
+    recv_n,
+    send_s,
+    recv_s,
+    send_b,
+    recv_b,
+    local,
+):
+    heads, size, ada_width = sizes
+    n_dp, n_fs = 4, 8
+    d_at, f_at = lax.axis_index("dp"), lax.axis_index("fsdp")
+    own_at = d_at * n_fs + f_at
+    slots, features = kept_ref.shape
+    cols = projected_ref.shape[2]
+    heads_per = cols // size
+    row_width = features // n_dp
+    half_rows = row_width // 2
+    unit = features // n_fs
+    low = jnp.bfloat16
+    full = jnp.float32
+    core, cross, near = (d_at ^ 1, f_at), (d_at ^ 2, f_at), (d_at, f_at ^ 1)
+    others = [(a, b) for a in range(n_dp) for b in range(n_fs) if a or b]
+    greet([(d_at ^ a, f_at ^ b) for a, b in others])
+    sent = []
+
+    def push(source, target, send, recv, device):
+        copy = remote(source, target, send, recv, device)
+        copy.start()
+        sent.append(copy)
+        return copy
+
+    def arrive(place, recv):
+        pltpu.make_async_copy(place, place, recv).wait()
+
+    stays = []
+    for kind, source in enumerate((hidden_rows, mixed_rows)):
+        for mask in (2, 3, 1):
+            push(
+                source.at[d_at ^ mask],
+                rows_got.at[kind, mask],
+                send_p.at[kind, mask],
+                recv_p.at[kind, mask],
+                (d_at ^ mask, f_at),
+            )
+        stays.append(
+            pltpu.make_async_copy(source.at[d_at], rows_got.at[kind, 0], local.at[kind])
+        )
+        stays[kind].start()
+
+    def image_step(image, carry):
+        raised = contract(hidden_all[image], one_ref[...], (1,), (1,)) + bias_ref[10:11, :]
+        active, slope = gelu_parts(raised)
+        act_ref[image] = active.astype(low)
+        d_active = jnp.dot(branch_all[image], two_ref[...], preferred_element_type=full)
+        d_raised_ref[image] = (d_active * slope).astype(low)
+        return carry
+
+    lax.fori_loop(0, n_dp, image_step, 0)
+
+    def flat(ref, start, count):
+        return ref[:, :, pl.ds(start, count)].reshape(n_dp * slots, count)
+
+    def weight_grad(kind, left, right):
+        step = features // 3
+        for part in range(3):
+            grads[kind, part * step : (part + 1) * step, :] = rows_rows(
+                flat(left, part * step, step), flat(right, 0, features)
+            ).astype(low)
+
+    def block_rows(index):
+        return pl.ds(pl.multiple_of(index * unit, 16), unit)
+
+    def send_block(kind, place, index):
+        push(
+            grads.at[kind, block_rows(index), :],
+            got_y.at[kind, place],
+            send_m.at[kind, place],
+            recv_m.at[kind, place],
+            near,
+        )
+
+    def fold_block(kind, place, index):
+        arrive(got_y.at[kind, place], recv_m.at[kind, place])
+        rows = block_rows(index)
+        grads[kind, rows, :] = (
+            grads[kind, rows, :].astype(full) + got_y[kind, place].astype(full)
+        ).astype(low)
+
+    def send_wide(kind, index, mask):
+        place = mask // 2 - 1
+        return remote(
+            grads.at[kind, block_rows(index), :],
+            got_z.at[kind, place],
+            send_m.at[kind, 4 + place],
+            recv_m.at[kind, 4 + place],
+            (d_at, index),
+        )
+
+    def fold_all(kind):
+        for place, wide in enumerate((2, 4, 6, 0)):
+            fold_block(kind, place, f_at ^ wide)
+            if wide:
+                copy = send_wide(kind, f_at ^ wide, wide)
+                copy.start()
+                sent.append(copy)
+
+    def finish(kind):
+        total = grads[kind, block_rows(f_at), :].astype(full)
+        for place in range(3):
+            arrive(got_z.at[kind, place], recv_m.at[kind, 4 + place])
+            total = total + got_z[kind, place].astype(full)
+        return total
+
+    weight_grad(1, branch_all, act_ref)
+    for place, wide in enumerate((2, 4, 6, 0)):
+        send_block(1, place, f_at ^ wide ^ 1)
+
+    def part_step(left, right, dims):
+        def step(image, carry):
+            part_ref[image] = contract(left[image], right[...], (1,), dims).astype(low)
+            return carry
+
+        lax.fori_loop(0, n_dp, step, 0)
+
+    def core_send(kind):
+        return [
+            push(
+                part_ref.at[image],
+                core_got.at[kind, place],
+                send_d.at[kind, place],
+                recv_d.at[kind, place],
+                core,
+            )
+            for place, image in enumerate((3, 1))
+        ]
+
+    def cross_send(kind):
+        arrive(core_got.at[kind, 0], recv_d.at[kind, 0])
+        cross_put[kind] = (
+            part_ref[2].astype(full) + core_got[kind, 0].astype(full)
+        ).astype(low)
+        push(
+            cross_put.at[kind], cross_got.at[kind], send_d.at[kind, 2], recv_d.at[kind, 2], cross
+        )
+        arrive(core_got.at[kind, 1], recv_d.at[kind, 1])
+
+    part_step(d_raised_ref, one_ref, (0,))
+    leaving = core_send(0)
+    cross_send(0)
+    own_part = part_ref[0].astype(full) + core_got[0, 1].astype(full)
+    weight_grad(0, d_raised_ref, hidden_all)
+    for place, wide in enumerate((2, 4, 6, 0)):
+        send_block(0, place, f_at ^ wide ^ 1)
+    fold_all(1)
+    one_sum = jnp.zeros((1, features), full)
+    for image in range(n_dp):
+        one_sum = one_sum + column_sums(d_raised_ref[image].astype(full))
+    branch_sum = column_sums(branch_all[0].astype(full))
+
+    mods = [mod_ref[row : row + 1, :] for row in range(6)]
+    kept = kept_ref[...]
+    attended = attended_ref[...]
+    middle = kept + mods[2] * attended
+    normed_two, rstd_two = normed(middle)
+    upstream = cot_ref[...].astype(full)
+    arrive(cross_got.at[0], recv_d.at[0, 2])
+    d_hidden_two = own_part + cross_got[0].astype(full)
+    d_mod_ref[3:4, :] = column_sums(d_hidden_two)
+    d_mod_ref[4:5, :] = column_sums(d_hidden_two * normed_two)
+    d_middle = upstream + norm_back(d_hidden_two * (1.0 + mods[4]), normed_two, rstd_two)
+    d_mod_ref[2:3, :] = column_sums(d_middle * attended)
+    d_attended = (mods[2] * d_middle).astype(low)
+    d_att_all[0] = d_attended
+    d_kept_ref[...] = d_middle
+    att_sum = column_sums(d_attended.astype(full))
+    d_mixed_ref[...] = contract(d_attended, proj_ref[...], (1,), (1,)).astype(low)
+    push(d_att_all.at[0], d_att_all.at[2], send_e.at[2], recv_e.at[2], cross)
+    push(d_att_all.at[0], d_att_all.at[1], send_e.at[1], recv_e.at[1], core)
+
+    for copy in leaving:
+        copy.wait_send()
+    part_step(act_ref, two_ref, (1,))
+    core_send(1)
+    cross_send(1)
+
+    def pass_block(f):
+        push(
+            d_proj_all.at[0, f],
+            d_proj_all.at[2, f],
+            send_p.at[2 + f, 2],
+            recv_p.at[2 + f, 2],
+            cross,
+        )
+        push(
+            d_proj_all.at[0, f],
+            d_proj_all.at[1, f],
+            send_p.at[2 + f, 1],
+            recv_p.at[2 + f, 1],
+            core,
+        )
+
+    def relay_block(f):
+        arrive(d_proj_all.at[2, f], recv_p.at[2 + f, 2])
+        push(
+            d_proj_all.at[2, f],
+            d_proj_all.at[3, f],
+            send_p.at[2 + f, 3],
+            recv_p.at[2 + f, 3],
+            core,
+        )
+
+    allowed = lax.broadcasted_iota(jnp.int32, (slots, slots), 1) < count_ref[0]
+    factor = 1.0 / math.sqrt(size)
+    done_after = {5: [0], 7: [3], 9: [6], 11: [1], 13: [4], 15: [2, 5, 7]}
+    relay_after = {11: [0], 13: [3], 15: [6]}
+    for h in range(heads):
+        places = [
+            ((kind * heads + h) // heads_per, (kind * heads + h) % heads_per)
+            for kind in range(3)
+        ]
+        q, k, v = [projected_ref[f, :, j * size : (j + 1) * size] for f, j in places]
+        pair, side = h // 2, h % 2
+        start = ((pair % 2) * n_dp + pair // 2) * half_rows + side * size
+        d_mix = d_mixed_ref[:, start : start + size]
+        scores = contract(q, k, (1,), (1,)) * factor
+        scores = jnp.where(allowed, scores, negative)
+        exponent = jnp.exp(scores - jnp.max(scores, axis=-1, keepdims=True))
+        softmax = exponent / jnp.sum(exponent, axis=-1, keepdims=True)
+        d_softmax = contract(d_mix, v, (1,), (1,))
+        delta = jnp.sum(d_softmax * softmax, axis=-1, keepdims=True)
+        d_scores = (softmax * (d_softmax - delta)).astype(low)
+        results = [
+            jnp.dot(d_scores, k, preferred_element_type=full) * factor,
+            rows_rows(d_scores, q) * factor,
+            rows_rows(softmax.astype(low), d_mix),
+        ]
+        for (f, j), result in zip(places, results):
+            d_proj_all[0, f, :, j * size : (j + 1) * size] = result.astype(low)
+        for f in done_after.get(h, []):
+            pass_block(f)
+        for f in relay_after.get(h, []):
+            relay_block(f)
+        if h == 2:
+            fold_all(0)
+        if h == 6:
+            arrive(d_att_all.at[2], recv_e.at[2])
+            push(d_att_all.at[2], d_att_all.at[3], send_e.at[3], recv_e.at[3], core)
+
+    for stay in stays:
+        stay.wait()
+    for kind in range(2):
+        for mask in (2, 3, 1):
+            arrive(rows_got.at[kind, mask], recv_p.at[kind, mask])
+    for mask in (1, 3):
+        arrive(d_att_all.at[mask], recv_e.at[mask])
+    grad_proj = rows_rows(
+        rows_got[1].reshape(n_dp * slots, row_width),
+        d_att_all[...].reshape(n_dp * slots, features),
+    ).astype(low)
+    for f in range(n_fs):
+        for part in range(2):
+            grads[
+                2,
+                f * unit : (f + 1) * unit,
+                2 * cols + part * unit : 2 * cols + (part + 1) * unit,
+            ] = grad_proj[part * half_rows : (part + 1) * half_rows, f * unit : (f + 1) * unit]
+
+    def qkv_grad(f):
+        result = rows_rows(
+            rows_got[0].reshape(n_dp * slots, row_width),
+            d_proj_all[:, f].reshape(n_dp * slots, cols),
+        ).astype(low)
+        for part in range(2):
+            grads[2, block_rows(f), part * cols : (part + 1) * cols] = result[
+                part * half_rows : (part + 1) * half_rows, :
+            ]
+
+    odd = f_at % 2
+    pairs = [(0, 3), (6, 1), (4, 5), (2, 7)]
+
+    def grad_pair(place):
+        even_f, odd_f = pairs[place]
+        for f in (even_f, odd_f):
+            for mask in (1, 3):
+                arrive(d_proj_all.at[mask, f], recv_p.at[2 + f, mask])
+        goes = jnp.where(odd == 0, odd_f, even_f)
+        qkv_grad(goes)
+        send_block(2, place, goes)
+        qkv_grad(even_f + odd_f - goes)
+
+    def fold_pair(place):
+        even_f, odd_f = pairs[place]
+        index = jnp.where(odd == 0, even_f, odd_f)
+        fold_block(2, place, index)
+
+        @pl.when(index != f_at)
+        def _():
+            send_wide(2, index, index ^ f_at).start()
+
+    grad_pair(0)
+    relay_block(1)
+    relay_block(4)
+    grad_pair(1)
+
+    loads = [
+        pltpu.make_async_copy(qkv_hbm.at[f], weight_ring.at[f % 2], local.at[2 + f % 2])
+        for f in range(n_fs)
+    ]
+    loads[0].start()
+    halves = [jnp.zeros((slots, features // 2), full) for part in range(2)]
+    for f in range(n_fs):
+        if f + 1 < n_fs:
+            loads[f + 1].start()
+        loads[f].wait()
+        own = d_proj_all[0, f]
+        for part in range(2):
+            halves[part] = halves[part] + contract(
+                own, weight_ring[f % 2, :, part * cols : (part + 1) * cols], (1,), (1,)
+            )
+        line = jnp.concatenate(
+            [
+                column_sums(own.astype(full)),
+                att_sum[:, f * unit : (f + 1) * unit],
+                branch_sum[:, f * unit : (f + 1) * unit],
+                one_sum[:, f * unit : (f + 1) * unit],
+            ],
+            axis=1,
+        )
+        store_tile(sum_put, f, line)
+        if f == 3:
+            relay_block(2)
+        if f == 6:
+            relay_block(5)
+    relay_block(7)
+    d_hidden_one = jnp.concatenate(
+        [
+            halves[part][:, d * half_rows : (d + 1) * half_rows]
+            for d in range(n_dp)
+            for part in range(2)
+        ],
+        axis=1,
+    )
+    normed_one, rstd_one = normed(kept)
+    d_mod_ref[0:1, :] = column_sums(d_hidden_one)
+    d_mod_ref[1:2, :] = column_sums(d_hidden_one * normed_one)
+
+    arrive(cross_got.at[1], recv_d.at[1, 2])
+    branch = (
+        part_ref[0].astype(full)
+        + core_got[1, 1].astype(full)
+        + cross_got[1].astype(full)
+        + bias_ref[9:10, :]
+    )
+    d_mod_ref[5:6, :] = column_sums(upstream * branch)
+
+    third = ada_width // 3
+    pieces = []
+    for row in range(6):
+        line = d_mod_ref[row : row + 1, :].astype(low).astype(full)
+        pieces += [line[:, step * third : (step + 1) * third] for step in range(n_dp)]
+    for f in range(n_fs):
+        store_tile(note_put, f, jnp.concatenate(pieces[3 * f : 3 * f + 3], axis=1))
+    for mask in range(1, n_fs):
+        push(
+            sum_put.at[f_at ^ mask],
+            sum_got.at[mask],
+            send_s.at[mask],
+            recv_s.at[mask],
+            (d_at, f_at ^ mask),
+        )
+    for place, (a, b) in enumerate(others):
+        push(
+            note_put.at[f_at ^ b],
+            note_got.at[own_at],
+            send_n.at[0, place],
+            recv_n.at[0, place],
+            (d_at ^ a, f_at ^ b),
+        )
+    keep_note = pltpu.make_async_copy(note_put.at[f_at], note_got.at[own_at], local.at[0])
+    keep_note.start()
+    keep_sum = pltpu.make_async_copy(sum_put.at[f_at], sum_got.at[0], local.at[1])
+    keep_sum.start()
+    grad_pair(2)
+    fold_pair(0)
+    grad_pair(3)
+    fold_pair(1)
+    d_kept_ref[...] = d_kept_ref[...] + norm_back(
+        d_hidden_one * (1.0 + mods[1]), normed_one, rstd_one
+    )
+    block_ref[...] = (middle + mods[5] * branch).astype(low)
+
+    keep_mlp = []
+    for kind in range(2):
+        total = finish(kind).astype(low)
+        for d in range(n_dp):
+            mlp_put[kind, d] = total[:, d * row_width : (d + 1) * row_width]
+        for mask in (2, 3, 1):
+            push(
+                mlp_put.at[kind, d_at ^ mask],
+                mlp_out.at[kind, d_at],
+                send_b.at[kind, mask],
+                recv_b.at[kind, mask],
+                (d_at ^ mask, f_at),
+            )
+        keep_mlp.append(
+            pltpu.make_async_copy(
+                mlp_put.at[kind, d_at], mlp_out.at[kind, d_at], local.at[2 + kind]
+            )
+        )
+        keep_mlp[kind].start()
+
+    keep_note.wait()
+    keep_sum.wait()
+    for mask in range(1, n_fs):
+        arrive(sum_got.at[mask], recv_s.at[mask])
+    for place, (a, b) in enumerate(others):
+        at = (d_at ^ a) * n_fs + (f_at ^ b)
+        arrive(note_got.at[at], recv_n.at[0, place])
+    sums = sum_got[0]
+    for mask in range(1, n_fs):
+        sums = sums + sum_got[mask]
+    notes = note_got[...]
+    all_d = jnp.concatenate([notes[:, row, :] for row in range(7)], axis=1)
+    totals = column_sums(all_d)
+    all_d = all_d.astype(low)
+    terms = contract(all_d, ada_ref[...], (1,), (1,))
+    for row in range(3):
+        last_put[:, row, :] = terms[:, row * 128 : (row + 1) * 128]
+    everyone = (n_dp * n_fs, 128)
+    for row in range(7):
+        last_put[:, 8 + row, :] = jnp.broadcast_to(sums[row : row + 1, :], everyone)
+        last_put[:, 16 + row, :] = jnp.broadcast_to(
+            totals[:, row * 128 : (row + 1) * 128], everyone
+        )
+    fold_pair(2)
+    for place, (a, b) in enumerate(others):
+        push(
+            last_put.at[(d_at ^ a) * n_fs + (f_at ^ b)],
+            last_got.at[own_at],
+            send_n.at[1, place],
+            recv_n.at[1, place],
+            (d_at ^ a, f_at ^ b),
+        )
+    keep_last = pltpu.make_async_copy(last_put.at[own_at], last_got.at[own_at], local.at[0])
+    keep_last.start()
+    fold_pair(3)
+    ada_out[...] = rows_rows(signal_ref[...], all_d)[: ada_out.shape[0], : ada_out.shape[1]]
+    att_out[...] = finish(2)
+    for kind in range(2):
+        keep_mlp[kind].wait()
+        for mask in (1, 2, 3):
+            arrive(mlp_out.at[kind, d_at ^ mask], recv_b.at[kind, mask])
+    keep_last.wait()
+    for place, (a, b) in enumerate(others):
+        at = (d_at ^ a) * n_fs + (f_at ^ b)
+        arrive(last_got.at[at], recv_n.at[1, place])
+    for copy in sent:
+        if not any(copy is gone for gone in leaving):
+            copy.wait_send()
+    for place in range(3):
+        rows = grads.at[2, block_rows(f_at), :]
+        pltpu.make_async_copy(rows, rows, send_m.at[2, 4 + place]).wait()
+
+
+def backward_kernel(forward, ada, kept, cot, count):
+    (
+        qkv_all,
+        one_all,
+        two_all,
+        projected,
+        attended,
+        hidden_all,
+        branch_all,
+        proj_dense,
+        hidden_rows,
+        mixed_rows,
+        mods,
+        bias,
+        signals,
+    ) = forward
+    n_dp, n_fs = lax.axis_size("dp"), lax.axis_size("fsdp")
+    n_all = n_dp * n_fs
+    slots, features = kept.shape
+    row_width = features // n_dp
+    unit = features // n_fs
+    ada_width = 6 * features // n_fs
+    cols = projected.shape[2]
+    low, full = jnp.bfloat16, jnp.float32
+    vmem = pl.BlockSpec(memory_space=pltpu.VMEM)
+    image = (slots, features)
+    shapes = [
+        (image, low),
+        (image, full),
+        ((2, n_dp, unit, row_width), low),
+        ((unit, features), full),
+        ((row_width, ada_width), full),
+        ((n_all, 24, 128), full),
+    ]
+    scratch = [
+        ((n_dp,) + image, low),
+        ((n_dp,) + image, low),
+        ((n_dp,) + image, low),
+        ((2, 2) + image, low),
+        ((2,) + image, low),
+        ((2,) + image, low),
+        ((3, features, features), low),
+        ((3, 4, unit, features), low),
+        ((3, 3, unit, features), low),
+        ((2, n_dp, slots, row_width), low),
+        ((n_dp,) + image, low),
+        (image, low),
+        ((n_dp, n_fs, slots, cols), low),
+        ((2,) + qkv_all.shape[1:], low),
+        ((2, n_dp, unit, row_width), low),
+        ((8, features), full),
+        ((n_fs, 8, 128), full),
+        ((n_fs, 8, 128), full),
+        ((n_fs, 8, 128), full),
+        ((n_all, 8, 128), full),
+        ((n_all, 24, 128), full),
+    ]
+    dma = pltpu.SemaphoreType.DMA
+    sems = [(3, 7), (2, 3), (4,), (2 + n_fs, 4), (2, n_all - 1), (n_fs,), (2, 4)]
+    return pl.pallas_call(
+        functools.partial(backward_body, (HEADS, features // HEADS, ada_width)),
+        out_shape=[jax.ShapeDtypeStruct(shape, kind) for shape, kind in shapes],
+        in_specs=[pl.BlockSpec(memory_space=pl.ANY)]
+        + [vmem] * 15
+        + [pl.BlockSpec(memory_space=pltpu.SMEM)],
+        out_specs=[vmem] * len(shapes),
+        scratch_shapes=[pltpu.VMEM(shape, kind) for shape, kind in scratch]
+        + [dma(shape) for shape in sems for side in range(2)]
+        + [dma((4,))],
+        compiler_params=pltpu.CompilerParams(
+            collective_id=6, has_side_effects=True, vmem_limit_bytes=64 * 1024 * 1024 - 65536
+        ),
+        name="backward",
+    )(
+        qkv_all,
+        ada,
+        signals,
+        proj_dense,
+        one_all,
+        two_all,
+        projected,
+        attended,
+        hidden_all,
+        branch_all,
+        hidden_rows,
+        mixed_rows,
+        kept,
+        mods,
+        bias,
+        cot,
+        count,
+    )
+
+
+def shards(
+    patches_in,
+    condition,
+    keep_count,
+    keep_index,
+    w_ada,
+    b_ada,
+    w_qkv,
+    qv_bias,
+    w_proj,
+    w_fc1,
+    fc1_bias,
+    w_fc2,
+    out_bias,
+    cotangent,
+):
+    n_dp, n_fs = lax.axis_size("dp"), lax.axis_size("fsdp")
+    n_all = n_dp * n_fs
+    d_at, f_at = lax.axis_index("dp"), lax.axis_index("fsdp")
+    features = patches_in.shape[2]
+    row_width = features // n_dp
+    half_rows = row_width // 2
+    low = jnp.bfloat16
+    full = jnp.float32
+
+    unit_width = w_fc1.shape[1] // n_dp
+    one_pieces = w_fc1.reshape(row_width, n_dp, unit_width).transpose(1, 2, 0)
+    two_pieces = (
+        w_fc2.reshape(n_fs // n_dp, n_dp, unit_width, w_fc2.shape[1])
+        .transpose(1, 3, 0, 2)
+        .reshape(n_dp, w_fc2.shape[1], -1)
+    )
+    pieces = jnp.concatenate([one_pieces, two_pieces], axis=2)
+
+    def beside(shard):
+        return jnp.concatenate([shard[:half_rows], shard[half_rows:]], axis=1)
+
+    cond_float = condition.astype(full)
+    signal = swish(cond_float).astype(low).astype(full)
+    shards_bias = [b_ada, qv_bias, fc1_bias, out_bias]
+    biases = jnp.concatenate(shards_bias).astype(full)
+    notes = jnp.concatenate(
+        [
+            jnp.pad(signal.reshape(n_dp, row_width), ((0, 0), (0, 384 - row_width))),
+            jnp.broadcast_to(jnp.pad(biases, (0, 640 - biases.shape[0])), (n_dp, 640)),
+        ],
+        axis=1,
+    ).reshape(n_dp, 8, 128)
+    ada_width = w_ada.shape[1]
+    ada = jnp.pad(w_ada, ((0, 384 - row_width), (0, 896 - ada_width)))
+
+    indices = keep_index[0]
+    inputs = patches_in[0]
+    kept_in = jnp.take(inputs, indices, axis=0).astype(full)
+    forward = forward_kernel(
+        notes,
+        ada,
+        pieces,
+        beside(w_qkv),
+        beside(w_proj),
+        kept_in,
+        cotangent[0],
+        keep_count,
+        (ada_width, qv_bias.shape[0], fc1_bias.shape[0], out_bias.shape[0]),
+    )
+    block_out, d_kept, mlp_out, att_out, grad_ada, last = backward_kernel(
+        forward, ada, kept_in, cotangent[0], keep_count
+    )
+    grad_patches = jnp.zeros(inputs.shape, full).at[indices].set(d_kept, unique_indices=True)[None]
+
+    qkv_cols, proj_cols = w_qkv.shape[1], w_proj.shape[1]
+
+    def above(left, width):
+        return jnp.concatenate(
+            [att_out[:, left : left + width], att_out[:, left + width : left + 2 * width]], axis=0
+        )
+
+    one_out = mlp_out[0].reshape(-1, row_width).T.astype(full)
+    two_out = (
+        mlp_out[1]
+        .reshape(n_dp, w_fc2.shape[1], n_fs // n_dp, unit_width)
+        .transpose(2, 0, 3, 1)
+        .reshape(w_fc2.shape)
+        .astype(full)
+    )
+
+    last = last.reshape(n_dp, n_fs, 3, -1)
+    d_signal = jnp.sum(last[:, :, 0, :row_width], axis=1).reshape(1, features)
+    unused, swish_pull = jax.vjp(swish, cond_float)
+    grad_condition = swish_pull(d_signal)[0]
+    own = d_at * n_fs + f_at
+    head_size = qv_bias.shape[0]
+    heads_per = qkv_cols // head_size
+
+    def line_of(kind, d, f):
+        start = (d, f, kind, 0)
+        return lax.dynamic_slice(last, start, (1, 1, 1, last.shape[3])).reshape(-1)
+
+    def summed(f):
+        start = (0, f, 1, 0)
+        return jnp.sum(
+            lax.dynamic_slice(last, start, (n_dp, 1, 1, last.shape[3])).reshape(n_dp, -1), axis=0
+        )
+
+    ada_count = b_ada.shape[0]
+    ada_bias = lax.dynamic_slice_in_dim(
+        line_of(2, d_at, own // n_dp), (own % n_dp) * ada_count, ada_count
+    )
+    block = jnp.where(own < HEADS, own, own + HEADS)
+    qv_out = lax.dynamic_slice_in_dim(
+        summed(block // heads_per), (block % heads_per) * head_size, head_size
+    )
+    per = proj_cols // head_size
+    place = own % HEADS
+    start = jnp.where(own < HEADS, qkv_cols, qkv_cols + proj_cols) + (place % per) * head_size
+    out_out = lax.dynamic_slice_in_dim(summed(place // per), start, head_size)
+    bias_out = lax.dynamic_slice_in_dim(
+        line_of(1, own % n_dp, own // n_dp), qkv_cols + 2 * proj_cols, unit_width
+    )
+    return (
+        block_out[None],
+        grad_patches,
+        grad_condition,
+        grad_ada,
+        ada_bias,
+        above(0, qkv_cols),
+        qv_out,
+        above(2 * qkv_cols, proj_cols),
+        one_out,
+        bias_out,
+        two_out,
+        out_out,
+    )
+
+
+def kernels_fit(*arrays):
+    w_qkv, w_fc1 = arrays[6], arrays[9]
+    features = arrays[0].shape[2]
+    unit_width = w_fc1.shape[1] // lax.axis_size("dp")
+    return (
+        w_qkv.shape[1] % (features // HEADS) == 0
+        and w_qkv.shape[0] % 16 == 0
+        and unit_width % 16 == 0
+        and unit_width == arrays[11].shape[1]
+        and lax.axis_size("dp") == 4
+        and lax.axis_size("fsdp") == 8
+    )
+
+
 def solution(mesh):
+    both = ("dp", "fsdp")
+    weight = P("dp", "fsdp")
+    flat = P(both)
     placed = (
-        P(("dp", "fsdp"), None, None),
-        P(("dp", "fsdp"), None),
-        P(("dp", "fsdp")),
-        P(("dp", "fsdp"), None),
-        P("dp", "fsdp"),
-        P(("dp", "fsdp")),
-        P("dp", "fsdp"),
-        P(("dp", "fsdp")),
-        P("dp", "fsdp"),
-        P("dp", "fsdp"),
-        P(("dp", "fsdp")),
-        P("dp", "fsdp"),
-        P(("dp", "fsdp")),
-        P(("dp", "fsdp"), None, None),
-    )
+        P(both, None, None),
+        P(both, None),
+        flat,
+        P(both, None),
+        weight,
+        flat,
+        weight,
+        flat,
+        weight,
+        weight,
+        flat,
+        weight,
+        flat,
+        P(both, None, None),
+    )
+
+    def chosen(*arrays):
+        return (shards if kernels_fit(*arrays) else plain_shards)(*arrays)
+
     return jax.shard_map(
-        shards,
+        chosen,
         mesh=mesh,
         in_specs=placed,
         out_specs=(
-            P(("dp", "fsdp"), None, None),
-            P(("dp", "fsdp"), None, None),
-            P(("dp", "fsdp"), None),
-            P("dp", "fsdp"),
-            P(("dp", "fsdp")),
-            P("dp", "fsdp"),
-            P(("dp", "fsdp")),
-            P("dp", "fsdp"),
-            P("dp", "fsdp"),
-            P(("dp", "fsdp")),
-            P("dp", "fsdp"),
-            P(("dp", "fsdp")),
+            P(both, None, None),
+            P(both, None, None),
+            P(both, None),
+            weight,
+            flat,
+            weight,
+            flat,
+            weight,
+            weight,
+            flat,
+            weight,
+            flat,
         ),
         check_vma=False,
     )

time: 1300 us -> 375 us (0.29)
  the two profiles are of different devices: /device:TPU:0 before, /device:TPU:31 now
where the time goes in v3:
time: 375 us; the launch traced here: 370 us
  Pallas kernels  337 us (90%)
  local copies, waits for them, and re-layouts  23.6 us (6%)
  other arithmetic  7.25 us (2%)
    pallas_call x1, Pallas kernels, backward_kernel(): pl.pallas_call(functools.partial(backward_body, (HEADS, features // HEADS...  181 us
    pallas_call x1, Pallas kernels, forward_kernel(): pl.pallas_call(functools.partial(forward_body, (HEADS, size, widths)), ou...  156 us

profile of v3, /device:TPU:31, one launch (start us, length us, event | category | flops | bytes accessed | tf_op | source)
XLA Modules:
  0.0 370.2 jit_solution(6900800724264423609)
XLA Ops:
  0.6 0.7 compare_select_fusion
  1.9 2.6 gather_fusion
  4.5 1.0 select_convert_fusion.kept_ref
  5.6 0.8 pad_maximum_fusion.3.qkv_ref
  6.7 0.7 pad_maximum_fusion.4.proj_ref
  7.5 0.9 pad.22.ada_ref
  9.0 0.8 reshape.96
  10.9 1.1 pad_maximum_fusion.piece_ref
  12.9 155.8 %forward.1 = (bf16[8,576,864]{2,1,0:T(8,128)(2,1)}, bf16[1152,1152]{1,0:T(8,128)(2,1)}, bf16[1152,1152]{1,0:T(8,128)(2,1)}, bf16[8,192,432]{2,1,0:T(8,128)(2,1)}...) custom-call(f32[4,8,128]{2,1,0:T(8,128)} %bitcast.41, ...), custom_call_target="tpu_custom_call" | custom-call | tf_op jit(solution)/shard_map/forward/pallas_call | solution.py:805
  168.7 181.4 %backward.1 = (bf16[192,1152]{1,0:T(8,128)(2,1)}, f32[192,1152]{1,0:T(8,128)}, bf16[2,4,144,288]{3,2,1,0:T(8,128)(2,1)}, f32[144,1152]{1,0:T(8,128)}, f32[288,864]{1,0:T(8,128)}, /*index=5*/f32[32,24,128]{2,1,0:T(8,128)}) custom-call(bf16[8,576,864]{2,1,0:T(8,128)(2,1)} %get-tuple-element.31.qkv_hbm, bf16[384,896]{1,0:T(8,128)(2,1)} %pad.22.ada_ref, ...), custom_call_target="tpu_custom_call" | custom-call | tf_op jit(solution)/shard_map/backward/pallas_call | solution.py:1421
  350.1 1.2 reshape.98
  352.1 1.2 fusion.11
  353.3 0.8 copy.39
  354.9 0.9 pad_maximum_fusion.1
  355.8 1.0 reshape.102
  356.8 0.8 copy.38
  357.6 1.8 reshape.100
  359.6 1.2 copy.37
  360.7 1.4 constant_dynamic-slice_fusion.1
  362.1 1.3 constant_dynamic-slice_fusion
  363.5 2.9 scatter_custom_fusion
  366.4 1.0 slice_reduce_fusion
  368.1 0.8 copy.50
  368.8 1.0 copy.51
  (61 shorter events, 5.1 us)
Async XLA Ops:
  1.3 0.6 copy-start.12
  1.9 2.6 copy-start.13
  4.5 1.1 copy-start.8
  4.5 1.9 copy-start.9
  4.5 2.9 copy-start.4
  5.6 3.4 copy-start.7
  9.0 1.6 copy-start.6
  10.6 1.4 copy-start.10
  10.6 1.5 copy-start.14
  10.6 1.5 copy-start.15
  10.6 1.5 copy-start.16
  10.6 1.5 copy-start.17
  350.1 4.6 %copy-start = (f32[144,1152]{1,0:T(8,128)S(1)}, f32[144,1152]{1,0:T(8,128)}, u32[]{:S(2)}) copy-start(f32[144,1152]{1,0:T(8,128)} %get-tuple-element.48) | copy-start | bytes 1990660
  351.4 1.9 copy-start.3
  353.3 2.4 copy-start.2
  359.5 7.9 %copy-start.11 = (bf16[1,1152]{1,0:T(2,128)(2,1)S(1)}, bf16[1,1152]{1,0:T(2,128)(2,1)}, u32[]{:S(2)}) copy-start(bf16[1,1152]{1,0:T(2,128)(2,1)} %param.15) | copy-start | bytes 6916
  359.5 8.5 %copy-start.5 = (bf16[192,1152]{1,0:T(8,128)(2,1)S(1)}, bf16[192,1152]{1,0:T(8,128)(2,1)}, u32[]{:S(2)}) copy-start(bf16[192,1152]{1,0:T(8,128)(2,1)} %get-tuple-element.44) | copy-start | bytes 1327108
  360.7 8.1 %copy-start.1 = (f32[288,864]{1,0:T(8,128)S(1)}, f32[288,864]{1,0:T(8,128)}, u32[]{:S(2)}) copy-start(f32[288,864]{1,0:T(8,128)} %get-tuple-element.101) | copy-start | bytes 2985988

commit v4 on v3

--- a/solution.py
+++ b/solution.py
@@ -403,19 +403,26 @@
     kept_ref,
     cot_ref,
     count_ref,
-    qkv_all,
-    one_all,
-    two_all,
-    projected_ref,
+    qkv_hbm,
+    one_hbm,
+    two_hbm,
+    projected_hbm,
+    hidden_hbm,
+    branch_hbm,
+    proj_hbm,
     attended_ref,
-    hidden_all,
-    branch_all,
-    proj_dense,
     hidden_rows,
     mixed_rows,
     mod_ref,
     bias_ref,
     signal_ref,
+    qkv_all,
+    one_all,
+    two_all,
+    projected_ref,
+    hidden_all,
+    branch_all,
+    proj_dense,
     proj_all,
     mixed_ref,
     piece_got,
@@ -433,6 +440,7 @@
     send_e,
     recv_e,
     local,
+    out_sem,
 ):
     heads, size, widths = sizes
     n_dp, n_fs = 4, 8
@@ -451,6 +459,17 @@
     own_blocks = (qkv_ref, proj_ref, one_block, two_block)
     gathered = (qkv_all, proj_all, one_all, two_all)
     started = []
+    middle_copies = []
+    stores = []
+    z_at = f_at // 2
+    in_middle = (z_at == 1) | (z_at == 2)
+    second = jnp.where(in_middle, 6, 4)
+    third = 10 - second
+
+    def store(source, target):
+        copy = pltpu.make_async_copy(source, target, out_sem.at[len(stores)])
+        copy.start()
+        stores.append(copy)
 
     def slot(array, a, b):
         if array < 2:
@@ -464,32 +483,67 @@
         copy.start()
         started.append(copy)
 
+    def block(array, a, b):
+        own = isinstance(b, int) and a == 0 and b == 0
+        return own_blocks[array] if own else slot(array, a, b)
+
     def pass_on(array, a, b, axis, mask, sem):
         device = (d_at ^ mask, f_at) if axis == 0 else (d_at, f_at ^ mask)
         to_a, to_b = (a ^ mask, b) if axis == 0 else (a, b ^ mask)
-        source = own_blocks[array] if a == 0 and b == 0 else slot(array, a, b)
-        push(source, slot(array, a, b), sem, recv_w.at[array, to_a, to_b], device)
+        push(block(array, a, b), slot(array, a, b), sem, recv_w.at[array, to_a, to_b], device)
+
+    def relay_middle(array, b, mask, place):
+        copy = remote(
+            block(array, 0, b),
+            slot(array, 0, b),
+            send_z.at[array, place],
+            recv_w.at[array, 0, b ^ mask],
+            (d_at, f_at ^ mask),
+        )
+
+        @pl.when(in_middle)
+        def _():
+            copy.start()
+
+        middle_copies.append(copy)
 
     def arrive(array, a, b):
         place = slot(array, a, b)
         pltpu.make_async_copy(place, place, recv_w.at[array, a, b]).wait()
 
-    def wide(array):
-        for mask in (2, 4, 6):
-            pass_on(array, 0, 0, 1, mask, send_z.at[array, mask // 2 - 1])
-
-    def near(array, b):
-        pass_on(array, 0, b, 1, 1, send_y.at[array, b // 2])
-
-    def onward(array, a, b):
+    def near(array, b, place):
+        pass_on(array, 0, b, 1, 1, send_y.at[array, place])
+
+    def onward(array, a, b, place):
         if a == 0:
-            pass_on(array, a, b, 0, 2, send_x.at[array, 0, b])
-        if a in (0, 2):
-            pass_on(array, a, b, 0, 1, send_x.at[array, 1 + a // 2, b])
-
-    near(0, 0)
-    wide(0)
-    onward(0, 0, 0)
+            pass_on(array, a, b, 0, 2, send_x.at[array, 0, place])
+        pass_on(array, a, b, 0, 1, send_x.at[array, 1 + a // 2, place])
+
+    order = [0, 1, 2, second, 3, third, second ^ 1, third ^ 1]
+
+    def begin(array):
+        near(array, 0, 0)
+        if array < 2:
+            onward(array, 0, 0, 0)
+        pass_on(array, 0, 0, 1, 2, send_z.at[array, 0])
+        relay_middle(array, 0, 6, 1)
+
+    def follow(array, step):
+        arrive(array, 0, order[step])
+        if step == 2:
+            relay_middle(array, 2, 6, 2)
+            near(array, 2, 1)
+        if step == 3:
+            relay_middle(array, 6, 2, 3)
+            near(array, second, 2)
+        if step == 5:
+            relay_middle(array, 4, 2, 4)
+            near(array, third, 3)
+        if array < 2:
+            onward(array, 0, order[step], step)
+
+    begin(0)
+    begin(1)
     for place, (a, b) in enumerate(others):
         push(
             note_ref.at[d_at ^ a],
@@ -506,7 +560,10 @@
     ]
     for stay in stays:
         stay.start()
-    wide(1)
+    kept = kept_ref[...]
+    normed_one, _ = normed(kept)
+    follow(0, 1)
+    follow(0, 2)
     for mask in (1, 2, 3):
         push(
             piece_ref.at[d_at ^ mask],
@@ -515,9 +572,6 @@
             recv_e.at[2, mask],
             (d_at ^ mask, f_at),
         )
-
-    kept = kept_ref[...]
-    normed_one, _ = normed(kept)
 
     stays[0].wait()
     for place, (a, b) in enumerate(others):
@@ -557,11 +611,31 @@
     keep_row = pltpu.make_async_copy(row_put.at[own_at], row_got.at[own_at], local.at[0])
     keep_row.start()
 
-    arrive(0, 0, 1)
-    onward(0, 0, 1)
-    arrive(0, 0, 2)
-    near(0, 2)
-    onward(0, 0, 2)
+    follow(0, 3)
+    follow(1, 1)
+    follow(1, 2)
+    follow(0, 4)
+    follow(0, 5)
+
+    stays[3].wait()
+    for mask in (1, 2, 3):
+        place = piece_got.at[d_at ^ mask]
+        pltpu.make_async_copy(place, place, recv_e.at[2, mask]).wait()
+    one_block[...] = jnp.concatenate([piece_got[d, :, :row_width] for d in range(n_dp)], axis=1)
+    two_block[...] = jnp.concatenate([piece_got[d, :, row_width:] for d in range(n_dp)], axis=1)
+    follow(0, 6)
+    follow(0, 7)
+    follow(1, 3)
+    begin(2)
+    follow(1, 4)
+    follow(1, 5)
+    begin(3)
+    follow(1, 6)
+    follow(1, 7)
+    keep_one = pltpu.make_async_copy(one_block, slot(2, 0, 0), local.at[3])
+    keep_one.start()
+    keep_two = pltpu.make_async_copy(two_block, slot(3, 0, 0), local.at[4])
+    keep_two.start()
 
     qv_width, one_width, out_width = widths[1:]
     starts = [ada_piece, ada_piece + qv_width, ada_piece + qv_width + one_width]
@@ -591,12 +665,6 @@
         [bias_piece(f * n_dp + d_at, starts[1], one_width) for f in range(n_fs)], axis=1
     )
 
-    arrive(0, 0, 4)
-    near(0, 4)
-    onward(0, 0, 4)
-    arrive(0, 0, 3)
-    onward(0, 0, 3)
-
     keep_row.wait()
     for place, (a, b) in enumerate(others):
         at = (d_at ^ a) * n_fs + (f_at ^ b)
@@ -607,8 +675,8 @@
     sums = jnp.concatenate([sums[:, row, :] for row in range(7)], axis=1)
     pieces = []
     for index in range(6 * n_dp):
-        f, third = index // 3, index % 3
-        pieces.append(sums[f : f + 1, third * row_width : (third + 1) * row_width])
+        f, part = index // 3, index % 3
+        pieces.append(sums[f : f + 1, part * row_width : (part + 1) * row_width])
     mods = []
     for row in range(6):
         mods.append(jnp.concatenate(pieces[row * n_dp : (row + 1) * n_dp], axis=1))
@@ -622,47 +690,6 @@
         hidden_rows[d] = jnp.concatenate(chunks[2 * d : 2 * d + 2], axis=1)
     halves = [jnp.concatenate(chunks[part::2], axis=1) for part in range(2)]
 
-    stays[3].wait()
-    for mask in (1, 2, 3):
-        place = piece_got.at[d_at ^ mask]
-        pltpu.make_async_copy(place, place, recv_e.at[2, mask]).wait()
-    one_block[...] = jnp.concatenate([piece_got[d, :, :row_width] for d in range(n_dp)], axis=1)
-    two_block[...] = jnp.concatenate([piece_got[d, :, row_width:] for d in range(n_dp)], axis=1)
-
-    arrive(0, 0, 6)
-    near(0, 6)
-    onward(0, 0, 6)
-    near(1, 0)
-    arrive(0, 0, 5)
-    onward(0, 0, 5)
-    arrive(0, 0, 7)
-    onward(0, 0, 7)
-    onward(1, 0, 0)
-    arrive(1, 0, 1)
-    onward(1, 0, 1)
-    arrive(1, 0, 2)
-    near(1, 2)
-    onward(1, 0, 2)
-    wide(2)
-    wide(3)
-    keep_one = pltpu.make_async_copy(one_block, slot(2, 0, 0), local.at[0])
-    keep_one.start()
-    keep_two = pltpu.make_async_copy(two_block, slot(3, 0, 0), local.at[3])
-    keep_two.start()
-    arrive(1, 0, 4)
-    near(1, 4)
-    onward(1, 0, 4)
-    arrive(1, 0, 3)
-    onward(1, 0, 3)
-    arrive(1, 0, 6)
-    near(1, 6)
-    onward(1, 0, 6)
-    near(2, 0)
-    arrive(1, 0, 5)
-    onward(1, 0, 5)
-    arrive(1, 0, 7)
-    onward(1, 0, 7)
-
     def spread_step(buffer, kind, mask):
         for key in [0] if mask == 2 else [0, 2]:
             push(
@@ -678,30 +705,24 @@
             place = buffer.at[key]
             pltpu.make_async_copy(place, place, recv_e.at[kind, key]).wait()
 
+    store(branch_all.at[0], branch_hbm.at[0])
+    spread_step(branch_all, 0, 2)
+
     stays[1].wait()
-    order = [0, 1, 2, 4, 3, 6, 5, 7]
-    for place, b in enumerate(order):
+    for step, b in enumerate(order):
         arrive(0, 2, b)
-        onward(0, 2, b)
+        onward(0, 2, b, step)
         arrive(0, 1, b)
         arrive(0, 3, b)
         f = f_at ^ b
         out = jnp.dot(halves[0], qkv_all[f, :, :cols], preferred_element_type=full)
         out = out + jnp.dot(halves[1], qkv_all[f, :, cols:], preferred_element_type=full)
         projected_ref[f] = (out + bias_ref[pl.ds(f, 1), :cols]).astype(low)
-    spread_step(branch_all, 0, 2)
-
-    relays = []
-    for array in (2, 3):
-        for mask in (2, 4, 6):
-            relays.append((array, mask))
-
-    def relay():
-        array, mask = relays.pop(0)
-        arrive(array, 0, mask)
-        near(array, mask)
-        if (array, mask) == (2, 6):
-            near(3, 0)
+        store(qkv_all.at[f], qkv_hbm.at[f])
+        if step in (2, 3, 4, 6):
+            follow(2, {2: 1, 3: 2, 4: 3, 6: 5}[step])
+        if step in (3, 5):
+            follow(3, {3: 1, 5: 2}[step])
 
     allowed = lax.broadcasted_iota(jnp.int32, (slots, slots), 1) < count_ref[0]
     factor = 1.0 / math.sqrt(size)
@@ -723,15 +744,13 @@
         mixed_ref[:, start : start + size] = mix
         start = (pair % 2) * half_rows + side * size
         mixed_rows[pair // 2, :, start : start + size] = mix
-        if h in (3, 7, 11):
-            relay()
         if h == 8:
-            spread_wait(branch_all, 0, [2])
-            spread_step(branch_all, 0, 1)
-
-    for b in order:
+            follow(3, 3)
+
+    store(projected_ref, projected_hbm)
+    for step, b in enumerate(order):
         arrive(1, 2, b)
-        onward(1, 2, b)
+        onward(1, 2, b, step)
     stays[2].wait()
     for b in order:
         arrive(1, 1, b)
@@ -750,20 +769,36 @@
     normed_two, _ = normed(middle)
     hidden_all[0] = (normed_two * (1.0 + mods[4]) + mods[3]).astype(low)
     spread_step(hidden_all, 1, 2)
-    relay()
+    store(hidden_all.at[0], hidden_hbm.at[0])
+    store(proj_dense, proj_hbm)
+    follow(3, 5)
+    spread_wait(branch_all, 0, [2])
+    spread_step(branch_all, 0, 1)
     spread_wait(hidden_all, 1, [2])
     spread_step(hidden_all, 1, 1)
-    relay()
-    relay()
+    for step in (4, 6, 7):
+        arrive(2, 0, order[step])
+    keep_one.wait()
+    store(one_all, one_hbm)
+    spread_wait(branch_all, 0, [1, 3])
     spread_wait(hidden_all, 1, [1, 3])
-    spread_wait(branch_all, 0, [1, 3])
-    for array in (2, 3):
-        for b in (1, 3, 5, 7):
-            arrive(array, 0, b)
-    keep_one.wait()
+    for key in (1, 2, 3):
+        store(hidden_all.at[key], hidden_hbm.at[key])
+        store(branch_all.at[key], branch_hbm.at[key])
+    for step in (4, 6, 7):
+        arrive(3, 0, order[step])
     keep_two.wait()
+    store(two_all, two_hbm)
     for copy in started:
         copy.wait_send()
+
+    @pl.when(in_middle)
+    def _():
+        for copy in middle_copies:
+            copy.wait_send()
+
+    for copy in stores:
+        copy.wait()
 
 
 def forward_kernel(notes, ada, pieces, qkv, proj, kept, cot, count, widths):
@@ -776,24 +811,25 @@
     n_all = n_dp * n_fs
     low, full = jnp.bfloat16, jnp.float32
     vmem = pl.BlockSpec(memory_space=pltpu.VMEM)
+    image = (slots, features)
     shapes = [
         ((n_fs, n_dp * half_rows, 2 * cols), low),
         ((n_fs * unit, features), low),
         ((features, n_fs * unit), low),
         ((n_fs, slots, cols), low),
-        ((slots, features), full),
-        ((n_dp, slots, features), low),
-        ((n_dp, slots, features), low),
+        ((n_dp,) + image, low),
+        ((n_dp,) + image, low),
         ((features, features), low),
+        (image, full),
         ((n_dp, slots, 2 * half_rows), low),
         ((n_dp, slots, 2 * half_rows), low),
         ((8, features), full),
         ((16, features), full),
         ((n_all, 384), low),
     ]
-    scratch = [
+    scratch = shapes[:7] + [
         ((n_fs, n_dp * half_rows, proj.shape[1]), low),
-        ((slots, features), low),
+        (image, low),
         (pieces.shape, low),
         ((unit, features), low),
         ((unit, features), low),
@@ -806,10 +842,11 @@
         functools.partial(forward_body, (HEADS, size, widths)),
         out_shape=[jax.ShapeDtypeStruct(shape, kind) for shape, kind in shapes],
         in_specs=[vmem] * 7 + [pl.BlockSpec(memory_space=pltpu.SMEM)],
-        out_specs=[vmem] * len(shapes),
+        out_specs=[pl.BlockSpec(memory_space=pl.ANY)] * 7 + [vmem] * 6,
         scratch_shapes=[pltpu.VMEM(shape, kind) for shape, kind in scratch]
-        + [dma((2, n_all - 1)), dma((2, n_all - 1)), dma((4, 3)), dma((4, 4))]
-        + [dma((2, 3, n_fs)), dma((4, n_dp, n_fs)), dma((3, 4)), dma((3, 4)), dma((4,))],
+        + [dma((2, n_all - 1)), dma((2, n_all - 1)), dma((4, 5)), dma((4, 4))]
+        + [dma((2, 3, n_fs)), dma((4, n_dp, n_fs)), dma((3, 4)), dma((3, 4)), dma((5,))]
+        + [dma((24,))],
         compiler_params=pltpu.CompilerParams(
             collective_id=5, has_side_effects=True, vmem_limit_bytes=64 * 1024 * 1024 - 65536
         ),
@@ -844,15 +881,15 @@
 def backward_body(
     sizes,
     qkv_hbm,
+    one_hbm,
+    two_hbm,
+    projected_hbm,
+    hidden_hbm,
+    branch_hbm,
+    proj_hbm,
     ada_ref,
     signal_ref,
-    proj_ref,
-    one_ref,
-    two_ref,
-    projected_ref,
     attended_ref,
-    hidden_all,
-    branch_all,
     hidden_rows,
     mixed_rows,
     kept_ref,
@@ -866,6 +903,12 @@
     att_out,
     ada_out,
     last_got,
+    one_ref,
+    two_ref,
+    projected_ref,
+    hidden_all,
+    branch_all,
+    proj_ref,
     act_ref,
     d_raised_ref,
     part_ref,
@@ -902,6 +945,7 @@
     send_b,
     recv_b,
     local,
+    load_sem,
 ):
     heads, size, ada_width = sizes
     n_dp, n_fs = 4, 8
@@ -916,6 +960,21 @@
     low = jnp.bfloat16
     full = jnp.float32
     core, cross, near = (d_at ^ 1, f_at), (d_at ^ 2, f_at), (d_at, f_at ^ 1)
+    loads = [
+        pltpu.make_async_copy(source, target, load_sem.at[place])
+        for place, (source, target) in enumerate(
+            [
+                (hidden_hbm, hidden_all),
+                (one_hbm, one_ref),
+                (branch_hbm, branch_all),
+                (two_hbm, two_ref),
+                (proj_hbm, proj_ref),
+                (projected_hbm, projected_ref),
+            ]
+        )
+    ]
+    for load in loads:
+        load.start()
     others = [(a, b) for a in range(n_dp) for b in range(n_fs) if a or b]
     greet([(d_at ^ a, f_at ^ b) for a, b in others])
     sent = []
@@ -952,6 +1011,8 @@
         d_raised_ref[image] = (d_active * slope).astype(low)
         return carry
 
+    for load in loads[:4]:
+        load.wait()
     lax.fori_loop(0, n_dp, image_step, 0)
 
     def flat(ref, start, count):
@@ -993,13 +1054,14 @@
             (d_at, index),
         )
 
-    def fold_all(kind):
-        for place, wide in enumerate((2, 4, 6, 0)):
-            fold_block(kind, place, f_at ^ wide)
-            if wide:
-                copy = send_wide(kind, f_at ^ wide, wide)
-                copy.start()
-                sent.append(copy)
+    waves = (2, 4, 6, 0)
+
+    def fold_wave(kind, place):
+        fold_block(kind, place, f_at ^ waves[place])
+        if waves[place]:
+            copy = send_wide(kind, f_at ^ waves[place], waves[place])
+            copy.start()
+            sent.append(copy)
 
     def finish(kind):
         total = grads[kind, block_rows(f_at), :].astype(full)
@@ -1048,7 +1110,7 @@
     weight_grad(0, d_raised_ref, hidden_all)
     for place, wide in enumerate((2, 4, 6, 0)):
         send_block(0, place, f_at ^ wide ^ 1)
-    fold_all(1)
+    fold_wave(1, 0)
     one_sum = jnp.zeros((1, features), full)
     for image in range(n_dp):
         one_sum = one_sum + column_sums(d_raised_ref[image].astype(full))
@@ -1060,6 +1122,8 @@
     middle = kept + mods[2] * attended
     normed_two, rstd_two = normed(middle)
     upstream = cot_ref[...].astype(full)
+    fold_wave(1, 1)
+    loads[4].wait()
     arrive(cross_got.at[0], recv_d.at[0, 2])
     d_hidden_two = own_part + cross_got[0].astype(full)
     d_mod_ref[3:4, :] = column_sums(d_hidden_two)
@@ -1074,42 +1138,39 @@
     push(d_att_all.at[0], d_att_all.at[2], send_e.at[2], recv_e.at[2], cross)
     push(d_att_all.at[0], d_att_all.at[1], send_e.at[1], recv_e.at[1], core)
 
-    for copy in leaving:
-        copy.wait_send()
-    part_step(act_ref, two_ref, (1,))
-    core_send(1)
-    cross_send(1)
-
-    def pass_block(f):
+    fold_wave(1, 2)
+    loads[5].wait()
+
+    n_pairs = n_fs // 2
+
+    def pass_pair(place):
         push(
-            d_proj_all.at[0, f],
-            d_proj_all.at[2, f],
-            send_p.at[2 + f, 2],
-            recv_p.at[2 + f, 2],
+            d_proj_all.at[0, place],
+            d_proj_all.at[2, place],
+            send_p.at[2 + place, 2],
+            recv_p.at[2 + place, 2],
             cross,
         )
         push(
-            d_proj_all.at[0, f],
-            d_proj_all.at[1, f],
-            send_p.at[2 + f, 1],
-            recv_p.at[2 + f, 1],
+            d_proj_all.at[0, place],
+            d_proj_all.at[1, place],
+            send_p.at[2 + place, 1],
+            recv_p.at[2 + place, 1],
             core,
         )
 
-    def relay_block(f):
-        arrive(d_proj_all.at[2, f], recv_p.at[2 + f, 2])
+    def relay_pair(place):
+        arrive(d_proj_all.at[2, place], recv_p.at[2 + place, 2])
         push(
-            d_proj_all.at[2, f],
-            d_proj_all.at[3, f],
-            send_p.at[2 + f, 3],
-            recv_p.at[2 + f, 3],
+            d_proj_all.at[2, place],
+            d_proj_all.at[3, place],
+            send_p.at[2 + place, 3],
+            recv_p.at[2 + place, 3],
             core,
         )
 
     allowed = lax.broadcasted_iota(jnp.int32, (slots, slots), 1) < count_ref[0]
     factor = 1.0 / math.sqrt(size)
-    done_after = {5: [0], 7: [3], 9: [6], 11: [1], 13: [4], 15: [2, 5, 7]}
-    relay_after = {11: [0], 13: [3], 15: [6]}
     for h in range(heads):
         places = [
             ((kind * heads + h) // heads_per, (kind * heads + h) % heads_per)
@@ -1132,16 +1193,23 @@
             rows_rows(softmax.astype(low), d_mix),
         ]
         for (f, j), result in zip(places, results):
-            d_proj_all[0, f, :, j * size : (j + 1) * size] = result.astype(low)
-        for f in done_after.get(h, []):
-            pass_block(f)
-        for f in relay_after.get(h, []):
-            relay_block(f)
-        if h == 2:
-            fold_all(0)
-        if h == 6:
+            start = (f % 2) * cols + j * size
+            d_proj_all[0, f // 2, :, start : start + size] = result.astype(low)
+        if h == 11:
+            pass_pair(0)
+        if h == 8:
             arrive(d_att_all.at[2], recv_e.at[2])
             push(d_att_all.at[2], d_att_all.at[3], send_e.at[3], recv_e.at[3], core)
+    for place in range(1, n_pairs):
+        pass_pair(place)
+    fold_wave(1, 3)
+
+    for copy in leaving:
+        copy.wait_send()
+    part_step(act_ref, two_ref, (1,))
+    core_send(1)
+    cross_send(1)
+    fold_wave(0, 0)
 
     for stay in stays:
         stay.wait()
@@ -1162,54 +1230,42 @@
                 2 * cols + part * unit : 2 * cols + (part + 1) * unit,
             ] = grad_proj[part * half_rows : (part + 1) * half_rows, f * unit : (f + 1) * unit]
 
-    def qkv_grad(f):
+    odd = f_at % 2
+
+    def grad_pair(place):
+        for mask in (1, 3):
+            arrive(d_proj_all.at[mask, place], recv_p.at[2 + place, mask])
         result = rows_rows(
             rows_got[0].reshape(n_dp * slots, row_width),
-            d_proj_all[:, f].reshape(n_dp * slots, cols),
+            d_proj_all[:, place].reshape(n_dp * slots, 2 * cols),
         ).astype(low)
-        for part in range(2):
-            grads[2, block_rows(f), part * cols : (part + 1) * cols] = result[
-                part * half_rows : (part + 1) * half_rows, :
-            ]
-
-    odd = f_at % 2
-    pairs = [(0, 3), (6, 1), (4, 5), (2, 7)]
-
-    def grad_pair(place):
-        even_f, odd_f = pairs[place]
-        for f in (even_f, odd_f):
-            for mask in (1, 3):
-                arrive(d_proj_all.at[mask, f], recv_p.at[2 + f, mask])
-        goes = jnp.where(odd == 0, odd_f, even_f)
-        qkv_grad(goes)
-        send_block(2, place, goes)
-        qkv_grad(even_f + odd_f - goes)
+        for side in range(2):
+            start = (2 * place + side) * unit
+            for part in range(2):
+                grads[2, start : start + unit, part * cols : (part + 1) * cols] = result[
+                    part * half_rows : (part + 1) * half_rows, side * cols : (side + 1) * cols
+                ]
+        send_block(2, place, 2 * place + 1 - odd)
 
     def fold_pair(place):
-        even_f, odd_f = pairs[place]
-        index = jnp.where(odd == 0, even_f, odd_f)
+        index = 2 * place + odd
         fold_block(2, place, index)
 
         @pl.when(index != f_at)
         def _():
             send_wide(2, index, index ^ f_at).start()
 
-    grad_pair(0)
-    relay_block(1)
-    relay_block(4)
-    grad_pair(1)
-
-    loads = [
+    weights = [
         pltpu.make_async_copy(qkv_hbm.at[f], weight_ring.at[f % 2], local.at[2 + f % 2])
         for f in range(n_fs)
     ]
-    loads[0].start()
+    weights[0].start()
     halves = [jnp.zeros((slots, features // 2), full) for part in range(2)]
     for f in range(n_fs):
         if f + 1 < n_fs:
-            loads[f + 1].start()
-        loads[f].wait()
-        own = d_proj_all[0, f]
+            weights[f + 1].start()
+        weights[f].wait()
+        own = d_proj_all[0, f // 2, :, (f % 2) * cols : (f % 2 + 1) * cols]
         for part in range(2):
             halves[part] = halves[part] + contract(
                 own, weight_ring[f % 2, :, part * cols : (part + 1) * cols], (1,), (1,)
@@ -1225,10 +1281,12 @@
         )
         store_tile(sum_put, f, line)
         if f == 3:
-            relay_block(2)
-        if f == 6:
-            relay_block(5)
-    relay_block(7)
+            relay_pair(0)
+            fold_wave(0, 1)
+            grad_pair(0)
+    relay_pair(1)
+    fold_wave(0, 2)
+    grad_pair(1)
     d_hidden_one = jnp.concatenate(
         [
             halves[part][:, d * half_rows : (d + 1) * half_rows]
@@ -1240,6 +1298,14 @@
     normed_one, rstd_one = normed(kept)
     d_mod_ref[0:1, :] = column_sums(d_hidden_one)
     d_mod_ref[1:2, :] = column_sums(d_hidden_one * normed_one)
+
+    relay_pair(2)
+    fold_wave(0, 3)
+    grad_pair(2)
+    fold_pair(0)
+    relay_pair(3)
+    grad_pair(3)
+    fold_pair(1)
 
     arrive(cross_got.at[1], recv_d.at[1, 2])
     branch = (
@@ -1277,17 +1343,14 @@
     keep_note.start()
     keep_sum = pltpu.make_async_copy(sum_put.at[f_at], sum_got.at[0], local.at[1])
     keep_sum.start()
-    grad_pair(2)
-    fold_pair(0)
-    grad_pair(3)
-    fold_pair(1)
+    fold_pair(2)
     d_kept_ref[...] = d_kept_ref[...] + norm_back(
         d_hidden_one * (1.0 + mods[1]), normed_one, rstd_one
     )
     block_ref[...] = (middle + mods[5] * branch).astype(low)
 
     keep_mlp = []
-    for kind in range(2):
+    for kind in (1, 0):
         total = finish(kind).astype(low)
         for d in range(n_dp):
             mlp_put[kind, d] = total[:, d * row_width : (d + 1) * row_width]
@@ -1304,7 +1367,9 @@
                 mlp_put.at[kind, d_at], mlp_out.at[kind, d_at], local.at[2 + kind]
             )
         )
-        keep_mlp[kind].start()
+        keep_mlp[-1].start()
+
+    fold_pair(3)
 
     keep_note.wait()
     keep_sum.wait()
@@ -1329,7 +1394,6 @@
         last_put[:, 16 + row, :] = jnp.broadcast_to(
             totals[:, row * 128 : (row + 1) * 128], everyone
         )
-    fold_pair(2)
     for place, (a, b) in enumerate(others):
         push(
             last_put.at[(d_at ^ a) * n_fs + (f_at ^ b)],
@@ -1340,7 +1404,6 @@
         )
     keep_last = pltpu.make_async_copy(last_put.at[own_at], last_got.at[own_at], local.at[0])
     keep_last.start()
-    fold_pair(3)
     ada_out[...] = rows_rows(signal_ref[...], all_d)[: ada_out.shape[0], : ada_out.shape[1]]
     att_out[...] = finish(2)
     for kind in range(2):
@@ -1365,10 +1428,10 @@
         one_all,
         two_all,
         projected,
-        attended,
         hidden_all,
         branch_all,
         proj_dense,
+        attended,
         hidden_rows,
         mixed_rows,
         mods,
@@ -1384,6 +1447,7 @@
     cols = projected.shape[2]
     low, full = jnp.bfloat16, jnp.float32
     vmem = pl.BlockSpec(memory_space=pltpu.VMEM)
+    anywhere = pl.BlockSpec(memory_space=pl.ANY)
     image = (slots, features)
     shapes = [
         (image, low),
@@ -1394,6 +1458,12 @@
         ((n_all, 24, 128), full),
     ]
     scratch = [
+        (one_all.shape, low),
+        (two_all.shape, low),
+        (projected.shape, low),
+        ((n_dp,) + image, low),
+        ((n_dp,) + image, low),
+        (proj_dense.shape, low),
         ((n_dp,) + image, low),
         ((n_dp,) + image, low),
         ((n_dp,) + image, low),
@@ -1406,7 +1476,7 @@
         ((2, n_dp, slots, row_width), low),
         ((n_dp,) + image, low),
         (image, low),
-        ((n_dp, n_fs, slots, cols), low),
+        ((n_dp, n_fs // 2, slots, 2 * cols), low),
         ((2,) + qkv_all.shape[1:], low),
         ((2, n_dp, unit, row_width), low),
         ((8, features), full),
@@ -1417,32 +1487,32 @@
         ((n_all, 24, 128), full),
     ]
     dma = pltpu.SemaphoreType.DMA
-    sems = [(3, 7), (2, 3), (4,), (2 + n_fs, 4), (2, n_all - 1), (n_fs,), (2, 4)]
+    sems = [(3, 7), (2, 3), (4,), (2 + n_fs // 2, 4), (2, n_all - 1), (n_fs,), (2, 4)]
     return pl.pallas_call(
         functools.partial(backward_body, (HEADS, features // HEADS, ada_width)),
         out_shape=[jax.ShapeDtypeStruct(shape, kind) for shape, kind in shapes],
-        in_specs=[pl.BlockSpec(memory_space=pl.ANY)]
-        + [vmem] * 15
+        in_specs=[anywhere] * 7
+        + [vmem] * 9
         + [pl.BlockSpec(memory_space=pltpu.SMEM)],
         out_specs=[vmem] * len(shapes),
         scratch_shapes=[pltpu.VMEM(shape, kind) for shape, kind in scratch]
         + [dma(shape) for shape in sems for side in range(2)]
-        + [dma((4,))],
+        + [dma((4,)), dma((6,))],
         compiler_params=pltpu.CompilerParams(
             collective_id=6, has_side_effects=True, vmem_limit_bytes=64 * 1024 * 1024 - 65536
         ),
         name="backward",
     )(
         qkv_all,
-        ada,
-        signals,
-        proj_dense,
         one_all,
         two_all,
         projected,
-        attended,
         hidden_all,
         branch_all,
+        proj_dense,
+        ada,
+        signals,
+        attended,
         hidden_rows,
         mixed_rows,
         kept,

time: 375 us -> 297 us (0.79)
  the two profiles are of different devices: /device:TPU:31 before, /device:TPU:0 now
where the time goes in v4:
time: 297 us; the launch traced here: 292 us
  Pallas kernels  259 us (87%)
  local copies, waits for them, and re-layouts  23.6 us (8%)
  other arithmetic  7.25 us (2%)
    pallas_call x1, Pallas kernels, backward_kernel(): pl.pallas_call(functools.partial(backward_body, (HEADS, features // HEADS...  141 us
    pallas_call x1, Pallas kernels, forward_kernel(): pl.pallas_call(functools.partial(forward_body, (HEADS, size, widths)), ou...  118 us

profile of v4, /device:TPU:0, one launch (start us, length us, event | category | flops | bytes accessed | tf_op | source)
XLA Modules:
  0.0 291.7 jit_solution(4617356044469133849)
XLA Ops:
  0.6 0.7 compare_select_fusion
  1.9 2.6 gather_fusion
  4.5 1.0 select_convert_fusion.kept_ref
  5.6 0.8 pad_maximum_fusion.3.qkv_ref
  6.7 0.7 pad_maximum_fusion.4.proj_ref
  7.5 0.9 pad.22.ada_ref
  9.0 0.8 reshape.96
  10.9 1.1 pad_maximum_fusion.piece_ref
  12.9 117.5 %forward.1 = (bf16[8,576,864]{2,1,0:T(8,128)(2,1)}, bf16[1152,1152]{1,0:T(8,128)(2,1)}, bf16[1152,1152]{1,0:T(8,128)(2,1)}, bf16[8,192,432]{2,1,0:T(8,128)(2,1)}...) custom-call(f32[4,8,128]{2,1,0:T(8,128)} %bitcast.41, ...), custom_call_target="tpu_custom_call" | custom-call | tf_op jit(solution)/shard_map/forward/pallas_call | solution.py:841
  130.4 141.4 %backward.1 = (bf16[192,1152]{1,0:T(8,128)(2,1)}, f32[192,1152]{1,0:T(8,128)}, bf16[2,4,144,288]{3,2,1,0:T(8,128)(2,1)}, f32[144,1152]{1,0:T(8,128)}, f32[288,864]{1,0:T(8,128)}, /*index=5*/f32[32,24,128]{2,1,0:T(8,128)}) custom-call(bf16[8,576,864]{2,1,0:T(8,128)(2,1)} %get-tuple-element.31.qkv_hbm, bf16[1152,1152]{1,0:T(8,128)(2,1)} %get-tuple-element.32.one_hbm, ...), custom_call_target="tpu_custom_call" | custom-call | tf_op jit(solution)/shard_map/backward/pallas_call | solution.py:1491
  271.8 1.2 reshape.98
  273.8 1.2 fusion.11
  275.0 0.8 copy.39
  276.6 0.9 pad_maximum_fusion.1
  277.5 1.0 reshape.102
  278.5 0.8 copy.38
  279.3 1.8 reshape.100
  281.2 1.2 copy.37
  282.4 1.4 constant_dynamic-slice_fusion.1
  283.8 1.3 constant_dynamic-slice_fusion
  285.2 2.9 scatter_custom_fusion
  288.0 1.0 slice_reduce_fusion
  289.7 0.8 copy.50
  290.5 1.0 copy.51
  (61 shorter events, 5.1 us)
Async XLA Ops:
  1.3 0.6 copy-start.12
  1.9 2.6 copy-start.13
  4.5 1.1 copy-start.8
  4.5 1.9 copy-start.9
  4.5 2.9 %copy-start.4 = (bf16[288,864]{1,0:T(8,128)(2,1)S(1)}, bf16[288,864]{1,0:T(8,128)(2,1)}, u32[]{:S(2)}) copy-start(bf16[288,864]{1,0:T(8,128)(2,1)} %param.18) | copy-start | bytes 1492996
  5.6 3.4 %copy-start.7 = (bf16[1152,144]{0,1:T(8,128)(2,1)S(1)}, bf16[1152,144]{0,1:T(8,128)(2,1)}, u32[]{:S(2)}) copy-start(bf16[1152,144]{0,1:T(8,128)(2,1)} %param.25) | copy-start | bytes 995332
  9.0 1.6 copy-start.6
  10.6 1.4 copy-start.10
  10.6 1.5 copy-start.14
  10.6 1.5 copy-start.15
  10.6 1.5 copy-start.16
  10.6 1.5 copy-start.17
  271.8 4.6 %copy-start = (f32[144,1152]{1,0:T(8,128)S(1)}, f32[144,1152]{1,0:T(8,128)}, u32[]{:S(2)}) copy-start(f32[144,1152]{1,0:T(8,128)} %get-tuple-element.48) | copy-start | bytes 1990660
  273.0 1.9 copy-start.3
  275.0 2.4 copy-start.2
  281.2 7.9 %copy-start.11 = (bf16[1,1152]{1,0:T(2,128)(2,1)S(1)}, bf16[1,1152]{1,0:T(2,128)(2,1)}, u32[]{:S(2)}) copy-start(bf16[1,1152]{1,0:T(2,128)(2,1)} %param.15) | copy-start | bytes 6916
  281.2 8.5 %copy-start.5 = (bf16[192,1152]{1,0:T(8,128)(2,1)S(1)}, bf16[192,1152]{1,0:T(8,128)(2,1)}, u32[]{:S(2)}) copy-start(bf16[192,1152]{1,0:T(8,128)(2,1)} %get-tuple-element.44) | copy-start | bytes 1327108
  282.4 8.1 %copy-start.1 = (f32[288,864]{1,0:T(8,128)S(1)}, f32[288,864]{1,0:T(8,128)}, u32[]{:S(2)}) copy-start(f32[288,864]{1,0:T(8,128)} %get-tuple-element.101) | copy-start | bytes 2985988

commit v5 on v4

--- a/solution.py
+++ b/solution.py
@@ -397,10 +397,12 @@
     sizes,
     note_ref,
     ada_ref,
-    piece_ref,
-    qkv_ref,
-    proj_ref,
-    kept_ref,
+    one_raw,
+    two_raw,
+    qkv_raw,
+    proj_raw,
+    patch_ref,
+    index_ref,
     cot_ref,
     count_ref,
     qkv_hbm,
@@ -416,6 +418,7 @@
     mod_ref,
     bias_ref,
     signal_ref,
+    kept_ref,
     qkv_all,
     one_all,
     two_all,
@@ -431,6 +434,9 @@
     note_got,
     row_put,
     row_got,
+    qkv_ref,
+    proj_ref,
+    piece_ref,
     send_n,
     recv_n,
     send_z,
@@ -454,7 +460,16 @@
     low = jnp.bfloat16
     full = jnp.float32
     others = [(a, b) for a in range(n_dp) for b in range(n_fs) if a or b]
-    greet([(d_at ^ a, f_at ^ b) for a, b in others])
+    barrier = pltpu.get_barrier_semaphore()
+    for a, b in others:
+        pl.semaphore_signal(
+            barrier, 1, device_id=(d_at ^ a, f_at ^ b), device_id_type=MESH
+        )
+    for part in range(2):
+        rows = slice(part * half_rows, (part + 1) * half_rows)
+        qkv_ref[:, part * cols : (part + 1) * cols] = qkv_raw[rows, :]
+        proj_ref[:, part * width : (part + 1) * width] = proj_raw[:, rows].T
+    pl.semaphore_wait(barrier, len(others))
 
     own_blocks = (qkv_ref, proj_ref, one_block, two_block)
     gathered = (qkv_all, proj_all, one_all, two_all)
@@ -552,6 +567,13 @@
             recv_n.at[0, place],
             (d_at ^ a, f_at ^ b),
         )
+    for d in range(n_dp):
+        piece_ref[d, :, :row_width] = one_raw[:, d * unit : (d + 1) * unit].T
+        for e in range(2):
+            start = (e * n_dp + d) * unit
+            piece_ref[d, :, row_width + e * unit : row_width + (e + 1) * unit] = two_raw[
+                :, start : start + unit
+            ]
     stays = [
         pltpu.make_async_copy(note_ref.at[d_at], note_got.at[own_at], local.at[0]),
         pltpu.make_async_copy(qkv_ref, slot(0, 0, 0), local.at[1]),
@@ -560,6 +582,10 @@
     ]
     for stay in stays:
         stay.start()
+    chosen = lax.broadcasted_iota(jnp.int32, (slots, patch_ref.shape[0]), 1) == index_ref[...]
+    kept_ref[...] = jnp.dot(
+        chosen.astype(full).astype(low), patch_ref[...], preferred_element_type=full
+    )
     kept = kept_ref[...]
     normed_one, _ = normed(kept)
     follow(0, 1)
@@ -579,6 +605,7 @@
         pltpu.make_async_copy(note_got.at[at], note_got.at[at], recv_n.at[0, place]).wait()
     notes = note_got[...]
     signals = jnp.concatenate([notes[:, row, :] for row in range(3)], axis=1).astype(low)
+    signals = signals[:, :row_width]
     signal_ref[...] = signals
     terms = jnp.dot(signals, ada_ref[...], preferred_element_type=full)
     ada_width = widths[0]
@@ -594,12 +621,14 @@
     )
     first = (d_at == 0).astype(full)
     for row in range(7):
-        piece = terms[:, row * 128 : (row + 1) * 128]
         count = min(128, ada_width - row * 128)
-        add = block_bias[:, row * 128 : row * 128 + count] * first
+        span = slice(row * 128, row * 128 + count)
+        piece = terms[:, span] + block_bias[:, span] * first
         if count < 128:
-            add = jnp.concatenate([add, jnp.zeros((1, 128 - count), full)], axis=1)
-        row_put[:, row, :] = piece + add
+            piece = jnp.concatenate(
+                [piece, jnp.zeros((piece.shape[0], 128 - count), full)], axis=1
+            )
+        row_put[:, row, :] = piece
     for place, (a, b) in enumerate(others):
         push(
             row_put.at[(d_at ^ a) * n_fs + (f_at ^ b)],
@@ -801,13 +830,14 @@
         copy.wait()
 
 
-def forward_kernel(notes, ada, pieces, qkv, proj, kept, cot, count, widths):
+def forward_kernel(notes, ada, one, two, qkv, proj, patches, index, cot, count, widths):
     n_dp, n_fs = lax.axis_size("dp"), lax.axis_size("fsdp")
-    slots, features = kept.shape
-    unit = pieces.shape[1]
+    slots, features = cot.shape
+    unit = features // n_fs
     size = features // HEADS
-    half_rows = qkv.shape[0]
-    cols = qkv.shape[1] // 2
+    half_rows = qkv.shape[0] // 2
+    cols = qkv.shape[1]
+    pieces = (n_dp, unit, 4 * half_rows)
     n_all = n_dp * n_fs
     low, full = jnp.bfloat16, jnp.float32
     vmem = pl.BlockSpec(memory_space=pltpu.VMEM)
@@ -825,24 +855,28 @@
         ((n_dp, slots, 2 * half_rows), low),
         ((8, features), full),
         ((16, features), full),
-        ((n_all, 384), low),
+        ((n_all, 2 * half_rows), low),
+        (image, full),
     ]
     scratch = shapes[:7] + [
-        ((n_fs, n_dp * half_rows, proj.shape[1]), low),
+        ((n_fs, n_dp * half_rows, 2 * unit), low),
         (image, low),
-        (pieces.shape, low),
+        (pieces, low),
         ((unit, features), low),
         ((unit, features), low),
         ((n_all, 8, 128), full),
         ((n_all, 8, 128), full),
         ((n_all, 8, 128), full),
+        ((half_rows, 2 * cols), low),
+        ((half_rows, 2 * unit), low),
+        (pieces, low),
     ]
     dma = pltpu.SemaphoreType.DMA
     return pl.pallas_call(
         functools.partial(forward_body, (HEADS, size, widths)),
         out_shape=[jax.ShapeDtypeStruct(shape, kind) for shape, kind in shapes],
-        in_specs=[vmem] * 7 + [pl.BlockSpec(memory_space=pltpu.SMEM)],
-        out_specs=[pl.BlockSpec(memory_space=pl.ANY)] * 7 + [vmem] * 6,
+        in_specs=[vmem] * 9 + [pl.BlockSpec(memory_space=pltpu.SMEM)],
+        out_specs=[pl.BlockSpec(memory_space=pl.ANY)] * 7 + [vmem] * 7,
         scratch_shapes=[pltpu.VMEM(shape, kind) for shape, kind in scratch]
         + [dma((2, n_all - 1)), dma((2, n_all - 1)), dma((4, 5)), dma((4, 4))]
         + [dma((2, 3, n_fs)), dma((4, n_dp, n_fs)), dma((3, 4)), dma((3, 4)), dma((5,))]
@@ -851,7 +885,7 @@
             collective_id=5, has_side_effects=True, vmem_limit_bytes=64 * 1024 * 1024 - 65536
         ),
         name="forward",
-    )(notes, ada, pieces, qkv, proj, kept, cot, count)
+    )(notes, ada, one, two, qkv, proj, patches, index, cot, count)
 
 
 def gelu_parts(raised):
@@ -887,22 +921,26 @@
     hidden_hbm,
     branch_hbm,
     proj_hbm,
+    hidden_rows,
+    mixed_rows,
     ada_ref,
     signal_ref,
     attended_ref,
-    hidden_rows,
-    mixed_rows,
     kept_ref,
     mod_ref,
     bias_ref,
+    index_ref,
     cot_ref,
     count_ref,
     block_ref,
-    d_kept_ref,
-    mlp_out,
-    att_out,
+    patch_out,
+    qkv_out,
+    proj_out,
+    one_out,
+    two_out,
     ada_out,
     last_got,
+    mlp_out,
     one_ref,
     two_ref,
     projected_ref,
@@ -1110,6 +1148,11 @@
     weight_grad(0, d_raised_ref, hidden_all)
     for place, wide in enumerate((2, 4, 6, 0)):
         send_block(0, place, f_at ^ wide ^ 1)
+    for copy in leaving:
+        copy.wait_send()
+    part_step(act_ref, two_ref, (1,))
+    core_send(1)
+    cross_send(1)
     fold_wave(1, 0)
     one_sum = jnp.zeros((1, features), full)
     for image in range(n_dp):
@@ -1132,7 +1175,7 @@
     d_mod_ref[2:3, :] = column_sums(d_middle * attended)
     d_attended = (mods[2] * d_middle).astype(low)
     d_att_all[0] = d_attended
-    d_kept_ref[...] = d_middle
+    patch_out[:slots, :] = d_middle
     att_sum = column_sums(d_attended.astype(full))
     d_mixed_ref[...] = contract(d_attended, proj_ref[...], (1,), (1,)).astype(low)
     push(d_att_all.at[0], d_att_all.at[2], send_e.at[2], recv_e.at[2], cross)
@@ -1141,29 +1184,30 @@
     fold_wave(1, 2)
     loads[5].wait()
 
-    n_pairs = n_fs // 2
+    leaps = (3, 2, 1, 0)
+    turn = [(f_at // 2) ^ leap for leap in leaps]
 
     def pass_pair(place):
         push(
-            d_proj_all.at[0, place],
-            d_proj_all.at[2, place],
+            d_proj_all.at[0, turn[place]],
+            d_proj_all.at[2, turn[place]],
             send_p.at[2 + place, 2],
             recv_p.at[2 + place, 2],
             cross,
         )
         push(
-            d_proj_all.at[0, place],
-            d_proj_all.at[1, place],
+            d_proj_all.at[0, turn[place]],
+            d_proj_all.at[1, turn[place]],
             send_p.at[2 + place, 1],
             recv_p.at[2 + place, 1],
             core,
         )
 
     def relay_pair(place):
-        arrive(d_proj_all.at[2, place], recv_p.at[2 + place, 2])
+        arrive(d_proj_all.at[2, turn[place]], recv_p.at[2 + place, 2])
         push(
-            d_proj_all.at[2, place],
-            d_proj_all.at[3, place],
+            d_proj_all.at[2, turn[place]],
+            d_proj_all.at[3, turn[place]],
             send_p.at[2 + place, 3],
             recv_p.at[2 + place, 3],
             core,
@@ -1195,22 +1239,131 @@
         for (f, j), result in zip(places, results):
             start = (f % 2) * cols + j * size
             d_proj_all[0, f // 2, :, start : start + size] = result.astype(low)
-        if h == 11:
-            pass_pair(0)
-        if h == 8:
-            arrive(d_att_all.at[2], recv_e.at[2])
-            push(d_att_all.at[2], d_att_all.at[3], send_e.at[3], recv_e.at[3], core)
-    for place in range(1, n_pairs):
+    for place in range(4):
         pass_pair(place)
     fold_wave(1, 3)
 
-    for copy in leaving:
-        copy.wait_send()
-    part_step(act_ref, two_ref, (1,))
-    core_send(1)
-    cross_send(1)
+
+    odd = f_at % 2
+
+    def grad_pair(place):
+        for mask in (1, 3):
+            arrive(d_proj_all.at[mask, turn[place]], recv_p.at[2 + place, mask])
+        result = rows_rows(
+            rows_got[0].reshape(n_dp * slots, row_width),
+            d_proj_all[:, turn[place]].reshape(n_dp * slots, 2 * cols),
+        ).astype(low)
+        for side in range(2):
+            rows = block_rows(2 * turn[place] + side)
+            for part in range(2):
+                grads[2, rows, part * cols : (part + 1) * cols] = result[
+                    part * half_rows : (part + 1) * half_rows, side * cols : (side + 1) * cols
+                ]
+        send_block(2, place, 2 * turn[place] + 1 - odd)
+
+    def fold_pair(place):
+        fold_block(2, place, 2 * turn[place] + odd)
+        if leaps[place]:
+            copy = send_wide(2, 2 * turn[place] + odd, 2 * leaps[place])
+            copy.start()
+            sent.append(copy)
+
+    arrive(cross_got.at[1], recv_d.at[1, 2])
+    branch = (
+        part_ref[0].astype(full)
+        + core_got[1, 1].astype(full)
+        + cross_got[1].astype(full)
+        + bias_ref[9:10, :]
+    )
+    d_mod_ref[5:6, :] = column_sums(upstream * branch)
+
+    tall = weight_ring.shape[1]
+    weights = [
+        pltpu.make_async_copy(
+            qkv_hbm.at[place // 2, pl.ds((place % 2) * tall, tall), :],
+            weight_ring.at[place % 2],
+            local.at[2 + place % 2],
+        )
+        for place in range(2 * n_fs)
+    ]
+    weights[0].start()
+    quarters = [[jnp.zeros((slots, tall), full) for side in range(2)] for part in range(2)]
+    for f in range(n_fs):
+        own = d_proj_all[0, f // 2, :, (f % 2) * cols : (f % 2 + 1) * cols]
+        for side in range(2):
+            place = 2 * f + side
+            if place + 1 < 2 * n_fs:
+                weights[place + 1].start()
+            weights[place].wait()
+            for part in range(2):
+                quarters[part][side] = quarters[part][side] + contract(
+                    own, weight_ring[side, :, part * cols : (part + 1) * cols], (1,), (1,)
+                )
+        line = jnp.concatenate(
+            [
+                column_sums(own.astype(full)),
+                att_sum[:, f * unit : (f + 1) * unit],
+                branch_sum[:, f * unit : (f + 1) * unit],
+                one_sum[:, f * unit : (f + 1) * unit],
+            ],
+            axis=1,
+        )
+        store_tile(sum_put, f, line)
+    d_hidden_one = jnp.concatenate(
+        [
+            quarters[part][d // 2][:, (d % 2) * half_rows : (d % 2 + 1) * half_rows]
+            for d in range(n_dp)
+            for part in range(2)
+        ],
+        axis=1,
+    )
+    normed_one, rstd_one = normed(kept)
+    d_mod_ref[0:1, :] = column_sums(d_hidden_one)
+    d_mod_ref[1:2, :] = column_sums(d_hidden_one * normed_one)
+
+    third = ada_width // 3
+    pieces = []
+    for row in range(6):
+        line = d_mod_ref[row : row + 1, :].astype(low).astype(full)
+        pieces += [line[:, step * third : (step + 1) * third] for step in range(n_dp)]
+    for f in range(n_fs):
+        store_tile(note_put, f, jnp.concatenate(pieces[3 * f : 3 * f + 3], axis=1))
+    for mask in range(1, n_fs):
+        push(
+            sum_put.at[f_at ^ mask],
+            sum_got.at[mask],
+            send_s.at[mask],
+            recv_s.at[mask],
+            (d_at, f_at ^ mask),
+        )
+    for place, (a, b) in enumerate(others):
+        push(
+            note_put.at[f_at ^ b],
+            note_got.at[own_at],
+            send_n.at[0, place],
+            recv_n.at[0, place],
+            (d_at ^ a, f_at ^ b),
+        )
+    keep_note = pltpu.make_async_copy(note_put.at[f_at], note_got.at[own_at], local.at[4])
+    keep_note.start()
+    keep_sum = pltpu.make_async_copy(sum_put.at[f_at], sum_got.at[0], local.at[5])
+    keep_sum.start()
+    arrive(d_att_all.at[2], recv_e.at[2])
+    push(d_att_all.at[2], d_att_all.at[3], send_e.at[3], recv_e.at[3], core)
+    d_kept = patch_out[:slots, :] + norm_back(
+        d_hidden_one * (1.0 + mods[1]), normed_one, rstd_one
+    )
+    chosen = lax.broadcasted_iota(jnp.int32, (slots, patch_out.shape[0]), 1) == index_ref[...]
+    chosen = chosen.astype(full).astype(low)
+    left = d_kept
+    spread_out = jnp.zeros(patch_out.shape, full)
+    for step in range(3):
+        part = left.astype(low)
+        spread_out = spread_out + rows_rows(chosen, part)
+        left = left - part.astype(full)
+    patch_out[...] = spread_out
+    block_ref[...] = (middle + mods[5] * branch).astype(low)
     fold_wave(0, 0)
-
     for stay in stays:
         stay.wait()
     for kind in range(2):
@@ -1230,127 +1383,21 @@
                 2 * cols + part * unit : 2 * cols + (part + 1) * unit,
             ] = grad_proj[part * half_rows : (part + 1) * half_rows, f * unit : (f + 1) * unit]
 
-    odd = f_at % 2
-
-    def grad_pair(place):
-        for mask in (1, 3):
-            arrive(d_proj_all.at[mask, place], recv_p.at[2 + place, mask])
-        result = rows_rows(
-            rows_got[0].reshape(n_dp * slots, row_width),
-            d_proj_all[:, place].reshape(n_dp * slots, 2 * cols),
-        ).astype(low)
-        for side in range(2):
-            start = (2 * place + side) * unit
-            for part in range(2):
-                grads[2, start : start + unit, part * cols : (part + 1) * cols] = result[
-                    part * half_rows : (part + 1) * half_rows, side * cols : (side + 1) * cols
-                ]
-        send_block(2, place, 2 * place + 1 - odd)
-
-    def fold_pair(place):
-        index = 2 * place + odd
-        fold_block(2, place, index)
-
-        @pl.when(index != f_at)
-        def _():
-            send_wide(2, index, index ^ f_at).start()
-
-    weights = [
-        pltpu.make_async_copy(qkv_hbm.at[f], weight_ring.at[f % 2], local.at[2 + f % 2])
-        for f in range(n_fs)
-    ]
-    weights[0].start()
-    halves = [jnp.zeros((slots, features // 2), full) for part in range(2)]
-    for f in range(n_fs):
-        if f + 1 < n_fs:
-            weights[f + 1].start()
-        weights[f].wait()
-        own = d_proj_all[0, f // 2, :, (f % 2) * cols : (f % 2 + 1) * cols]
-        for part in range(2):
-            halves[part] = halves[part] + contract(
-                own, weight_ring[f % 2, :, part * cols : (part + 1) * cols], (1,), (1,)
-            )
-        line = jnp.concatenate(
-            [
-                column_sums(own.astype(full)),
-                att_sum[:, f * unit : (f + 1) * unit],
-                branch_sum[:, f * unit : (f + 1) * unit],
-                one_sum[:, f * unit : (f + 1) * unit],
-            ],
-            axis=1,
-        )
-        store_tile(sum_put, f, line)
-        if f == 3:
-            relay_pair(0)
-            fold_wave(0, 1)
-            grad_pair(0)
+    relay_pair(0)
+    grad_pair(0)
+    fold_wave(0, 1)
+
     relay_pair(1)
+    grad_pair(1)
     fold_wave(0, 2)
-    grad_pair(1)
-    d_hidden_one = jnp.concatenate(
-        [
-            halves[part][:, d * half_rows : (d + 1) * half_rows]
-            for d in range(n_dp)
-            for part in range(2)
-        ],
-        axis=1,
-    )
-    normed_one, rstd_one = normed(kept)
-    d_mod_ref[0:1, :] = column_sums(d_hidden_one)
-    d_mod_ref[1:2, :] = column_sums(d_hidden_one * normed_one)
-
     relay_pair(2)
+    grad_pair(2)
     fold_wave(0, 3)
-    grad_pair(2)
     fold_pair(0)
-    relay_pair(3)
-    grad_pair(3)
-    fold_pair(1)
-
-    arrive(cross_got.at[1], recv_d.at[1, 2])
-    branch = (
-        part_ref[0].astype(full)
-        + core_got[1, 1].astype(full)
-        + cross_got[1].astype(full)
-        + bias_ref[9:10, :]
-    )
-    d_mod_ref[5:6, :] = column_sums(upstream * branch)
-
-    third = ada_width // 3
-    pieces = []
-    for row in range(6):
-        line = d_mod_ref[row : row + 1, :].astype(low).astype(full)
-        pieces += [line[:, step * third : (step + 1) * third] for step in range(n_dp)]
-    for f in range(n_fs):
-        store_tile(note_put, f, jnp.concatenate(pieces[3 * f : 3 * f + 3], axis=1))
-    for mask in range(1, n_fs):
-        push(
-            sum_put.at[f_at ^ mask],
-            sum_got.at[mask],
-            send_s.at[mask],
-            recv_s.at[mask],
-            (d_at, f_at ^ mask),
-        )
-    for place, (a, b) in enumerate(others):
-        push(
-            note_put.at[f_at ^ b],
-            note_got.at[own_at],
-            send_n.at[0, place],
-            recv_n.at[0, place],
-            (d_at ^ a, f_at ^ b),
-        )
-    keep_note = pltpu.make_async_copy(note_put.at[f_at], note_got.at[own_at], local.at[0])
-    keep_note.start()
-    keep_sum = pltpu.make_async_copy(sum_put.at[f_at], sum_got.at[0], local.at[1])
-    keep_sum.start()
-    fold_pair(2)
-    d_kept_ref[...] = d_kept_ref[...] + norm_back(
-        d_hidden_one * (1.0 + mods[1]), normed_one, rstd_one
-    )
-    block_ref[...] = (middle + mods[5] * branch).astype(low)
 
     keep_mlp = []
-    for kind in (1, 0):
+
+    def give_back(kind):
         total = finish(kind).astype(low)
         for d in range(n_dp):
             mlp_put[kind, d] = total[:, d * row_width : (d + 1) * row_width]
@@ -1369,8 +1416,8 @@
         )
         keep_mlp[-1].start()
 
-    fold_pair(3)
-
+    relay_pair(3)
+    grad_pair(3)
     keep_note.wait()
     keep_sum.wait()
     for mask in range(1, n_fs):
@@ -1385,15 +1432,17 @@
     all_d = jnp.concatenate([notes[:, row, :] for row in range(7)], axis=1)
     totals = column_sums(all_d)
     all_d = all_d.astype(low)
+    all_d = all_d[:, :ada_width]
     terms = contract(all_d, ada_ref[...], (1,), (1,))
-    for row in range(3):
-        last_put[:, row, :] = terms[:, row * 128 : (row + 1) * 128]
-    everyone = (n_dp * n_fs, 128)
-    for row in range(7):
-        last_put[:, 8 + row, :] = jnp.broadcast_to(sums[row : row + 1, :], everyone)
-        last_put[:, 16 + row, :] = jnp.broadcast_to(
-            totals[:, row * 128 : (row + 1) * 128], everyone
-        )
+    sum_line = jnp.concatenate([sums[row : row + 1, :] for row in range(7)], axis=1)
+    common = jnp.concatenate(
+        [sum_line[:, :ada_width], totals[:, :ada_width], jnp.zeros((1, 32), full)], axis=1
+    )
+    lines = jnp.concatenate(
+        [terms, jnp.broadcast_to(common, (n_dp * n_fs, common.shape[1]))], axis=1
+    )
+    for row in range(16):
+        last_put[:, row, :] = lines[:, row * 128 : (row + 1) * 128]
     for place, (a, b) in enumerate(others):
         push(
             last_put.at[(d_at ^ a) * n_fs + (f_at ^ b)],
@@ -1404,12 +1453,29 @@
         )
     keep_last = pltpu.make_async_copy(last_put.at[own_at], last_got.at[own_at], local.at[0])
     keep_last.start()
-    ada_out[...] = rows_rows(signal_ref[...], all_d)[: ada_out.shape[0], : ada_out.shape[1]]
-    att_out[...] = finish(2)
-    for kind in range(2):
-        keep_mlp[kind].wait()
+    fold_pair(1)
+    give_back(1)
+    fold_pair(2)
+    give_back(0)
+    ada_out[...] = rows_rows(signal_ref[...], all_d)
+    fold_pair(3)
+    for kind in (1, 0):
+        keep_mlp[1 - kind].wait()
         for mask in (1, 2, 3):
             arrive(mlp_out.at[kind, d_at ^ mask], recv_b.at[kind, mask])
+    for d in range(n_dp):
+        one_out[:, d * unit : (d + 1) * unit] = mlp_out[0, d].astype(full).T
+        for e in range(2):
+            start = (e * n_dp + d) * unit
+            two_out[:, start : start + unit] = mlp_out[1, d, :, e * unit : (e + 1) * unit].astype(
+                full
+            )
+    total = finish(2)
+    for part in range(2):
+        rows = slice(part * half_rows, (part + 1) * half_rows)
+        qkv_out[rows, :] = total[:, part * cols : (part + 1) * cols]
+        start = 2 * cols + part * unit
+        proj_out[:, rows] = total[:, start : start + unit].T
     keep_last.wait()
     for place, (a, b) in enumerate(others):
         at = (d_at ^ a) * n_fs + (f_at ^ b)
@@ -1417,12 +1483,9 @@
     for copy in sent:
         if not any(copy is gone for gone in leaving):
             copy.wait_send()
-    for place in range(3):
-        rows = grads.at[2, block_rows(f_at), :]
-        pltpu.make_async_copy(rows, rows, send_m.at[2, 4 + place]).wait()
-
-
-def backward_kernel(forward, ada, kept, cot, count):
+
+
+def backward_kernel(forward, ada, index, patches, cot, count):
     (
         qkv_all,
         one_all,
@@ -1437,6 +1500,7 @@
         mods,
         bias,
         signals,
+        kept,
     ) = forward
     n_dp, n_fs = lax.axis_size("dp"), lax.axis_size("fsdp")
     n_all = n_dp * n_fs
@@ -1451,13 +1515,16 @@
     image = (slots, features)
     shapes = [
         (image, low),
-        (image, full),
-        ((2, n_dp, unit, row_width), low),
+        (patches, full),
+        ((row_width, cols), full),
+        ((unit, row_width), full),
+        ((row_width, n_dp * unit), full),
         ((unit, features), full),
         ((row_width, ada_width), full),
-        ((n_all, 24, 128), full),
+        ((n_all, 16, 128), full),
     ]
     scratch = [
+        ((2, n_dp, unit, row_width), low),
         (one_all.shape, low),
         (two_all.shape, low),
         (projected.shape, low),
@@ -1477,27 +1544,27 @@
         ((n_dp,) + image, low),
         (image, low),
         ((n_dp, n_fs // 2, slots, 2 * cols), low),
-        ((2,) + qkv_all.shape[1:], low),
+        ((2, qkv_all.shape[1] // 2, qkv_all.shape[2]), low),
         ((2, n_dp, unit, row_width), low),
         ((8, features), full),
         ((n_fs, 8, 128), full),
         ((n_fs, 8, 128), full),
         ((n_fs, 8, 128), full),
         ((n_all, 8, 128), full),
-        ((n_all, 24, 128), full),
+        ((n_all, 16, 128), full),
     ]
     dma = pltpu.SemaphoreType.DMA
     sems = [(3, 7), (2, 3), (4,), (2 + n_fs // 2, 4), (2, n_all - 1), (n_fs,), (2, 4)]
     return pl.pallas_call(
         functools.partial(backward_body, (HEADS, features // HEADS, ada_width)),
         out_shape=[jax.ShapeDtypeStruct(shape, kind) for shape, kind in shapes],
-        in_specs=[anywhere] * 7
-        + [vmem] * 9
+        in_specs=[anywhere] * 9
+        + [vmem] * 8
         + [pl.BlockSpec(memory_space=pltpu.SMEM)],
         out_specs=[vmem] * len(shapes),
         scratch_shapes=[pltpu.VMEM(shape, kind) for shape, kind in scratch]
         + [dma(shape) for shape in sems for side in range(2)]
-        + [dma((4,)), dma((6,))],
+        + [dma((6,)), dma((6,))],
         compiler_params=pltpu.CompilerParams(
             collective_id=6, has_side_effects=True, vmem_limit_bytes=64 * 1024 * 1024 - 65536
         ),
@@ -1510,14 +1577,15 @@
         hidden_all,
         branch_all,
         proj_dense,
+        hidden_rows,
+        mixed_rows,
         ada,
         signals,
         attended,
-        hidden_rows,
-        mixed_rows,
         kept,
         mods,
         bias,
+        index,
         cot,
         count,
     )
@@ -1548,18 +1616,6 @@
     low = jnp.bfloat16
     full = jnp.float32
 
-    unit_width = w_fc1.shape[1] // n_dp
-    one_pieces = w_fc1.reshape(row_width, n_dp, unit_width).transpose(1, 2, 0)
-    two_pieces = (
-        w_fc2.reshape(n_fs // n_dp, n_dp, unit_width, w_fc2.shape[1])
-        .transpose(1, 3, 0, 2)
-        .reshape(n_dp, w_fc2.shape[1], -1)
-    )
-    pieces = jnp.concatenate([one_pieces, two_pieces], axis=2)
-
-    def beside(shard):
-        return jnp.concatenate([shard[:half_rows], shard[half_rows:]], axis=1)
-
     cond_float = condition.astype(full)
     signal = swish(cond_float).astype(low).astype(full)
     shards_bias = [b_ada, qv_bias, fc1_bias, out_bias]
@@ -1572,45 +1628,30 @@
         axis=1,
     ).reshape(n_dp, 8, 128)
     ada_width = w_ada.shape[1]
-    ada = jnp.pad(w_ada, ((0, 384 - row_width), (0, 896 - ada_width)))
-
-    indices = keep_index[0]
-    inputs = patches_in[0]
-    kept_in = jnp.take(inputs, indices, axis=0).astype(full)
+    unit_width = w_fc1.shape[1] // n_dp
+    index = keep_index.reshape(-1, 1)
+    patches = patches_in.reshape(patches_in.shape[1:])
+    upstream = cotangent.reshape(cotangent.shape[1:])
     forward = forward_kernel(
         notes,
-        ada,
-        pieces,
-        beside(w_qkv),
-        beside(w_proj),
-        kept_in,
-        cotangent[0],
+        w_ada,
+        w_fc1,
+        w_fc2.T,
+        w_qkv,
+        w_proj.T,
+        patches,
+        index,
+        upstream,
         keep_count,
         (ada_width, qv_bias.shape[0], fc1_bias.shape[0], out_bias.shape[0]),
     )
-    block_out, d_kept, mlp_out, att_out, grad_ada, last = backward_kernel(
-        forward, ada, kept_in, cotangent[0], keep_count
-    )
-    grad_patches = jnp.zeros(inputs.shape, full).at[indices].set(d_kept, unique_indices=True)[None]
-
+    block_out, grad_patches, qkv_out, proj_out, one_out, two_out, grad_ada, last = (
+        backward_kernel(forward, w_ada, index, patches.shape, upstream, keep_count)
+    )
     qkv_cols, proj_cols = w_qkv.shape[1], w_proj.shape[1]
 
-    def above(left, width):
-        return jnp.concatenate(
-            [att_out[:, left : left + width], att_out[:, left + width : left + 2 * width]], axis=0
-        )
-
-    one_out = mlp_out[0].reshape(-1, row_width).T.astype(full)
-    two_out = (
-        mlp_out[1]
-        .reshape(n_dp, w_fc2.shape[1], n_fs // n_dp, unit_width)
-        .transpose(2, 0, 3, 1)
-        .reshape(w_fc2.shape)
-        .astype(full)
-    )
-
-    last = last.reshape(n_dp, n_fs, 3, -1)
-    d_signal = jnp.sum(last[:, :, 0, :row_width], axis=1).reshape(1, features)
+    groups = last[:, :3, :].reshape(n_dp, n_fs, 3, 128).sum(axis=1)
+    d_signal = groups.reshape(n_dp, 384)[:, :row_width].reshape(1, features)
     unused, swish_pull = jax.vjp(swish, cond_float)
     grad_condition = swish_pull(d_signal)[0]
     own = d_at * n_fs + f_at
@@ -1618,18 +1659,16 @@
     heads_per = qkv_cols // head_size
 
     def line_of(kind, d, f):
-        start = (d, f, kind, 0)
-        return lax.dynamic_slice(last, start, (1, 1, 1, last.shape[3])).reshape(-1)
+        source = lax.dynamic_slice_in_dim(last, d * n_fs + f, 1, 0).reshape(-1)
+        start = row_width + kind * ada_width
+        return source[start : start + ada_width]
 
     def summed(f):
-        start = (0, f, 1, 0)
-        return jnp.sum(
-            lax.dynamic_slice(last, start, (n_dp, 1, 1, last.shape[3])).reshape(n_dp, -1), axis=0
-        )
+        return sum(line_of(0, d, f) for d in range(n_dp))
 
     ada_count = b_ada.shape[0]
     ada_bias = lax.dynamic_slice_in_dim(
-        line_of(2, d_at, own // n_dp), (own % n_dp) * ada_count, ada_count
+        line_of(1, d_at, own // n_dp), (own % n_dp) * ada_count, ada_count
     )
     block = jnp.where(own < HEADS, own, own + HEADS)
     qv_out = lax.dynamic_slice_in_dim(
@@ -1640,20 +1679,20 @@
     start = jnp.where(own < HEADS, qkv_cols, qkv_cols + proj_cols) + (place % per) * head_size
     out_out = lax.dynamic_slice_in_dim(summed(place // per), start, head_size)
     bias_out = lax.dynamic_slice_in_dim(
-        line_of(1, own % n_dp, own // n_dp), qkv_cols + 2 * proj_cols, unit_width
+        line_of(0, own % n_dp, own // n_dp), qkv_cols + 2 * proj_cols, unit_width
     )
     return (
         block_out[None],
-        grad_patches,
+        grad_patches[None],
         grad_condition,
         grad_ada,
         ada_bias,
-        above(0, qkv_cols),
+        qkv_out,
         qv_out,
-        above(2 * qkv_cols, proj_cols),
+        proj_out.T,
         one_out,
         bias_out,
-        two_out,
+        two_out.T,
         out_out,
     )
 

time: 297 us -> 275 us (0.926)
  local copies, waits for them, and re-layouts: 23.6 us -> 12.6 us
  Pallas kernels: 259 us -> 254 us
  other arithmetic: 7.25 us -> 3.94 us
    pallas_call x1, Pallas kernels: 141 us -> 136 us  [backward_kernel(): pl.pallas_call(functools.partial(backward_body, (HEADS, features // HEADS...]
    convert_element_type x4 -> x0, local copies, waits for them, and re-layouts: 4.74 us -> none  [the longest x3 3.57 us: shards(): two_out = mlp_out[1].reshape(n_dp, w_fc2.shape[1], n_fs // n_dp, unit_wid...]
    concatenate x5 -> x0, other arithmetic: 3.52 us -> none  [the longest x2 1.55 us: beside(): return jnp.concatenate([shard[:half_rows], shard[half_rows:]], axis=1)]
    unnamed x43 -> x21, local copies, waits for them, and re-layouts: 4.24 us -> 7.62 us
where the time goes in v5:
time: 275 us; the launch traced here: 272 us
  Pallas kernels  254 us (92%)
  local copies, waits for them, and re-layouts  12.6 us (5%)
  other arithmetic  3.94 us (1%)
    pallas_call x1, Pallas kernels, backward_kernel(): pl.pallas_call(functools.partial(backward_body, (HEADS, features // HEADS...  136 us
    pallas_call x1, Pallas kernels, forward_kernel(): pl.pallas_call(functools.partial(forward_body, (HEADS, size, widths)), ou...  118 us
    unnamed x21, local copies, waits for them, and re-layouts  7.62 us

profile of v5, /device:TPU:0, one launch (start us, length us, event | category | flops | bytes accessed | tf_op | source)
XLA Modules:
  0.0 271.7 jit_solution(9607044210948590217)
XLA Ops:
  0.6 0.7 convert_reduce_fusion
  1.4 0.1 reshape.79
  1.5 0.8 fusion.8
  2.3 0.6 copy.34
  2.9 1.4 copy.28.index_ref
  5.0 117.9 %forward.1 = (bf16[8,576,864]{2,1,0:T(8,128)(2,1)}, bf16[1152,1152]{1,0:T(8,128)(2,1)}, bf16[1152,1152]{1,0:T(8,128)(2,1)}, bf16[8,192,432]{2,1,0:T(8,128)(2,1)}...) custom-call(f32[4,8,128]{2,1,0:T(8,128)} %bitcast.50, ...), custom_call_target="tpu_custom_call" | custom-call | tf_op jit(solution)/shard_map/forward/pallas_call | solution.py:875
  122.9 135.7 %backward.1 = (bf16[192,1152]{1,0:T(8,128)(2,1)}, f32[256,1152]{1,0:T(8,128)}, f32[288,432]{1,0:T(8,128)}, f32[144,288]{1,0:T(8,128)}, f32[288,576]{1,0:T(8,128)...) custom-call(bf16[8,576,864]{2,1,0:T(8,128)(2,1)} %get-tuple-element.34.qkv_hbm, ...), custom_call_target="tpu_custom_call" | custom-call | tf_op jit(solution)/shard_map/backward/pallas_call | solution.py:1558
  258.6 1.0 bitcast_reduce_fusion
  259.6 0.1 reshape.86
  259.7 1.3 negate_add_fusion
  261.0 0.9 dynamic-slice_bitcast_fusion.3
  262.0 0.6 dynamic_slice.43
  262.6 0.1 slice_add_fusion
  262.7 0.6 dynamic_slice.48
  263.3 0.6 dynamic_slice.56
  263.9 0.6 dynamic_slice.55
  264.5 1.8 copy.44
  266.3 0.0 copy-done
  266.3 1.0 copy.45
  267.3 1.0 copy.46
  268.3 0.8 copy.47
  269.1 0.7 copy.48
  269.8 0.9 copy.49
  270.6 0.8 copy.50
  (16 shorter events, 0.1 us)
Async XLA Ops:
  258.6 7.7 %copy-start = (f32[256,1152]{1,0:T(8,128)S(1)}, f32[256,1152]{1,0:T(8,128)}, u32[]{:S(2)}) copy-start(f32[256,1152]{1,0:T(8,128)} %get-tuple-element.49) | copy-start | bytes 3538948
  261.0 6.3 %copy-start.1 = (f32[288,864]{1,0:T(8,128)S(1)}, f32[288,864]{1,0:T(8,128)}, u32[]{:S(2)}) copy-start(f32[288,864]{1,0:T(8,128)} %get-tuple-element.83) | copy-start | bytes 2985988
  266.3 2.0 copy-start.4
  267.3 1.8 copy-start.5
  267.3 2.5 copy-start.2
  268.3 2.4 copy-start.3
